TPU v7x, 32 devices: a whole 2x2x4 slice. The times are simulated.
32 devices in a mesh: dp: 16 (over z, x, core), fsdp: 2 (over y).
Axes of the slice: x: 2, y: 2, z: 4, core: 2. Of those that a mesh axis runs over, the one named last changes fastest.
Arguments:
- inputs: float32 [96, 197, 384], P(('dp', 'fsdp')), may hold values from -6 to 6
- ln1_gain: float32 [384], P('fsdp'), may hold values from 0.5 to 2
- ln1_shift: float32 [384], P('fsdp'), may hold values from -3 to 3
- w_qkv: float32 [384, 1152], P('fsdp'), may hold values from -0.3125 to 0.3125
- q_bias: float32 [384], P('fsdp'), may hold values from -3 to 3
- v_bias: float32 [384], P('fsdp'), may hold values from -3 to 3
- w_proj: float32 [384, 384], P('fsdp'), may hold values from -0.875 to 0.875
- proj_bias: float32 [384], P('fsdp'), may hold values from -3 to 3
- ln2_gain: float32 [384], P('fsdp'), may hold values from 0.5 to 2
- ln2_shift: float32 [384], P('fsdp'), may hold values from -3 to 3
- w_fc1: float32 [384, 1536], P('fsdp'), may hold values from -0.3125 to 0.3125
- fc1_bias: float32 [1536], P('fsdp'), may hold values from -3 to 3
- w_fc2: float32 [1536, 384], P('fsdp'), may hold values from -0.21875 to 0.21875
- fc2_bias: float32 [384], P('fsdp'), may hold values from -3 to 3
- grad_output: float32 [96, 197, 384], P(('dp', 'fsdp')), may hold values from -6 to 6
Outputs:
- output: float32 [96, 197, 384], P(('dp', 'fsdp'))
- grad_inputs: float32 [96, 197, 384], P(('dp', 'fsdp'))
- grad_ln1_gain: float32 [384], P('fsdp')
- grad_ln1_shift: float32 [384], P('fsdp')
- grad_w_qkv: float32 [384, 1152], P('fsdp')
- grad_q_bias: float32 [384], P('fsdp')
- grad_v_bias: float32 [384], P('fsdp')
- grad_w_proj: float32 [384, 384], P('fsdp')
- grad_proj_bias: float32 [384], P('fsdp')
- grad_ln2_gain: float32 [384], P('fsdp')
- grad_ln2_shift: float32 [384], P('fsdp')
- grad_w_fc1: float32 [384, 1536], P('fsdp')
- grad_fc1_bias: float32 [1536], P('fsdp')
- grad_w_fc2: float32 [1536, 384], P('fsdp')
- grad_fc2_bias: float32 [384], P('fsdp')
All inputs are finite; a program needn't handle non-finite values.
Results may differ from a plain program's by a relative error of at most 0.00026.
Values sent between devices are 32-bit elements; how exact they have to be, the bound alone decides.
No kernel may reach another device: no remote copies, remote signals or barrier semaphores. Data moves between devices by JAX's collectives and lax.ppermute only.
A program may use at most 128 MiB of HBM per device.

v0:
```python
import math

import jax
import jax.numpy as jnp
from jax import lax
from jax.experimental import pallas as pl
from jax.experimental.pallas import tpu as pltpu
from jax.sharding import PartitionSpec as P


HEAD_DIM = 64
LANES = 128
EPS = 1e-06
F32 = jnp.float32
BF16 = jnp.bfloat16
VMEM_LIMIT = 56 * 1024 * 1024


def split(v):
    hi = v.astype(BF16)
    lo = (v - hi.astype(F32)).astype(BF16)
    return hi, lo


def dot(a, b, ca, cb):
    return lax.dot_general(a, b, (((ca,), (cb,)), ((), ())), preferred_element_type=F32)


def dot3(a, b, ca, cb):
    ah, al = a
    bh, bl = b
    return dot(ah, bh, ca, cb) + (dot(ah, bl, ca, cb) + dot(al, bh, ca, cb))


def row_sum(v):
    return jnp.sum(v, axis=0, keepdims=True)


def norm_parts(v):
    center = v - jnp.mean(v, axis=-1, keepdims=True)
    inv = lax.rsqrt(jnp.mean(center * center, axis=-1, keepdims=True) + EPS)
    return center * inv, inv


def norm_back(dh, n, inv, gain):
    s = dh * gain
    return inv * (
        s - jnp.mean(s, axis=-1, keepdims=True) - n * jnp.mean(s * n, axis=-1, keepdims=True)
    )


def load_weight(offs, k, pieces, hi_ref, lo_ref):
    for p in pieces:
        at = pl.multiple_of(offs[k], 16)
        hi, lo = split(p[...])
        hi_ref[pl.ds(at, p.shape[0]), :] = hi
        lo_ref[pl.ds(at, p.shape[0]), :] = lo
        k += 1
    return k


def load_rows(offs, k, pieces, ref):
    n = ref.shape[0] // 3
    for p in pieces:
        hi, lo = split(p[...])
        for base, part in ((0, hi), (n, hi), (2 * n, lo)):
            ref[pl.ds(pl.multiple_of(base + offs[k], 16), p.shape[0]), :] = part
        k += 1


def load_cols(offs, k, pieces, ref):
    n = ref.shape[1] // 3
    for p in pieces:
        at = pl.ds(pl.multiple_of(offs[k], 16), p.shape[0])
        hi, lo = split(p[...])
        ref[at, :n] = hi
        ref[at, n : 2 * n] = hi
        ref[at, 2 * n :] = lo
        k += 1


def tall(v):
    hi, lo = split(v)
    return jnp.concatenate([hi, lo, hi], axis=1)


def fold(t):
    n = t.shape[1] // 2
    return t[:, :n] + t[:, n:]


def dot_rows(v, w3):
    hi, lo = split(v)
    n = w3.shape[0] // 3
    return fold(dot(hi, w3[n:], 1, 1)) + dot(lo, w3[:n], 1, 1)


def dot_outer(v3, w):
    n = v3.shape[1] // 3
    t = dot(v3[:, : 2 * n], w[0], 0, 0)
    return t[:n] + (t[n:] + dot(v3[:, :n], w[1], 0, 0))


def both(hi_ref, lo_ref):
    return hi_ref[...], lo_ref[...]


def lane_lt(shape):
    return lax.broadcasted_iota(jnp.int32, shape, 1) < HEAD_DIM


def swap(v):
    return pltpu.roll(v, HEAD_DIM, 1)


def pair_left(v, low):
    hi = v.astype(BF16).astype(F32)
    lo = v - hi
    zero = jnp.zeros_like(v)
    h0 = jnp.concatenate([jnp.where(low, hi, swap(lo)), jnp.where(low, hi, zero)], axis=1)
    h1 = jnp.concatenate([jnp.where(low, swap(lo), hi), jnp.where(low, zero, hi)], axis=1)
    return h0.astype(BF16), h1.astype(BF16)


def pair_right(v, low):
    hi = v.astype(BF16).astype(F32)
    lo = v - hi
    rolled = swap(hi)
    h0 = jnp.concatenate([jnp.where(low, hi, rolled), lo], axis=1)
    h1 = jnp.concatenate([jnp.where(low, rolled, hi), lo], axis=1)
    return h0.astype(BF16), h1.astype(BF16)


def wide(v):
    hi, lo = split(v)
    return hi, jnp.concatenate([hi, lo], axis=1)


def dot_wide(ph, pl_, w, ca):
    hi, cat = w
    t = dot(ph, cat, ca, 0)
    return t[:, :LANES] + (t[:, LANES:] + dot(pl_, hi, ca, 0))


def part_rows(g_ref, send_ref, keep_ref, core):
    n, rows, cols = keep_ref.shape
    for i in range(n):
        lanes = slice(i * cols, (i + 1) * cols)
        send_ref[i] = g_ref[pl.ds(pl.multiple_of((1 - core) * rows, 8), rows), lanes]
        keep_ref[i] = g_ref[pl.ds(pl.multiple_of(core * rows, 8), rows), lanes]


def part_cols(g_ref, send_ref, keep_ref, core):
    n, rows, cols = keep_ref.shape
    for i in range(n):
        at = pl.multiple_of((1 - core) * cols, LANES)
        send_ref[i] = g_ref[i * rows : (i + 1) * rows, pl.ds(at, cols)]
        at = pl.multiple_of(core * cols, LANES)
        keep_ref[i] = g_ref[i * rows : (i + 1) * rows, pl.ds(at, cols)]


def last():
    return pl.program_id(0) == pl.num_programs(0) - 1


def first():
    return pl.program_id(0) == 0


def qkv_kernel(np_, offs, x_ref, vec_ref, *refs):
    w_pieces = refs[:np_]
    qkv_ref, w3 = refs[np_:]

    @pl.when(first())
    def _():
        load_rows(offs, 0, w_pieces, w3)

    d = x_ref.shape[2]
    vec = vec_ref[...]
    n1, _ = norm_parts(x_ref[0])
    h1 = n1 * vec[0:1] + vec[1:2]
    qkv = dot(tall(h1), w3[...], 1, 0)
    qkv_ref[0, :, :d] = qkv[:, :d] + vec[2:3]
    qkv_ref[0, :, d : 2 * d] = qkv[:, d : 2 * d]
    qkv_ref[0, :, 2 * d :] = qkv[:, 2 * d :] + vec[3:4]


def attn_fwd_kernel(offs, qkv_ref, ctx_ref, ph_ref, pl_ref):
    d = ctx_ref.shape[2]
    low = lane_lt((qkv_ref.shape[1], LANES))
    for j in range(d // LANES):
        sl = slice(j * LANES, (j + 1) * LANES)
        q = qkv_ref[0, :, sl] * (1.0 / math.sqrt(HEAD_DIM))
        k = qkv_ref[0, :, d + j * LANES : d + (j + 1) * LANES]
        v = qkv_ref[0, :, 2 * d + j * LANES : 2 * d + (j + 1) * LANES]
        qs = pair_left(q, low)
        ks = pair_right(k, low)
        vw = wide(v)
        outs = []
        for i in range(2):
            s = dot(qs[i], ks[i], 1, 1)
            e = jnp.exp(s - jnp.max(s, axis=-1, keepdims=True))
            p = e * (1.0 / jnp.sum(e, axis=-1, keepdims=True))
            hi, lo = split(p)
            ph_ref[0, 2 * j + i] = hi
            pl_ref[0, 2 * j + i] = lo
            outs.append(dot_wide(hi, lo, vw, 1))
        ctx_ref[0, :, sl] = jnp.where(low, outs[0], outs[1])


def fill_rows(buf_ref, ref):
    n, s, _ = ref.shape
    step = buf_ref.shape[0] // n
    buf_ref[...] = jnp.zeros_like(buf_ref)
    for i in range(n):
        buf_ref[i * step : i * step + s, :] = ref[i]


def take_rows(ref, rows_ref):
    n, s, _ = ref.shape
    step = rows_ref.shape[0] // n
    for i in range(n):
        ref[i] = rows_ref[i * step : i * step + s, :]


def mlp_kernel(np_, offs, x_ref, ctx_ref, dy_ref, vec_ref, b1_ref, wp, w1, *refs):
    n, n2 = np_
    pp, p1, p2 = refs[:n], refs[n : 2 * n], refs[2 * n : 2 * n + n2]
    refs = refs[2 * n + n2 :]
    out_ref, mid_ref, dh2_ref, gb1_ref, gb2_ref = refs[:5]
    send2_ref, keep2_ref, send1_ref, keep1_ref = refs[5:9]
    wph, wpl, w1r, w2c, h3, y3, mids, outs, dh2s, g2_ref, g1_ref = refs[9:]
    i = pl.program_id(0)
    d = x_ref.shape[2]
    cols = b1_ref.shape[1]
    at = pl.ds(pl.multiple_of(i * cols, LANES), cols)

    @pl.when(first())
    def _():
        vec = vec_ref[...]
        load_weight(offs, 0, [wp, *pp], wph, wpl)
        load_cols(offs, n + 1, p2, w2c)
        fill_rows(outs, ctx_ref)
        fill_rows(mids, x_ref)
        mid = mids[...] + dot3(split(outs[...]), both(wph, wpl), 1, 0) + vec[4:5]
        mids[...] = mid
        n2, _ = norm_parts(mid)
        h3[...] = tall(n2 * vec[5:6] + vec[6:7])
        fill_rows(dh2s, dy_ref)
        dy = dh2s[...]
        y3[...] = tall(dy)
        gb2_ref[...] = row_sum(dy)
        outs[...] = mid + vec[7:8]
        dh2s[...] = jnp.zeros_like(dh2s)

    load_rows(offs, 0, [w1, *p1], w1r)
    pre = dot(h3[...], w1r[...], 1, 0) + b1_ref[...]
    half = 0.5 * (1.0 + lax.erf(pre * (1.0 / math.sqrt(2.0))))
    act = split(pre * half)
    slope = half + pre * jnp.exp(-0.5 * pre * pre) * (1.0 / math.sqrt(2.0 * math.pi))
    outs[...] += fold(dot(act[0], w2c[at, d:], 1, 0)) + dot(act[1], w2c[at, :d], 1, 0)
    g2_ref[:, at] = dot_outer(y3[...], act)
    dpre = dot(y3[...], w2c[at, :], 1, 1) * slope
    gb1_ref[...] = row_sum(dpre)
    dh2s[...] += dot_rows(dpre, w1r[...])
    g1_ref[:, at] = dot_outer(h3[...], split(dpre))

    @pl.when(last())
    def _():
        take_rows(out_ref, outs)
        take_rows(mid_ref, mids)
        take_rows(dh2_ref, dh2s)
        core = offs[n + 1 + len(p2)]
        part_rows(g2_ref, send2_ref, keep2_ref, core)
        part_cols(g1_ref, send1_ref, keep1_ref, core)


def mid_kernel(np_, offs, dh2_ref, ctx_ref, dy_ref, mid_ref, vec_ref, *refs):
    gp_ref, gv_ref, dmid_ref, dctx_ref, wph, wpl = refs[np_:]

    @pl.when(first())
    def _():
        load_weight(offs, 0, refs[:np_], wph, wpl)
        gp_ref[...] = jnp.zeros_like(gp_ref)
        gv_ref[...] = jnp.zeros_like(gv_ref)

    n2, inv2 = norm_parts(mid_ref[0])
    dh2 = dh2_ref[0]
    dmid = dy_ref[0] + norm_back(dh2, n2, inv2, vec_ref[5:6])
    dmid_ref[0] = dmid
    gv_ref[0:1] += row_sum(dmid)
    gv_ref[1:2] += row_sum(dh2 * n2)
    gv_ref[2:3] += row_sum(dh2)
    dmid = split(dmid)
    gp_ref[...] += dot3(split(ctx_ref[0]), dmid, 0, 0)
    dctx_ref[0] = dot3(dmid, both(wph, wpl), 1, 1)


def attn_bwd_kernel(
    offs, x_ref, qkv_ref, ph_ref, pl_ref, ctx_ref, dctx_ref, vec_ref, gp_ref, *refs
):
    dj_ref, send_ref, keep_ref, g_ref = refs
    d = ctx_ref.shape[2]

    @pl.when(first())
    def _():
        g_ref[:, : 3 * d] = jnp.zeros((d, 3 * d), F32)
        g_ref[:, 3 * d :] = gp_ref[...]

    scale = 1.0 / math.sqrt(HEAD_DIM)
    low = lane_lt((ctx_ref.shape[1], LANES))
    for j in range(d // LANES):
        sl = slice(j * LANES, (j + 1) * LANES)
        q = qkv_ref[0, :, j * LANES : (j + 1) * LANES] * scale
        k = qkv_ref[0, :, d + j * LANES : d + (j + 1) * LANES]
        v = qkv_ref[0, :, 2 * d + j * LANES : 2 * d + (j + 1) * LANES]
        dc = dctx_ref[0, :, sl]
        prod = dc * ctx_ref[0, :, sl]
        delta0 = jnp.sum(jnp.where(low, prod, 0.0), axis=-1, keepdims=True)
        delta1 = jnp.sum(jnp.where(low, 0.0, prod), axis=-1, keepdims=True)
        deltas = (delta0, delta1)
        dcs = pair_left(dc, low)
        vs = pair_right(v, low)
        qw, kw, dcw = wide(q), wide(k), wide(dc)
        dq, dk, dv = [], [], []
        for i in range(2):
            ph = ph_ref[0, 2 * j + i]
            p_lo = pl_ref[0, 2 * j + i]
            dp = dot(dcs[i], vs[i], 1, 1)
            ds = (ph.astype(F32) + p_lo.astype(F32)) * (dp - deltas[i])
            dsh, dsl = split(ds)
            dv.append(dot_wide(ph, p_lo, dcw, 0))
            dq.append(dot_wide(dsh, dsl, kw, 1))
            dk.append(dot_wide(dsh, dsl, qw, 0))
        dj_ref[0, :, sl] = jnp.where(low, dq[0], dq[1]) * scale
        dj_ref[0, :, d + j * LANES : d + (j + 1) * LANES] = jnp.where(low, dk[0], dk[1])
        dj_ref[0, :, 2 * d + j * LANES : 2 * d + (j + 1) * LANES] = jnp.where(low, dv[0], dv[1])
    n1, _ = norm_parts(x_ref[0])
    h1 = n1 * vec_ref[0:1] + vec_ref[1:2]
    g_ref[:, : 3 * d] += dot_outer(tall(h1), split(dj_ref[0]))

    @pl.when(last())
    def _():
        part_cols(g_ref, send_ref, keep_ref, offs[0])


def input_grad_kernel(np_, offs, x_ref, dj_ref, dmid_ref, vec_ref, *refs):
    w_pieces = refs[:np_]
    gva_ref, gb1_ref, gb2_ref = refs[np_ : np_ + 3]
    gs_ref, dx_ref, w3, gv_ref = refs[np_ + 3 :]

    @pl.when(first())
    def _():
        load_rows(offs, 0, w_pieces, w3)
        gv_ref[...] = jnp.zeros_like(gv_ref)

    d = x_ref.shape[2]
    n1, inv1 = norm_parts(x_ref[0])
    dj = dj_ref[0]
    sums = row_sum(dj)
    gv_ref[2:3] += sums[:, :d]
    gv_ref[3:4] += sums[:, 2 * d :]
    dh1 = dot_rows(dj, w3[...])
    gv_ref[0:1] += row_sum(dh1 * n1)
    gv_ref[1:2] += row_sum(dh1)
    dx_ref[0] = dmid_ref[0] + norm_back(dh1, n1, inv1, vec_ref[0:1])

    @pl.when(last())
    def _():
        shards, _, w = gs_ref.shape
        per = gb1_ref.shape[1] // (shards * w)
        for h in range(shards):
            sl = slice(h * w, (h + 1) * w)
            gs_ref[h, 0:4] = gv_ref[0:4, sl]
            gs_ref[h, 4:7] = gva_ref[0:3, sl]
            gs_ref[h, 7:8] = gb2_ref[:, sl]
            for j in range(per):
                at = (h * per + j) * w
                gs_ref[h, 8 + j : 9 + j] = gb1_ref[:, at : at + w]


def per_image(shape):
    n = len(shape)
    return pl.BlockSpec((1,) + tuple(shape[1:]), lambda i, offs: (i,) + (0,) * (n - 1))


def fixed(shape):
    n = len(shape)
    return pl.BlockSpec(tuple(shape), lambda i, offs: (0,) * n)


def block_at(shape, col):
    return pl.BlockSpec(shape, lambda i, offs: (0, col))


def run(kernel, offs, images, consts, outs, scratch, flops, blocks={}):
    count = images[0].shape[0]
    in_specs = [per_image(a.shape) for a in images] + [
        block_at(*blocks[i]) if i in blocks else fixed(a.shape) for i, a in enumerate(consts)
    ]
    out_specs = [per_image(s) if im else fixed(s) for s, _, im in outs]
    return pl.pallas_call(
        kernel,
        out_shape=[jax.ShapeDtypeStruct(s, t) for s, t, _ in outs],
        grid_spec=pltpu.PrefetchScalarGridSpec(
            num_scalar_prefetch=1,
            grid=(count,),
            in_specs=in_specs,
            out_specs=out_specs,
            scratch_shapes=scratch,
        ),
        cost_estimate=pl.CostEstimate(flops=flops, transcendentals=0, bytes_accessed=8 << 20),
        compiler_params=pltpu.CompilerParams(
            dimension_semantics=("arbitrary",), vmem_limit_bytes=VMEM_LIMIT
        ),
    )(offs, *images, *consts)


def pair_scratch(rows, cols):
    return [pltpu.VMEM((rows, cols), BF16), pltpu.VMEM((rows, cols), BF16)]


def image(*shape, dtype=F32):
    return (shape, dtype, True)


def const(*shape):
    return (shape, F32, False)


def qkv_call(x, vec, w):
    offs, pieces = w
    b, s, d = x.shape
    return run(
        lambda *r: qkv_kernel(len(pieces), *r),
        offs,
        [x],
        [vec, *pieces],
        [image(b, s, 3 * d)],
        [pltpu.VMEM((3 * d, 3 * d), BF16)],
        18 * b * s * d * d,
    )[0]


def attn_fwd(qkv, zero):
    b, s, d = qkv.shape
    d = d // 3
    heads = d // HEAD_DIM
    probs = image(b, heads, s, s, dtype=BF16)
    return run(
        attn_fwd_kernel, zero, [qkv], [], [image(b, s, d), probs, probs], [],
        30 * b * s * d * d,
    )


def cols_block(shape, cols, at):
    return pl.BlockSpec((shape[0], cols), lambda i, offs: (0, at(i)))


def mlp(x, ctx, dy, vec, b1, joint, w2, core, shards):
    offs, (wp, w1, *pieces) = joint
    b, s, d = x.shape
    ff = b1.shape[1]
    rows = b * (-(-s // 8) * 8)
    c = ff // 3
    half2, half1 = (shards, d // 2, ff // shards), (shards, d // shards, ff // 2)
    shapes = [(b, s, d), (b, s, d), (b, s, d), (1, ff), (1, d), half2, half2, half1, half1]
    n = len(pieces)
    specs = [fixed(a.shape) for a in (x, ctx, dy, vec)]
    specs += [cols_block(b1.shape, c, lambda i: i), fixed(wp.shape)]
    specs += [cols_block(w1.shape, c, lambda i: i)]
    specs += [cols_block(p.shape, d, lambda i: ff // d) for p in pieces]
    specs += [cols_block(p.shape, c, lambda i: i) for p in pieces]
    specs += [fixed(p.shape) for p in w2[1]]
    out_specs = [fixed(t) for t in shapes]
    out_specs[3] = cols_block((1, ff), c, lambda i: i)
    big = pltpu.VMEM((rows, d), F32)
    tall_one = pltpu.VMEM((rows, 3 * d), BF16)
    return pl.pallas_call(
        lambda *r: mlp_kernel((n, len(w2[1])), *r),
        name="mlp",
        out_shape=[jax.ShapeDtypeStruct(t, F32) for t in shapes],
        grid_spec=pltpu.PrefetchScalarGridSpec(
            num_scalar_prefetch=1,
            grid=(ff // c,),
            in_specs=specs,
            out_specs=out_specs,
            scratch_shapes=pair_scratch(d, d)
            + [pltpu.VMEM((3 * d, c), BF16), pltpu.VMEM((ff, 3 * d), BF16)]
            + [tall_one, tall_one, big, big, big]
            + [pltpu.VMEM((d, ff), F32)] * 2,
        ),
        cost_estimate=pl.CostEstimate(
            flops=40 * b * s * d * ff, transcendentals=0, bytes_accessed=8 << 20
        ),
        compiler_params=pltpu.CompilerParams(
            dimension_semantics=("arbitrary",), vmem_limit_bytes=VMEM_LIMIT
        ),
    )(
        jnp.concatenate([offs, w2[0], core]),
        *(x, ctx, dy, vec, b1, wp, w1),
        *pieces,
        *pieces,
        *w2[1],
    )


def mlp_mid(dh2, ctx, dy, mid, vec, joint):
    offs, (wp, _, *pieces) = joint
    b, s, d = mid.shape
    return run(
        lambda *r: mid_kernel(1 + len(pieces), *r),
        offs,
        [dh2, ctx, dy, mid],
        [vec, wp, *pieces],
        [const(d, d), const(8, d), image(b, s, d), image(b, s, d)],
        pair_scratch(d, d),
        12 * b * s * d * d,
        {2 + i: ((p.shape[0], d), p.shape[1] // d - 1) for i, p in enumerate(pieces)},
    )


def attn_bwd(x, qkv, ph, p_lo, ctx, dctx, vec, gwp, core, shards):
    b, s, d = ctx.shape
    half = const(shards, d // shards, 2 * d)
    return run(
        attn_bwd_kernel,
        core,
        [x, qkv, ph, p_lo, ctx, dctx],
        [vec, gwp],
        [image(b, s, 3 * d), half, half],
        [pltpu.VMEM((d, 4 * d), F32)],
        60 * b * s * d * d,
    )


def input_grad(x, dj, dmid, vec, w, gva, gb1, gb2, shards):
    offs, pieces = w
    b, s, d = x.shape
    rows = 8 + gb1.shape[1] // d
    return run(
        lambda *r: input_grad_kernel(len(pieces), *r),
        offs,
        [x, dj, dmid],
        [vec, *pieces, gva, gb1, gb2],
        [const(shards, rows, d // shards), image(b, s, d)],
        [pltpu.VMEM((3 * d, 3 * d), BF16), pltpu.VMEM((8, d), F32)],
        18 * b * s * d * d,
    )


def tie(v, *after):
    return lax.optimization_barrier((v, *after))[0]


def ints(*values):
    return jnp.stack([jnp.asarray(v, jnp.int32) for v in values])


def swap_with(v, n_dp, n_fsdp, dp_bits, fsdp_bits):
    perm = []
    for i in range(n_dp * n_fsdp):
        d, f = divmod(i, n_fsdp)
        perm.append((i, (d ^ dp_bits) * n_fsdp + (f ^ fsdp_bits)))
    return lax.ppermute(v, ("dp", "fsdp"), perm)


class Pairs:
    def __init__(self, n_dp):
        self.n_dp, self.nz = n_dp, n_dp // 4
        self.bits = self.nz.bit_length() - 1
        dp = lax.axis_index("dp")
        self.core, self.x, self.z = dp % 2, (dp // 2) % 2, dp // 4
        self.y = lax.axis_index("fsdp")

    def over_core(self, v):
        return swap_with(v, self.n_dp, 2, 1, 0)

    def over_x(self, v):
        return swap_with(v, self.n_dp, 2, 2, 0)

    def over_y(self, v):
        return swap_with(v, self.n_dp, 2, 0, 1)

    def over_z(self, v, k):
        return swap_with(v, self.n_dp, 2, 4 * k, 0)

    def quarter(self, w):
        rows = w.shape[0] // 4
        return lax.dynamic_slice_in_dim(w, (2 * self.core + self.x) * rows, rows, 0)

    def quarter_offs(self, rows):
        base = (1 - self.y) * rows
        q = rows // 4
        order = [(c, x) for c in (self.core, 1 - self.core) for x in (self.x, 1 - self.x)]
        return ints(self.y * rows, *(base + (2 * c + x) * q for c, x in order))

    def finish(self, a):
        b = self.over_x(a)
        return [a, b, self.over_core(a), self.over_core(b)]

    def halve(self, axis, at, got, keep):
        both = [pick(got, i, axis) + pick(keep, i, axis) for i in (1 - at, at)]
        return both[0], both[1]

    def halve_x(self, got, keep):
        shape = keep.shape
        shape = shape[:-2] + (2, shape[-2] // 2, shape[-1])
        return self.halve(len(shape) - 3, self.x, got.reshape(shape), keep.reshape(shape))

    def halve_z(self, bit, got, keep):
        shape = keep.shape
        shape = shape[:-3] + (shape[-3] // 2, 2) + shape[-2:]
        at = (self.z // (1 << bit)) % 2
        return self.halve(len(shape) - 3, at, got.reshape(shape), keep.reshape(shape))

    def reduce_z(self, got, keep, small=None):
        shape = keep.shape
        shape = shape[:-2] + (self.nz, shape[-2] // self.nz, shape[-1])
        got, keep = got.reshape(shape), keep.reshape(shape)
        for bit in range(self.bits):
            send, keep = self.halve_z(bit, got, keep)
            if small is not None:
                send, small = lax.optimization_barrier((send, small))
                small = small + self.over_z(small, 1 << bit)
            got = self.over_z(send, 1 << bit)
        total = got + keep
        total = total.reshape(total.shape[:-3] + total.shape[-2:])
        return total if small is None else (total, small)

    def gather_z(self, v, bits):
        for bit in bits:
            v = jnp.stack([v, self.over_z(v, 1 << bit)])
        return v

    def placed(self, bits, with_x):
        out = []
        names = list(bits) + (["x"] if with_x else [])
        for i in range(1 << len(names)):
            at = [(i >> k) & 1 for k in range(len(names))]
            dz = sum(a << n for a, n in zip(at, names) if n != "x")
            dx = sum(a for a, n in zip(at, names) if n == "x")
            out.append((dx, dz))
        return out

    def join(self, stacks, moves, put, outs, scratch=(), finish=None):
        nz = self.nz
        n_out = len(outs)

        def kernel(pos, *refs):
            ins, refs = refs[: len(stacks)], refs[len(stacks) :]
            for core in range(2):

                @pl.when(pos[0] == core)
                def _():
                    for ref, places in zip(ins, moves):
                        for k, (dc, dx, dz) in enumerate(places):
                            row = (pos[1] ^ dx) * nz + (pos[2] ^ dz)
                            put(ref.at[k], core ^ dc, row, refs)

            if finish is not None:
                finish(refs)

        return pl.pallas_call(
            kernel,
            out_shape=[jax.ShapeDtypeStruct(s, F32) for s in outs],
            grid_spec=pltpu.PrefetchScalarGridSpec(
                num_scalar_prefetch=1,
                grid=(1,),
                in_specs=[fixed(a.shape) for a in stacks],
                out_specs=[fixed(s) for s in outs],
                scratch_shapes=list(scratch),
            ),
            compiler_params=pltpu.CompilerParams(vmem_limit_bytes=VMEM_LIMIT),
        )(ints(self.core, self.x, self.z), *stacks)

    def join_attn(self, stacks, moves, d):
        _, r, cols = stacks[0].shape
        rows = 2 * self.nz * r

        def put(ref, core, row, refs):
            at = pl.ds(pl.multiple_of(row * r, 8), r)
            if core == 0:
                refs[0][at, :cols] = ref[...]
            else:
                n = 3 * d - cols
                refs[0][at, cols:] = ref[:, :n]
                refs[1][at, :] = ref[:, n:]

        return self.join(stacks, moves, put, [(rows, 3 * d), (rows, d)])

    def join_mlp(self, stacks, moves):
        _, _, r, cols = stacks[0].shape
        rows = 2 * self.nz * r

        def put(ref, core, row, refs):
            at = pl.multiple_of(row * r, 8)
            refs[2][pl.ds(core * rows + at, r), :] = ref[0]
            refs[1][pl.ds(at, r), core * cols : (core + 1) * cols] = ref[1]

        def finish(refs):
            refs[0][...] = refs[2][...].T

        outs = [(cols, 2 * rows), (rows, 2 * cols)]
        scratch = [pltpu.VMEM((2 * rows, cols), F32)]
        return self.join(stacks, moves, put, outs, scratch, finish)


def pick(v, i, axis=0):
    return lax.dynamic_index_in_dim(v, i, axis, keepdims=False)


def whole_mesh_step(n_fsdp, x, vec, b1f, wqkv, wproj, wfc1, wfc2, dy):
    def gather(w):
        return lax.all_gather(w, "fsdp", axis=0, tiled=True)

    def total(v):
        part = lax.psum_scatter(v, "fsdp", scatter_dimension=0, tiled=True)
        return lax.psum(part, "dp")[0]

    zero = ints(0)
    d = x.shape[2]
    w_qkv, w_2 = (zero, [gather(wqkv)]), (zero, [gather(wfc2)])
    joint = zero, [gather(wproj), gather(wfc1)]
    qkv = qkv_call(x, vec, w_qkv)
    ctx, ph, p_lo = attn_fwd(qkv, zero)
    out, mid, dh2, gb1, gb2, send2, keep2, send1, keep1 = mlp(
        x, ctx, dy, vec, b1f, joint, w_2, zero, n_fsdp
    )
    gwp, gva, dmid, dctx = mlp_mid(dh2, ctx, dy, mid, vec, joint)
    dj, send0, keep0 = attn_bwd(x, qkv, ph, p_lo, ctx, dctx, vec, gwp, zero, n_fsdp)
    gs, dx = input_grad(x, dj, dmid, vec, w_qkv, gva, gb1, gb2, n_fsdp)
    ga = jnp.concatenate([total(keep0), total(send0)], axis=1)
    gw1 = jnp.concatenate([total(keep1), total(send1)], axis=1)
    gw2 = jnp.concatenate([total(keep2), total(send2)], axis=0).T
    return out, dx, ga[:, : 3 * d], ga[:, 3 * d :], gw1, gw2, total(gs)


def pair_step(n_dp, x, vec, b1f, wqkv, wproj, wfc1, wfc2, dy):
    c = Pairs(n_dp)
    core = ints(c.core)
    d = x.shape[2]
    came = c.over_y(c.quarter(wqkv))
    w_qkv = c.quarter_offs(wqkv.shape[0]), [wqkv, *c.finish(came)]
    joint = tie(jnp.concatenate([c.quarter(wfc1), c.quarter(wproj)], axis=1), came)
    joint = c.over_y(joint)
    w_2 = c.over_y(tie(c.quarter(wfc2), came))
    qkv = qkv_call(x, vec, w_qkv)
    pieces = c.finish(tie(joint, qkv))
    joint = c.quarter_offs(wproj.shape[0]), [wproj, wfc1, *pieces]
    ctx, ph, p_lo = attn_fwd(qkv, core)
    w_2 = c.quarter_offs(wfc2.shape[0]), [wfc2, *c.finish(tie(w_2, qkv))]
    out, mid, dh2, gb1, gb2, send2, keep2, send1, keep1 = mlp(
        x, ctx, dy, vec, b1f, joint, w_2, core, 2
    )
    got2 = c.over_core(send2)
    got1 = c.over_core(send1)
    gwp, gva, dmid, dctx = mlp_mid(dh2, ctx, dy, mid, vec, joint)
    send2, keep2 = c.halve_x(got2, keep2)
    send1, keep1 = c.halve(0, c.y, got1, keep1)
    got2 = c.over_x(send2)
    got1 = c.over_y(send1)
    dctx = tie(dctx, send1, keep1, send2, keep2)
    dj, send0, keep0 = attn_bwd(x, qkv, ph, p_lo, ctx, dctx, vec, gwp, core, 2)
    got0 = c.over_core(send0)
    send2, keep2 = c.halve(0, c.y, got2, keep2)
    send1, keep1 = c.halve_x(got1, keep1)
    got2 = c.over_y(send2)
    got1 = c.over_x(send1)
    dj = tie(dj, send0, send1, keep1, send2, keep2)
    gs, dx = input_grad(x, dj, dmid, vec, w_qkv, gva, gb1, gb2, 2)
    send0, keep0 = c.halve(0, c.y, got0, keep0)
    got0 = c.over_y(send0)
    gs = tie(gs, send0)
    gs = gs + c.over_core(gs)
    gs_got = c.over_y(pick(gs, 1 - c.y))
    gs = pick(gs, c.y)
    gotf, keepf = jnp.stack([got2, got1]), jnp.stack([keep2, keep1])
    f = c.reduce_z(gotf, keepf)
    up = tuple(range(c.bits))
    f = c.gather_z(f, up[::-1])
    gs = gs + gs_got
    gs_got = c.over_x(gs)
    send0, keep0 = c.halve_x(got0, keep0)
    got0 = c.over_x(tie(send0, gs))
    gs = gs + gs_got
    a, gs = c.reduce_z(got0, keep0, gs)
    a = c.gather_z(tie(a, gs), up[:0:-1])
    a = jnp.stack([a, c.over_x(a)])
    a = a.reshape((-1,) + a.shape[-2:])
    fr = f.reshape((-1,) + f.shape[-3:])
    f = [fr, c.over_x(fr)]
    f = f + [c.over_core(v) for v in f]
    pf = c.placed(up[::-1], False)
    pa = c.placed(up[:0:-1], True)
    mf = [[(i // 2, i % 2, dz) for _, dz in pf] for i in range(4)]
    ma = [[(i // 2, dx_, dz ^ (i % 2)) for dx_, dz in pa] for i in range(4)]
    gw2, gw1 = c.join_mlp(f, mf)
    a = [a, c.over_z(a, 1)]
    a = a + [c.over_core(v) for v in a]
    gwqkv, gwproj = c.join_attn(a, ma, d)
    return out, dx, gwqkv, gwproj, gw1, gw2, gs


def is_pairs(n_dp, n_fsdp):
    return n_fsdp == 2 and n_dp >= 8 and (n_dp & (n_dp - 1)) == 0


def body(n_dp, n_fsdp, x, g1, s1, wqkv, qb, vb, wproj, pb, g2, s2, wfc1, b1, wfc2, b2, dy):
    pairs = is_pairs(n_dp, n_fsdp)
    w = g1.shape[0]
    small = jnp.concatenate([jnp.stack([g1, s1, qb, vb, pb, g2, s2, b2]), b1.reshape(-1, w)])
    if pairs:
        other = swap_with(small, n_dp, n_fsdp, 0, 1)
        is_first = lax.axis_index("fsdp") == 0
        small = jnp.stack([jnp.where(is_first, small, other), jnp.where(is_first, other, small)])
    else:
        small = lax.all_gather(small, "fsdp", axis=0)
    vec = small[:, :8].transpose(1, 0, 2).reshape(8, -1)
    b1f = small[:, 8:].reshape(1, -1)
    args = (x, vec, b1f, wqkv, wproj, wfc1, wfc2, dy)
    step = pair_step(n_dp, *args) if pairs else whole_mesh_step(n_fsdp, *args)
    out, dx, gwqkv, gwproj, gw1, gw2, gs = step
    return (
        out,
        dx,
        gs[0],
        gs[1],
        gwqkv,
        gs[2],
        gs[3],
        gwproj,
        gs[4],
        gs[5],
        gs[6],
        gw1,
        gs[8:].reshape(-1),
        gw2,
        gs[7],
    )


def solution(mesh):
    n_dp, n_fsdp = mesh.shape["dp"], mesh.shape["fsdp"]
    act = P(("dp", "fsdp"), None, None)
    vec = P("fsdp")
    mat = P("fsdp", None)
    in_specs = (act, vec, vec, mat, vec, vec, mat, vec, vec, vec, mat, vec, mat, vec, act)
    out_specs = (act,) + in_specs[:1] + in_specs[1:14]
    return jax.shard_map(
        lambda *a: body(n_dp, n_fsdp, *a),
        mesh=mesh,
        in_specs=in_specs,
        out_specs=out_specs,
        check_vma=False,
    )
```

profile of v0, /device:TPU:0, one launch (start us, length us, event | category | flops | bytes accessed | tf_op | source)
XLA Modules:
  0.0 224.5 jit_solution(15120325870895222371)
XLA Ops:
  2.2 3.0 %collective-permute-start = (f32[12,192]{1,0:T(8,128)S(1)}, f32[12,192]{1,0:T(8,128)S(1)}, u32[]{:S(2)}, u32[]{:S(2)}) collective-permute-start(f32[12,192]{1,0:T(8,128)S(1)} %concatenate.13), channel_id=1, source_target_pairs={{0,1},{1,0},{2,3},{3,2},{4,5},{5,4},{6,7},{7,6},{8,9},{9,8},{10,11... | collective-permute-start | bytes 27656 | tf_op jit(solution)/shard_map/ppermute | solution.py:565
  8.2 4.9 %collective-permute-done.1.r_4_.r_6_ = f32[48,1152]{1,0:T(8,128)S(1)} collective-permute-done((f32[48,1152]{1,0:T(8,128)S(1)}, f32[48,1152]{1,0:T(8,128)S(1)}, u32[]{:S(2)}, u32[]{:S(2)}) %collective-permute-start.1) | collective-permute-done | bytes 221216 | tf_op jit(solution)/shard_map/ppermute | solution.py:565
  16.9 2.3 %collective-permute-done.2.r_5_.r_7_ = f32[48,1152]{1,0:T(8,128)S(1)} collective-permute-done((f32[48,1152]{1,0:T(8,128)S(1)}, f32[48,1152]{1,0:T(8,128)S(1)}, u32[]{:S(2)}, u32[]{:S(2)}) %collective-permute-start.2) | collective-permute-done | bytes 221216 | tf_op jit(solution)/shard_map/ppermute | solution.py:565
  22.4 6.8 %shard_map.262.qkv_ref = f32[3,197,1152]{2,1,0:T(8,128)} custom-call(s32[5]{0:T(128)} %stack.151.r_0_, f32[3,197,384]{2,1,0:T(8,128)} %r_1_.5, f32[8,384]{1,0:T(8,128)} %reshape.141.r_2_.r_4_.r_5_.vec_ref, f32[192,1152]{1,0:T(8,128)} %r_5_.1, f32[48,1152]{1,0:T(8,128)} %copy-done.18, f32[48,1152]{1,0:T(8,128)} %copy-done.19, f32[48,1152]{1,0:T(8,128)} %copy-done.20, ...), custom_call_target="tpu_custom_call" | custom-call | flops 1568636928 | bytes 8388608 | tf_op jit(solution)/shard_map/pallas_call | solution.py:402
  32.1 8.6 %collective-permute-done.6.r_9_.r_13_.r_8_ = f32[48,1920]{1,0:T(8,128)S(1)} collective-permute-done((f32[48,1920]{1,0:T(8,128)S(1)}, f32[48,1920]{1,0:T(8,128)S(1)}, u32[]{:S(2)}, u32[]{:S(2)}) %collective-permute-start.6) | collective-permute-done | bytes 368672 | tf_op jit(solution)/shard_map/ppermute | solution.py:565
  42.0 4.4 %collective-permute-done.10.r_18_ = f32[192,384]{1,0:T(8,128)S(1)} collective-permute-done((f32[192,384]{1,0:T(8,128)S(1)}, f32[192,384]{1,0:T(8,128)S(1)}, u32[]{:S(2)}, u32[]{:S(2)}) %collective-permute-start.10) | collective-permute-done | bytes 294944 | tf_op jit(solution)/shard_map/ppermute | solution.py:565
  47.1 9.1 %shard_map.263 = (f32[3,197,384]{2,1,0:T(8,128)}, bf16[3,6,197,197]{3,2,1,0:T(8,128)(2,1)}, bf16[3,6,197,197]{3,2,1,0:T(8,128)(2,1)}) custom-call(s32[1]{0:T(128)} %bitcast.10.offs, f32[3,197,1152]{2,1,0:T(8,128)} %shard_map.262.qkv_ref), custom_call_target="tpu_custom_call" | custom-call | flops 2614394880 | bytes 8388608 | tf_op jit(solution)/shard_map/pallas_call | solution.py:402
  57.3 26.7 %mlp.1 = (f32[3,197,384]{2,1,0:T(8,128)}, f32[3,197,384]{2,1,0:T(8,128)}, f32[3,197,384]{2,1,0:T(8,128)}, f32[1,1536]{1,0:T(1,128)}, f32[1,384]{1,0:T(1,128)}, /...) custom-call(s32[11]{0:T(128)} %concatenate.12.r_0_, ...), custom_call_target="tpu_custom_call" | custom-call | flops 13943439360 | bytes 8388608 | tf_op jit(solution)/shard_map/mlp/pallas_call | solution.py:479
  84.6 6.8 %shard_map.264 = (f32[384,384]{1,0:T(8,128)}, f32[8,384]{1,0:T(8,128)}, f32[3,197,384]{2,1,0:T(8,128)}, f32[3,197,384]{2,1,0:T(8,128)}) custom-call(s32[5]{0:T(128)} %stack.151.r_0_, f32[3,197,384]{2,1,0:T(8,128)} %get-tuple-element.61.r_1_, f32[3,197,384]{2,1,0:T(8,128)} %get-tuple-element.53.r_2_.ctx_ref, f32[3,197,384]{2,1,0:T(8,128)} %r_3_.5, ...), custom_call_target="tpu_custom_call" | custom-call | flops 1045757952 | bytes 8388608 | tf_op jit(solution)/shard_map/pallas_call | solution.py:402
  92.5 2.3 %dynamic-slice_add_fusion.2 = (f32[1,192,768]{2,1,0:T(8,128)S(1)}, f32[192,768]{1,0:T(8,128)}) fusion(f32[2,192,768]{2,1,0:T(8,128)S(1)} %copy-done.5, s32[]{:T(128)S(6)} %select_n.132, f32[2,192,768]{2,1,0:T(8,128)} %copy-done.6, s32[]{:T(128)S(6)} %select_n.130), kind=kLoop, calls=%fused_computation.14 | loop fusion | flops 294912 | bytes 3538952 | tf_op jit(solution)/shard_map/add | solution.py:603
  96.8 13.4 %shard_map.265 = (f32[3,197,1152]{2,1,0:T(8,128)}, f32[2,192,768]{2,1,0:T(8,128)}, f32[2,192,768]{2,1,0:T(8,128)}) custom-call(s32[1]{0:T(128)} %bitcast.10.offs, f32[3,197,384]{2,1,0:T(8,128)} %r_1_.5, f32[3,197,1152]{2,1,0:T(8,128)} %shard_map.262.qkv_ref, bf16[3,6,197,197]{3,2,1,0:T(8,128)(2,1)} %get-tuple-element.59.ph_ref, ...), custom_call_target="tpu_custom_call" | custom-call | flops 5228789760 | bytes 8388608 | tf_op jit(solution)/shard_map/pallas_call | solution.py:402
  115.6 11.3 %collective-permute-done.16 = f32[2,96,768]{2,1,0:T(8,128)} collective-permute-done((f32[2,96,768]{2,1,0:T(8,128)}, f32[2,96,768]{2,1,0:T(8,128)}, u32[]{:S(2)}, u32[]{:S(2)}) %collective-permute-start.16) | collective-permute-done | bytes 589856 | tf_op jit(solution)/shard_map/ppermute | solution.py:565
  126.9 1.8 bitcast_add_fusion.1
  129.8 2.8 %collective-permute-done.33 = f32[96,768]{1,0:T(8,128)S(1)} collective-permute-done((f32[96,768]{1,0:T(8,128)S(1)}, f32[96,768]{1,0:T(8,128)S(1)}, u32[]{:S(2)}, u32[]{:S(2)}) %collective-permute-start.33) | collective-permute-done | bytes 294944 | tf_op jit(solution)/shard_map/ppermute | solution.py:565
  132.5 4.3 %collective-permute-done.32 = f32[96,768]{1,0:T(8,128)} collective-permute-done((f32[96,768]{1,0:T(8,128)}, f32[96,768]{1,0:T(8,128)}, u32[]{:S(2)}, u32[]{:S(2)}) %collective-permute-start.32) | collective-permute-done | bytes 294944 | tf_op jit(solution)/shard_map/ppermute | solution.py:565
  136.9 1.8 fusion.5
  138.7 1.6 collective-permute-start.34
  141.9 7.9 %shard_map.266 = (f32[2,12,192]{2,1,0:T(8,128)}, f32[3,197,384]{2,1,0:T(8,128)}) custom-call(s32[5]{0:T(128)} %stack.151.r_0_, f32[3,197,384]{2,1,0:T(8,128)} %r_1_.5, f32[3,197,1152]{2,1,0:T(8,128)} %get-tuple-element.72.r_2_, f32[3,197,384]{2,1,0:T(8,128)} %get-tuple-element.73.r_3_, f32[8,384]{1,0:T(8,128)} %reshape.141.r_2_.r_4_.r_5_.vec_ref, ...), custom_call_target="tpu_custom_call" | custom-call | flops 1568636928 | bytes 8388608 | tf_op jit(solution)/shard_map/pallas_call | solution.py:402
  153.3 2.7 %collective-permute-start.35 = (f32[2,1,24,768]{3,2,1,0:T(8,128)S(1)}, f32[2,1,24,768]{3,2,1,0:T(8,128)S(1)}, u32[]{:S(2)}, u32[]{:S(2)}) collective-permute-start(f32[2,1,24,768]{3,2,1,0:T(8,128)S(1)} %bitcast_add_fusion.4), channel_id=1, source_target_pairs={{0,16},{1,17},{2,18},{3,19},{4,20},{5,21},{6,22},{7,23},{8,24},{9,... | collective-permute-start | bytes 442376 | tf_op jit(solution)/shard_map/ppermute | solution.py:565
  157.6 5.3 %collective-permute-done.35 = f32[2,1,24,768]{3,2,1,0:T(8,128)S(1)} collective-permute-done((f32[2,1,24,768]{3,2,1,0:T(8,128)S(1)}, f32[2,1,24,768]{3,2,1,0:T(8,128)S(1)}, u32[]{:S(2)}, u32[]{:S(2)}) %collective-permute-start.35) | collective-permute-done | bytes 147488 | tf_op jit(solution)/shard_map/ppermute | solution.py:565
  163.1 1.6 collective-permute-start.22
  164.6 2.2 collective-permute-done.22
  166.9 5.0 %collective-permute-done.36 = f32[2,24,768]{2,1,0:T(8,128)S(1)} collective-permute-done((f32[2,24,768]{2,1,0:T(8,128)S(1)}, f32[2,24,768]{2,1,0:T(8,128)S(1)}, u32[]{:S(2)}, u32[]{:S(2)}) %collective-permute-start.36) | collective-permute-done | bytes 147488 | tf_op jit(solution)/shard_map/ppermute | solution.py:565
  172.1 2.1 collective-permute-start.23
  174.2 10.2 %collective-permute-done.24 = f32[12,192]{1,0:T(8,128)S(1)} collective-permute-done((f32[12,192]{1,0:T(8,128)S(1)}, f32[12,192]{1,0:T(8,128)S(1)}, u32[]{:S(2)}, u32[]{:S(2)}) %collective-permute-start.24) | collective-permute-done | bytes 9248 | tf_op jit(solution)/shard_map/ppermute | solution.py:565
  185.6 1.9 collective-permute-start.26
  191.0 1.8 collective-permute-start.27
  192.8 3.5 %collective-permute-done.27 = f32[24,768]{1,0:T(8,128)S(1)} collective-permute-done((f32[24,768]{1,0:T(8,128)S(1)}, f32[24,768]{1,0:T(8,128)S(1)}, u32[]{:S(2)}, u32[]{:S(2)}) %collective-permute-start.27) | collective-permute-done | bytes 73760 | tf_op jit(solution)/shard_map/ppermute | solution.py:565
  197.9 6.7 %collective-permute-done.28 = f32[2,24,768]{2,1,0:T(8,128)S(1)} collective-permute-done((f32[2,24,768]{2,1,0:T(8,128)S(1)}, f32[2,24,768]{2,1,0:T(8,128)S(1)}, u32[]{:S(2)}, u32[]{:S(2)}) %collective-permute-start.28) | collective-permute-done | bytes 147488 | tf_op jit(solution)/shard_map/ppermute | solution.py:565
  205.8 5.6 %collective-permute-done.29.refs_1_ = f32[4,24,768]{2,1,0:T(8,128)S(1)} collective-permute-done((f32[4,24,768]{2,1,0:T(8,128)S(1)}, f32[4,24,768]{2,1,0:T(8,128)S(1)}, u32[]{:S(2)}, u32[]{:S(2)}) %collective-permute-start.29) | collective-permute-done | bytes 294944 | tf_op jit(solution)/shard_map/ppermute | solution.py:565
  216.3 3.8 %shard_map.268 = (f32[768,384]{1,0:T(8,128)}, f32[192,1536]{1,0:T(8,128)}) custom-call(s32[3]{0:T(128)} %pad_add_fusion.pos, f32[4,2,24,768]{3,2,1,0:T(8,128)} %bitcast.108, f32[4,2,24,768]{3,2,1,0:T(8,128)} %copy-done.7, f32[4,2,24,768]{3,2,1,0:T(8,128)} %copy-done.8, f32[4,2,24,768]{3,2,1,0:T(8,128)} %copy-done.10), custom_call_target="tpu_custom_call" | custom-call | tf_op jit(solution)/shard_map/pallas_call | solution.py:664
  221.5 3.0 %shard_map.267 = (f32[192,1152]{1,0:T(8,128)}, f32[192,384]{1,0:T(8,128)}) custom-call(s32[3]{0:T(128)} %pad_add_fusion.pos, f32[4,24,768]{2,1,0:T(8,128)} %bitcast.113, f32[4,24,768]{2,1,0:T(8,128)} %copy-done.15, f32[4,24,768]{2,1,0:T(8,128)} %copy-done.16, f32[4,24,768]{2,1,0:T(8,128)} %copy-done.17), custom_call_target="tpu_custom_call" | custom-call | tf_op jit(solution)/shard_map/pallas_call | solution.py:664
  (154 shorter events, 48.0 us)
Async XLA Ops:
  2.2 17.0 %collective-permute-start = (f32[12,192]{1,0:T(8,128)S(1)}, f32[12,192]{1,0:T(8,128)S(1)}, u32[]{:S(2)}, u32[]{:S(2)}) collective-permute-start(f32[12,192]{1,0:T(8,128)S(1)} %concatenate.13), channel_id=1, source_target_pairs={{0,1},{1,0},{2,3},{3,2},{4,5},{5,4},{6,7},{7,6},{8,9},{9,8},{10,11... | collective-permute-start | bytes 27656 | tf_op jit(solution)/shard_map/ppermute | solution.py:565
  6.2 7.0 %collective-permute-start.1 = (f32[48,1152]{1,0:T(8,128)S(1)}, f32[48,1152]{1,0:T(8,128)S(1)}, u32[]{:S(2)}, u32[]{:S(2)}) collective-permute-start(f32[48,1152]{1,0:T(8,128)S(1)} %constant_dynamic-slice_fusion.3), channel_id=1, source_target_pairs={{0,1},{1,0},{2,3},{3,2},{4,5},{5,4},{6,7},{7,6},{8,9},{9,8},{10,11... | collective-permute-start | bytes 663560 | tf_op jit(solution)/shard_map/ppermute | solution.py:565
  16.4 12.9 %collective-permute-start.5 = (f32[48,1920]{1,0:T(8,128)S(1)}, f32[48,1920]{1,0:T(8,128)S(1)}, u32[]{:S(2)}, u32[]{:S(2)}) collective-permute-start(f32[48,1920]{1,0:T(8,128)S(1)} %pad_maximum_fusion.1), channel_id=1, source_target_pairs={{0,1},{1,0},{2,3},{3,2},{4,5},{5,4},{6,7},{7,6},{8,9},{9,8},{10,11... | collective-permute-start | bytes 1105928 | tf_op jit(solution)/shard_map/ppermute | solution.py:565
  19.3 12.3 %collective-permute-start.9 = (f32[192,384]{1,0:T(8,128)S(1)}, f32[192,384]{1,0:T(8,128)S(1)}, u32[]{:S(2)}, u32[]{:S(2)}) collective-permute-start(f32[192,384]{1,0:T(8,128)S(1)} %constant_dynamic-slice_fusion), channel_id=1, source_target_pairs={{0,1},{1,0},{2,3},{3,2},{4,5},{5,4},{6,7},{7,6},{8,9},{9,8},{10,11... | collective-permute-start | bytes 884744 | tf_op jit(solution)/shard_map/ppermute | solution.py:565
  29.3 11.5 %collective-permute-start.6 = (f32[48,1920]{1,0:T(8,128)S(1)}, f32[48,1920]{1,0:T(8,128)S(1)}, u32[]{:S(2)}, u32[]{:S(2)}) collective-permute-start(f32[48,1920]{1,0:T(8,128)S(1)} %collective-permute-done.5.r_8_.r_12_.r_7_), channel_id=1, source_target_pairs={{0,4},{1,5},{2,6},{3,7},{4,0},{5,1},{6,2},{7,3},{8,12},{9,13},{10,... | collective-permute-start | bytes 1105928 | tf_op jit(solution)/shard_map/ppermute | solution.py:565
  31.6 14.7 %collective-permute-start.10 = (f32[192,384]{1,0:T(8,128)S(1)}, f32[192,384]{1,0:T(8,128)S(1)}, u32[]{:S(2)}, u32[]{:S(2)}) collective-permute-start(f32[192,384]{1,0:T(8,128)S(1)} %collective-permute-done.9.r_17_), channel_id=1, source_target_pairs={{0,4},{1,5},{2,6},{3,7},{4,0},{5,1},{6,2},{7,3},{8,12},{9,13},{10,... | collective-permute-start | bytes 884744 | tf_op jit(solution)/shard_map/ppermute | solution.py:565
  32.1 24.1 %collective-permute-start.7 = (f32[48,1920]{1,0:T(8,128)S(1)}, f32[48,1920]{1,0:T(8,128)S(1)}, u32[]{:S(2)}, u32[]{:S(2)}) collective-permute-start(f32[48,1920]{1,0:T(8,128)S(1)} %collective-permute-done.5.r_8_.r_12_.r_7_), channel_id=1, source_target_pairs={{0,2},{1,3},{2,0},{3,1},{4,6},{5,7},{6,4},{7,5},{8,10},{9,11},{10,... | collective-permute-start | bytes 1105928 | tf_op jit(solution)/shard_map/ppermute | solution.py:565
  40.8 15.5 %collective-permute-start.8 = (f32[48,1920]{1,0:T(8,128)S(1)}, f32[48,1920]{1,0:T(8,128)S(1)}, u32[]{:S(2)}, u32[]{:S(2)}) collective-permute-start(f32[48,1920]{1,0:T(8,128)S(1)} %collective-permute-done.6.r_9_.r_13_.r_8_), channel_id=1, source_target_pairs={{0,2},{1,3},{2,0},{3,1},{4,6},{5,7},{6,4},{7,5},{8,10},{9,11},{10,... | collective-permute-start | bytes 1105928 | tf_op jit(solution)/shard_map/ppermute | solution.py:565
  41.5 14.7 %collective-permute-start.11 = (f32[192,384]{1,0:T(8,128)S(1)}, f32[192,384]{1,0:T(8,128)S(1)}, u32[]{:S(2)}, u32[]{:S(2)}) collective-permute-start(f32[192,384]{1,0:T(8,128)S(1)} %collective-permute-done.9.r_17_), channel_id=1, source_target_pairs={{0,2},{1,3},{2,0},{3,1},{4,6},{5,7},{6,4},{7,5},{8,10},{9,11},{10,... | collective-permute-start | bytes 884744 | tf_op jit(solution)/shard_map/ppermute | solution.py:565
  46.4 9.9 %collective-permute-start.12 = (f32[192,384]{1,0:T(8,128)S(1)}, f32[192,384]{1,0:T(8,128)S(1)}, u32[]{:S(2)}, u32[]{:S(2)}) collective-permute-start(f32[192,384]{1,0:T(8,128)S(1)} %collective-permute-done.10.r_18_), channel_id=1, source_target_pairs={{0,2},{1,3},{2,0},{3,1},{4,6},{5,7},{6,4},{7,5},{8,10},{9,11},{10,... | collective-permute-start | bytes 884744 | tf_op jit(solution)/shard_map/ppermute | solution.py:565
  84.0 7.5 %collective-permute-start.13 = (f32[2,192,768]{2,1,0:T(8,128)}, f32[2,192,768]{2,1,0:T(8,128)S(1)}, u32[]{:S(2)}, u32[]{:S(2)}) collective-permute-start(f32[2,192,768]{2,1,0:T(8,128)} %get-tuple-element.64), channel_id=1, source_target_pairs={{0,2},{1,3},{2,0},{3,1},{4,6},{5,7},{6,4},{7,5},{8,10},{9,11},{10,... | collective-permute-start | bytes 3538952 | tf_op jit(solution)/shard_map/ppermute | solution.py:565
  84.5 11.3 %collective-permute-start.14 = (f32[2,192,768]{2,1,0:T(8,128)}, f32[2,192,768]{2,1,0:T(8,128)S(1)}, u32[]{:S(2)}, u32[]{:S(2)}) collective-permute-start(f32[2,192,768]{2,1,0:T(8,128)} %get-tuple-element.66), channel_id=1, source_target_pairs={{0,2},{1,3},{2,0},{3,1},{4,6},{5,7},{6,4},{7,5},{8,10},{9,11},{10,... | collective-permute-start | bytes 3538952 | tf_op jit(solution)/shard_map/ppermute | solution.py:565
  94.8 18.3 %collective-permute-start.15 = (f32[192,768]{1,0:T(8,128)}, f32[192,768]{1,0:T(8,128)S(1)}, u32[]{:S(2)}, u32[]{:S(2)}) collective-permute-start(f32[192,768]{1,0:T(8,128)} %get-tuple-element.94), channel_id=1, source_target_pairs={{0,1},{1,0},{2,3},{3,2},{4,5},{5,4},{6,7},{7,6},{8,9},{9,8},{10,11... | collective-permute-start | bytes 1769480 | tf_op jit(solution)/shard_map/ppermute | solution.py:565
  110.2 30.0 %collective-permute-start.17 = (f32[2,192,768]{2,1,0:T(8,128)}, f32[2,192,768]{2,1,0:T(8,128)S(1)}, u32[]{:S(2)}, u32[]{:S(2)}) collective-permute-start(f32[2,192,768]{2,1,0:T(8,128)} %get-tuple-element.71), channel_id=1, source_target_pairs={{0,2},{1,3},{2,0},{3,1},{4,6},{5,7},{6,4},{7,5},{8,10},{9,11},{10,... | collective-permute-start | bytes 3538952 | tf_op jit(solution)/shard_map/ppermute | solution.py:565
  110.4 16.5 %collective-permute-start.16 = (f32[2,96,768]{2,1,0:T(8,128)}, f32[2,96,768]{2,1,0:T(8,128)}, u32[]{:S(2)}, u32[]{:S(2)}) collective-permute-start(f32[2,96,768]{2,1,0:T(8,128)} %fusion), channel_id=1, source_target_pairs={{0,4},{1,5},{2,6},{3,7},{4,0},{5,1},{6,2},{7,3},{8,12},{9,13},{10,... | collective-permute-start | bytes 1769480 | tf_op jit(solution)/shard_map/ppermute | solution.py:565
  115.0 17.5 %collective-permute-start.33 = (f32[96,768]{1,0:T(8,128)S(1)}, f32[96,768]{1,0:T(8,128)S(1)}, u32[]{:S(2)}, u32[]{:S(2)}) collective-permute-start(f32[96,768]{1,0:T(8,128)S(1)} %get-tuple-element.98), channel_id=1, source_target_pairs={{0,4},{1,5},{2,6},{3,7},{4,0},{5,1},{6,2},{7,3},{8,12},{9,13},{10,... | collective-permute-start | bytes 884744 | tf_op jit(solution)/shard_map/ppermute | solution.py:565
  128.8 8.1 %collective-permute-start.32 = (f32[96,768]{1,0:T(8,128)}, f32[96,768]{1,0:T(8,128)}, u32[]{:S(2)}, u32[]{:S(2)}) collective-permute-start(f32[96,768]{1,0:T(8,128)} %get-tuple-element.100), channel_id=1, source_target_pairs={{0,1},{1,0},{2,3},{3,2},{4,5},{5,4},{6,7},{7,6},{8,9},{9,8},{10,11... | collective-permute-start | bytes 884744 | tf_op jit(solution)/shard_map/ppermute | solution.py:565
  138.7 14.6 %collective-permute-start.34 = (f32[2,2,24,768]{3,2,1,0:T(8,128)}, f32[2,2,24,768]{3,2,1,0:T(8,128)S(1)}, u32[]{:S(2)}, u32[]{:S(2)}) collective-permute-start(f32[2,2,24,768]{3,2,1,0:T(8,128)} %get-tuple-element.95), channel_id=1, source_target_pairs={{0,8},{1,9},{2,10},{3,11},{4,12},{5,13},{6,14},{7,15},{8,0},{9,1},... | collective-permute-start | bytes 884744 | tf_op jit(solution)/shard_map/ppermute | solution.py:565
  141.2 14.8 %collective-permute-start.18 = (f32[192,768]{1,0:T(8,128)}, f32[192,768]{1,0:T(8,128)S(1)}, u32[]{:S(2)}, u32[]{:S(2)}) collective-permute-start(f32[192,768]{1,0:T(8,128)} %get-tuple-element.91), channel_id=1, source_target_pairs={{0,1},{1,0},{2,3},{3,2},{4,5},{5,4},{6,7},{7,6},{8,9},{9,8},{10,11... | collective-permute-start | bytes 1769480 | tf_op jit(solution)/shard_map/ppermute | solution.py:565
  153.3 9.6 %collective-permute-start.35 = (f32[2,1,24,768]{3,2,1,0:T(8,128)S(1)}, f32[2,1,24,768]{3,2,1,0:T(8,128)S(1)}, u32[]{:S(2)}, u32[]{:S(2)}) collective-permute-start(f32[2,1,24,768]{3,2,1,0:T(8,128)S(1)} %bitcast_add_fusion.4), channel_id=1, source_target_pairs={{0,16},{1,17},{2,18},{3,19},{4,20},{5,21},{6,22},{7,23},{8,24},{9,... | collective-permute-start | bytes 442376 | tf_op jit(solution)/shard_map/ppermute | solution.py:565
  156.1 15.9 %collective-permute-start.21 = (f32[96,768]{1,0:T(8,128)S(1)}, f32[96,768]{1,0:T(8,128)S(1)}, u32[]{:S(2)}, u32[]{:S(2)}) collective-permute-start(f32[96,768]{1,0:T(8,128)S(1)} %get-tuple-element.81), channel_id=1, source_target_pairs={{0,4},{1,5},{2,6},{3,7},{4,0},{5,1},{6,2},{7,3},{8,12},{9,13},{10,... | collective-permute-start | bytes 884744 | tf_op jit(solution)/shard_map/ppermute | solution.py:565
  163.0 8.9 %collective-permute-start.36 = (f32[2,24,768]{2,1,0:T(8,128)S(1)}, f32[2,24,768]{2,1,0:T(8,128)S(1)}, u32[]{:S(2)}, u32[]{:S(2)}) collective-permute-start(f32[2,24,768]{2,1,0:T(8,128)S(1)} %bitcast.123), channel_id=1, source_target_pairs={{0,16},{1,17},{2,18},{3,19},{4,20},{5,21},{6,22},{7,23},{8,24},{9,... | collective-permute-start | bytes 442376 | tf_op jit(solution)/shard_map/ppermute | solution.py:565
  171.9 15.5 %collective-permute-start.37 = (f32[2,2,24,768]{3,2,1,0:T(8,128)S(1)}, f32[2,2,24,768]{3,2,1,0:T(8,128)S(1)}, u32[]{:S(2)}, u32[]{:S(2)}) collective-permute-start(f32[2,2,24,768]{3,2,1,0:T(8,128)S(1)} %get-tuple-element.106), channel_id=1, source_target_pairs={{0,8},{1,9},{2,10},{3,11},{4,12},{5,13},{6,14},{7,15},{8,0},{9,1},... | collective-permute-start | bytes 884744 | tf_op jit(solution)/shard_map/ppermute | solution.py:565
  172.1 12.4 %collective-permute-start.23 = (f32[2,24,768]{2,1,0:T(8,128)S(1)}, f32[2,24,768]{2,1,0:T(8,128)S(1)}, u32[]{:S(2)}, u32[]{:S(2)}) collective-permute-start(f32[2,24,768]{2,1,0:T(8,128)S(1)} %get-tuple-element.82), channel_id=1, source_target_pairs={{0,8},{1,9},{2,10},{3,11},{4,12},{5,13},{6,14},{7,15},{8,0},{9,1},... | collective-permute-start | bytes 442376 | tf_op jit(solution)/shard_map/ppermute | solution.py:565
  174.1 10.3 %collective-permute-start.24 = (f32[12,192]{1,0:T(8,128)S(1)}, f32[12,192]{1,0:T(8,128)S(1)}, u32[]{:S(2)}, u32[]{:S(2)}) collective-permute-start(f32[12,192]{1,0:T(8,128)S(1)} %add.324), channel_id=1, source_target_pairs={{0,8},{1,9},{2,10},{3,11},{4,12},{5,13},{6,14},{7,15},{8,0},{9,1},... | collective-permute-start | bytes 27656 | tf_op jit(solution)/shard_map/ppermute | solution.py:565
  187.5 17.7 %collective-permute-start.38 = (f32[4,2,24,768]{3,2,1,0:T(8,128)S(1)}, f32[4,2,24,768]{3,2,1,0:T(8,128)S(1)}, u32[]{:S(2)}, u32[]{:S(2)}) collective-permute-start(f32[4,2,24,768]{3,2,1,0:T(8,128)S(1)} %bitcast.106), channel_id=1, source_target_pairs={{0,4},{1,5},{2,6},{3,7},{4,0},{5,1},{6,2},{7,3},{8,12},{9,13},{10,... | collective-permute-start | bytes 1769480 | tf_op jit(solution)/shard_map/ppermute | solution.py:565
  196.3 8.3 %collective-permute-start.28 = (f32[2,24,768]{2,1,0:T(8,128)S(1)}, f32[2,24,768]{2,1,0:T(8,128)S(1)}, u32[]{:S(2)}, u32[]{:S(2)}) collective-permute-start(f32[2,24,768]{2,1,0:T(8,128)S(1)} %get-tuple-element.108), channel_id=1, source_target_pairs={{0,4},{1,5},{2,6},{3,7},{4,0},{5,1},{6,2},{7,3},{8,12},{9,13},{10,... | collective-permute-start | bytes 442376 | tf_op jit(solution)/shard_map/ppermute | solution.py:565
  204.6 6.8 %collective-permute-start.29 = (f32[4,24,768]{2,1,0:T(8,128)S(1)}, f32[4,24,768]{2,1,0:T(8,128)S(1)}, u32[]{:S(2)}, u32[]{:S(2)}) collective-permute-start(f32[4,24,768]{2,1,0:T(8,128)S(1)} %bitcast.111), channel_id=1, source_target_pairs={{0,8},{1,9},{2,10},{3,11},{4,12},{5,13},{6,14},{7,15},{8,0},{9,1},... | collective-permute-start | bytes 884744 | tf_op jit(solution)/shard_map/ppermute | solution.py:565
  205.2 9.4 %collective-permute-start.39 = (f32[4,2,24,768]{3,2,1,0:T(8,128)S(1)}, f32[4,2,24,768]{3,2,1,0:T(8,128)S(1)}, u32[]{:S(2)}, u32[]{:S(2)}) collective-permute-start(f32[4,2,24,768]{3,2,1,0:T(8,128)S(1)} %bitcast.107), channel_id=1, source_target_pairs={{0,2},{1,3},{2,0},{3,1},{4,6},{5,7},{6,4},{7,5},{8,10},{9,11},{10,... | collective-permute-start | bytes 1769480 | tf_op jit(solution)/shard_map/ppermute | solution.py:565
  205.2 9.4 %collective-permute-start.40 = (f32[4,2,24,768]{3,2,1,0:T(8,128)S(1)}, f32[4,2,24,768]{3,2,1,0:T(8,128)S(1)}, u32[]{:S(2)}, u32[]{:S(2)}) collective-permute-start(f32[4,2,24,768]{3,2,1,0:T(8,128)S(1)} %collective-permute-done.38.refs_1_), channel_id=1, source_target_pairs={{0,2},{1,3},{2,0},{3,1},{4,6},{5,7},{6,4},{7,5},{8,10},{9,11},{10,... | collective-permute-start | bytes 1769480 | tf_op jit(solution)/shard_map/ppermute | solution.py:565
  205.8 14.4 %collective-permute-start.30 = (f32[4,24,768]{2,1,0:T(8,128)S(1)}, f32[4,24,768]{2,1,0:T(8,128)S(1)}, u32[]{:S(2)}, u32[]{:S(2)}) collective-permute-start(f32[4,24,768]{2,1,0:T(8,128)S(1)} %bitcast.112), channel_id=1, source_target_pairs={{0,2},{1,3},{2,0},{3,1},{4,6},{5,7},{6,4},{7,5},{8,10},{9,11},{10,... | collective-permute-start | bytes 884744 | tf_op jit(solution)/shard_map/ppermute | solution.py:565
  211.4 8.7 %collective-permute-start.31 = (f32[4,24,768]{2,1,0:T(8,128)S(1)}, f32[4,24,768]{2,1,0:T(8,128)S(1)}, u32[]{:S(2)}, u32[]{:S(2)}) collective-permute-start(f32[4,24,768]{2,1,0:T(8,128)S(1)} %collective-permute-done.29.refs_1_), channel_id=1, source_target_pairs={{0,2},{1,3},{2,0},{3,1},{4,6},{5,7},{6,4},{7,5},{8,10},{9,11},{10,... | collective-permute-start | bytes 884744 | tf_op jit(solution)/shard_map/ppermute | solution.py:565
  (35 other events, 231.7 us)
where the time goes:
time: 225 us
  waiting for transfers between devices  81.7 us (36%)
  Pallas kernels  77.5 us (34%)
  starting transfers between devices  34.3 us (15%)
  local copies, waits for them, and re-layouts  17.9 us (8%)
  other arithmetic  11.9 us (5%)
    ppermute x41, waiting for transfers between devices, swap_with(): return lax.ppermute(v, ('dp', 'fsdp'), perm)  81.7 us
    pallas_call x5, Pallas kernels, run(): pl.pallas_call(kernel, out_shape=[jax.ShapeDtypeStruct(s, t) for s, t, _...  44 us
    ppermute x41, starting transfers between devices, swap_with(): return lax.ppermute(v, ('dp', 'fsdp'), perm)  34.3 us
    pallas_call x1, Pallas kernels, mlp(): pl.pallas_call(lambda *r: mlp_kernel((n, len(w2[1])), *r), name='mlp', ou...  26.7 us
    add x11, other arithmetic, halve(): both = [pick(got, i, axis) + pick(keep, i, axis) for i in (1 - at, at)]  10.2 us
    unnamed x52, local copies, waits for them, and re-layouts  7.26 us
    pallas_call x2, Pallas kernels, join(): pl.pallas_call(kernel, out_shape=[jax.ShapeDtypeStruct(s, F32) for s in o...  6.81 us
  transfers between devices with their start and end apart: 41, of which 18 were waited for; matrix products, arithmetic and copies ran while one was open for 9% of the time, Pallas kernels for 21%

commit v1 on v0

--- a/solution.py
+++ b/solution.py
@@ -13,7 +13,7 @@
 EPS = 1e-06
 F32 = jnp.float32
 BF16 = jnp.bfloat16
-VMEM_LIMIT = 56 * 1024 * 1024
+MIB = 1 << 20
 
 
 def split(v):
@@ -150,12 +150,13 @@
         keep_ref[i] = g_ref[pl.ds(pl.multiple_of(core * rows, 8), rows), lanes]
 
 
-def part_cols(g_ref, send_ref, keep_ref, core):
+def part_cols(g_ref, send_ref, keep_ref, core, group=0):
     n, rows, cols = keep_ref.shape
+    half = g_ref.shape[1] // 2
     for i in range(n):
-        at = pl.multiple_of((1 - core) * cols, LANES)
+        at = pl.multiple_of((1 - core) * half + group * cols, LANES)
         send_ref[i] = g_ref[i * rows : (i + 1) * rows, pl.ds(at, cols)]
-        at = pl.multiple_of(core * cols, LANES)
+        at = pl.multiple_of(core * half + group * cols, LANES)
         keep_ref[i] = g_ref[i * rows : (i + 1) * rows, pl.ds(at, cols)]
 
 
@@ -299,7 +300,7 @@
 def attn_bwd_kernel(
     offs, x_ref, qkv_ref, ph_ref, pl_ref, ctx_ref, dctx_ref, vec_ref, gp_ref, *refs
 ):
-    dj_ref, send_ref, keep_ref, g_ref = refs
+    dj_ref, send0_ref, keep0_ref, send1_ref, keep1_ref, g_ref = refs
     d = ctx_ref.shape[2]
 
     @pl.when(first())
@@ -341,7 +342,8 @@
 
     @pl.when(last())
     def _():
-        part_cols(g_ref, send_ref, keep_ref, offs[0])
+        part_cols(g_ref, send0_ref, keep0_ref, offs[0], 0)
+        part_cols(g_ref, send1_ref, keep1_ref, offs[0], 1)
 
 
 def input_grad_kernel(np_, offs, x_ref, dj_ref, dmid_ref, vec_ref, *refs):
@@ -393,7 +395,7 @@
     return pl.BlockSpec(shape, lambda i, offs: (0, col))
 
 
-def run(kernel, offs, images, consts, outs, scratch, flops, blocks={}):
+def run(kernel, offs, images, consts, outs, scratch, flops, blocks={}, vmem=12):
     count = images[0].shape[0]
     in_specs = [per_image(a.shape) for a in images] + [
         block_at(*blocks[i]) if i in blocks else fixed(a.shape) for i, a in enumerate(consts)
@@ -411,7 +413,7 @@
         ),
         cost_estimate=pl.CostEstimate(flops=flops, transcendentals=0, bytes_accessed=8 << 20),
         compiler_params=pltpu.CompilerParams(
-            dimension_semantics=("arbitrary",), vmem_limit_bytes=VMEM_LIMIT
+            dimension_semantics=("arbitrary",), vmem_limit_bytes=vmem * MIB
         ),
     )(offs, *images, *consts)
 
@@ -494,7 +496,7 @@
             flops=40 * b * s * d * ff, transcendentals=0, bytes_accessed=8 << 20
         ),
         compiler_params=pltpu.CompilerParams(
-            dimension_semantics=("arbitrary",), vmem_limit_bytes=VMEM_LIMIT
+            dimension_semantics=("arbitrary",), vmem_limit_bytes=56 * MIB
         ),
     )(
         jnp.concatenate([offs, w2[0], core]),
@@ -517,20 +519,22 @@
         pair_scratch(d, d),
         12 * b * s * d * d,
         {2 + i: ((p.shape[0], d), p.shape[1] // d - 1) for i, p in enumerate(pieces)},
+        vmem=56,
     )
 
 
 def attn_bwd(x, qkv, ph, p_lo, ctx, dctx, vec, gwp, core, shards):
     b, s, d = ctx.shape
-    half = const(shards, d // shards, 2 * d)
+    part = const(shards, d // shards, d)
     return run(
         attn_bwd_kernel,
         core,
         [x, qkv, ph, p_lo, ctx, dctx],
         [vec, gwp],
-        [image(b, s, 3 * d), half, half],
+        [image(b, s, 3 * d), part, part, part, part],
         [pltpu.VMEM((d, 4 * d), F32)],
         60 * b * s * d * d,
+        vmem=40,
     )
 
 
@@ -585,18 +589,18 @@
     def over_z(self, v, k):
         return swap_with(v, self.n_dp, 2, 4 * k, 0)
 
-    def quarter(self, w):
+    def quarter(self, w, side):
         rows = w.shape[0] // 4
-        return lax.dynamic_slice_in_dim(w, (2 * self.core + self.x) * rows, rows, 0)
-
-    def quarter_offs(self, rows):
+        return lax.dynamic_slice_in_dim(w, (2 * self.core + side) * rows, rows, 0)
+
+    def quarter_offs(self, rows, side):
         base = (1 - self.y) * rows
         q = rows // 4
-        order = [(c, x) for c in (self.core, 1 - self.core) for x in (self.x, 1 - self.x)]
-        return ints(self.y * rows, *(base + (2 * c + x) * q for c, x in order))
-
-    def finish(self, a):
-        b = self.over_x(a)
+        order = [(c, i) for c in (self.core, 1 - self.core) for i in (side, 1 - side)]
+        return ints(self.y * rows, *(base + (2 * c + i) * q for c, i in order))
+
+    def finish(self, a, over):
+        b = over(a)
         return [a, b, self.over_core(a), self.over_core(b)]
 
     def halve(self, axis, at, got, keep):
@@ -614,24 +618,46 @@
         at = (self.z // (1 << bit)) % 2
         return self.halve(len(shape) - 3, at, got.reshape(shape), keep.reshape(shape))
 
-    def reduce_z(self, got, keep, small=None):
+    def reduce_z(self, got, keep):
         shape = keep.shape
         shape = shape[:-2] + (self.nz, shape[-2] // self.nz, shape[-1])
         got, keep = got.reshape(shape), keep.reshape(shape)
         for bit in range(self.bits):
             send, keep = self.halve_z(bit, got, keep)
-            if small is not None:
-                send, small = lax.optimization_barrier((send, small))
-                small = small + self.over_z(small, 1 << bit)
             got = self.over_z(send, 1 << bit)
         total = got + keep
-        total = total.reshape(total.shape[:-3] + total.shape[-2:])
-        return total if small is None else (total, small)
-
-    def gather_z(self, v, bits):
-        for bit in bits:
+        return total.reshape(total.shape[:-3] + total.shape[-2:])
+
+    def all_reduce_z(self, v):
+        for bit in range(self.bits):
+            v = v + self.over_z(v, 1 << bit)
+        return v
+
+    def gather(self, v):
+        high = list(range(self.bits))[:0:-1]
+        for bit in high[:-1]:
             v = jnp.stack([v, self.over_z(v, 1 << bit)])
-        return v
+        if high:
+            got = self.over_z(v, 1 << high[-1])
+            two = [jnp.stack([v[..., i, :, :], got[..., i, :, :]]) for i in range(2)]
+        else:
+            two = [v[..., i, :, :] for i in range(2)]
+        two = [t.reshape((-1,) + t.shape[-2:]) for t in two]
+        got0 = self.over_x(two[0])
+        got1 = self.over_z(two[1], 1)
+        two = [jnp.concatenate([two[0], got0]), jnp.concatenate([two[1], got1])]
+        got0 = self.over_z(two[0], 1)
+        got1 = self.over_x(two[1])
+        stacks = [two[0], got0, two[1], got1]
+        stacks = stacks + [self.over_core(t) for t in stacks]
+        base = self.placed(high, False)
+        moves = []
+        for dc in range(2):
+            group0 = [(0, dc, dx, dz) for dx in range(2) for _, dz in base]
+            group1 = [(1, dc, 0, dz ^ low) for low in range(2) for _, dz in base]
+            moves += [group0, [(g, c, dx, dz ^ 1) for g, c, dx, dz in group0]]
+            moves += [group1, [(g, c, 1 - dx, dz) for g, c, dx, dz in group1]]
+        return stacks, moves
 
     def placed(self, bits, with_x):
         out = []
@@ -654,9 +680,9 @@
                 @pl.when(pos[0] == core)
                 def _():
                     for ref, places in zip(ins, moves):
-                        for k, (dc, dx, dz) in enumerate(places):
+                        for k, (group, dc, dx, dz) in enumerate(places):
                             row = (pos[1] ^ dx) * nz + (pos[2] ^ dz)
-                            put(ref.at[k], core ^ dc, row, refs)
+                            put(ref.at[k], group, core ^ dc, row, refs)
 
             if finish is not None:
                 finish(refs)
@@ -671,32 +697,33 @@
                 out_specs=[fixed(s) for s in outs],
                 scratch_shapes=list(scratch),
             ),
-            compiler_params=pltpu.CompilerParams(vmem_limit_bytes=VMEM_LIMIT),
+            compiler_params=pltpu.CompilerParams(vmem_limit_bytes=8 * MIB),
         )(ints(self.core, self.x, self.z), *stacks)
 
     def join_attn(self, stacks, moves, d):
+        r = stacks[0].shape[1]
+        rows = 2 * self.nz * r
+
+        def put(ref, group, core, row, refs):
+            at = pl.ds(pl.multiple_of(row * r, 8), r)
+            k = 2 * core + group
+            if k < 3:
+                refs[0][at, k * d : (k + 1) * d] = ref[...]
+            else:
+                refs[1][at, :] = ref[...]
+
+        return self.join(stacks, moves, put, [(rows, 3 * d), (rows, d)])
+
+    def join_mlp(self, stacks, moves):
         _, r, cols = stacks[0].shape
         rows = 2 * self.nz * r
 
-        def put(ref, core, row, refs):
-            at = pl.ds(pl.multiple_of(row * r, 8), r)
-            if core == 0:
-                refs[0][at, :cols] = ref[...]
+        def put(ref, group, core, row, refs):
+            at = pl.multiple_of(row * r, 8)
+            if group == 0:
+                refs[2][pl.ds(core * rows + at, r), :] = ref[...]
             else:
-                n = 3 * d - cols
-                refs[0][at, cols:] = ref[:, :n]
-                refs[1][at, :] = ref[:, n:]
-
-        return self.join(stacks, moves, put, [(rows, 3 * d), (rows, d)])
-
-    def join_mlp(self, stacks, moves):
-        _, _, r, cols = stacks[0].shape
-        rows = 2 * self.nz * r
-
-        def put(ref, core, row, refs):
-            at = pl.multiple_of(row * r, 8)
-            refs[2][pl.ds(core * rows + at, r), :] = ref[0]
-            refs[1][pl.ds(at, r), core * cols : (core + 1) * cols] = ref[1]
+                refs[1][pl.ds(at, r), core * cols : (core + 1) * cols] = ref[...]
 
         def finish(refs):
             refs[0][...] = refs[2][...].T
@@ -728,28 +755,30 @@
         x, ctx, dy, vec, b1f, joint, w_2, zero, n_fsdp
     )
     gwp, gva, dmid, dctx = mlp_mid(dh2, ctx, dy, mid, vec, joint)
-    dj, send0, keep0 = attn_bwd(x, qkv, ph, p_lo, ctx, dctx, vec, gwp, zero, n_fsdp)
+    dj, *parts = attn_bwd(x, qkv, ph, p_lo, ctx, dctx, vec, gwp, zero, n_fsdp)
     gs, dx = input_grad(x, dj, dmid, vec, w_qkv, gva, gb1, gb2, n_fsdp)
-    ga = jnp.concatenate([total(keep0), total(send0)], axis=1)
+    ga = jnp.concatenate([total(parts[i]) for i in (1, 3, 0, 2)], axis=1)
     gw1 = jnp.concatenate([total(keep1), total(send1)], axis=1)
     gw2 = jnp.concatenate([total(keep2), total(send2)], axis=0).T
-    return out, dx, ga[:, : 3 * d], ga[:, 3 * d :], gw1, gw2, total(gs)
+    return out, dx, ga[:, : 3 * d], ga[:, 3 * d :], gw1, gw2, small_grads(total(gs))
 
 
 def pair_step(n_dp, x, vec, b1f, wqkv, wproj, wfc1, wfc2, dy):
     c = Pairs(n_dp)
     core = ints(c.core)
     d = x.shape[2]
-    came = c.over_y(c.quarter(wqkv))
-    w_qkv = c.quarter_offs(wqkv.shape[0]), [wqkv, *c.finish(came)]
-    joint = tie(jnp.concatenate([c.quarter(wfc1), c.quarter(wproj)], axis=1), came)
-    joint = c.over_y(joint)
-    w_2 = c.over_y(tie(c.quarter(wfc2), came))
+    z0 = c.z % 2
+    came = c.over_y(c.quarter(wqkv, c.x))
+    w_qkv = c.quarter_offs(wqkv.shape[0], c.x), [wqkv, *c.finish(came, c.over_x)]
+    joint = [c.quarter(wfc1, c.x), c.quarter(wproj, c.x)]
+    joint = c.over_y(jnp.concatenate(joint, axis=1))
+    w_2 = c.over_y(c.quarter(wfc2, z0))
     qkv = qkv_call(x, vec, w_qkv)
-    pieces = c.finish(tie(joint, qkv))
-    joint = c.quarter_offs(wproj.shape[0]), [wproj, wfc1, *pieces]
+    pieces = c.finish(tie(joint, qkv), c.over_x)
+    joint = c.quarter_offs(wproj.shape[0], c.x), [wproj, wfc1, *pieces]
     ctx, ph, p_lo = attn_fwd(qkv, core)
-    w_2 = c.quarter_offs(wfc2.shape[0]), [wfc2, *c.finish(tie(w_2, qkv))]
+    pieces = c.finish(tie(w_2, qkv), lambda v: c.over_z(v, 1))
+    w_2 = c.quarter_offs(wfc2.shape[0], z0), [wfc2, *pieces]
     out, mid, dh2, gb1, gb2, send2, keep2, send1, keep1 = mlp(
         x, ctx, dy, vec, b1f, joint, w_2, core, 2
     )
@@ -761,45 +790,41 @@
     got2 = c.over_x(send2)
     got1 = c.over_y(send1)
     dctx = tie(dctx, send1, keep1, send2, keep2)
-    dj, send0, keep0 = attn_bwd(x, qkv, ph, p_lo, ctx, dctx, vec, gwp, core, 2)
-    got0 = c.over_core(send0)
+    dj, send3, keep3, send4, keep4 = attn_bwd(x, qkv, ph, p_lo, ctx, dctx, vec, gwp, core, 2)
+    got3 = c.over_core(send3)
+    got4 = c.over_core(send4)
     send2, keep2 = c.halve(0, c.y, got2, keep2)
     send1, keep1 = c.halve_x(got1, keep1)
     got2 = c.over_y(send2)
     got1 = c.over_x(send1)
-    dj = tie(dj, send0, send1, keep1, send2, keep2)
+    dj = tie(dj, send3, send4, send1, keep1, send2, keep2)
     gs, dx = input_grad(x, dj, dmid, vec, w_qkv, gva, gb1, gb2, 2)
-    send0, keep0 = c.halve(0, c.y, got0, keep0)
-    got0 = c.over_y(send0)
-    gs = tie(gs, send0)
-    gs = gs + c.over_core(gs)
-    gs_got = c.over_y(pick(gs, 1 - c.y))
-    gs = pick(gs, c.y)
+    send3, keep3 = c.halve_x(got3, keep3)
+    send4, keep4 = c.halve(0, c.y, got4, keep4)
+    got3 = c.over_x(send3)
+    got4 = c.over_y(send4)
+    gs = gs + c.over_core(tie(gs, send3, send4))
+    gs_y = c.over_y(pick(gs, 1 - c.y))
+    gs = pick(gs, c.y) + gs_y
+    gs_x = c.over_x(gs)
     gotf, keepf = jnp.stack([got2, got1]), jnp.stack([keep2, keep1])
     f = c.reduce_z(gotf, keepf)
-    up = tuple(range(c.bits))
-    f = c.gather_z(f, up[::-1])
-    gs = gs + gs_got
-    gs_got = c.over_x(gs)
-    send0, keep0 = c.halve_x(got0, keep0)
-    got0 = c.over_x(tie(send0, gs))
-    gs = gs + gs_got
-    a, gs = c.reduce_z(got0, keep0, gs)
-    a = c.gather_z(tie(a, gs), up[:0:-1])
-    a = jnp.stack([a, c.over_x(a)])
-    a = a.reshape((-1,) + a.shape[-2:])
-    fr = f.reshape((-1,) + f.shape[-3:])
-    f = [fr, c.over_x(fr)]
-    f = f + [c.over_core(v) for v in f]
-    pf = c.placed(up[::-1], False)
-    pa = c.placed(up[:0:-1], True)
-    mf = [[(i // 2, i % 2, dz) for _, dz in pf] for i in range(4)]
-    ma = [[(i // 2, dx_, dz ^ (i % 2)) for dx_, dz in pa] for i in range(4)]
-    gw2, gw1 = c.join_mlp(f, mf)
-    a = [a, c.over_z(a, 1)]
-    a = a + [c.over_core(v) for v in a]
-    gwqkv, gwproj = c.join_attn(a, ma, d)
-    return out, dx, gwqkv, gwproj, gw1, gw2, gs
+    f, moves_f = c.gather(f)
+    send3, keep3 = c.halve(0, c.y, got3, keep3)
+    send4, keep4 = c.halve_x(got4, keep4)
+    got3 = c.over_y(send3)
+    got4 = c.over_x(send4)
+    gota, keepa = jnp.stack([got3, got4]), jnp.stack([keep3, keep4])
+    a = c.reduce_z(gota, keepa)
+    gs = c.all_reduce_z(gs + gs_x)
+    a, moves_a = c.gather(a)
+    gw2, gw1 = c.join_mlp(f, moves_f)
+    gwqkv, gwproj = c.join_attn(a, moves_a, d)
+    return out, dx, gwqkv, gwproj, gw1, gw2, small_grads(gs)
+
+
+def small_grads(gs):
+    return [*(gs[i] for i in range(8)), gs[8:].reshape(-1)]
 
 
 def is_pairs(n_dp, n_fsdp):
@@ -834,7 +859,7 @@
         gs[5],
         gs[6],
         gw1,
-        gs[8:].reshape(-1),
+        gs[8],
         gw2,
         gs[7],
     )

time: 225 us -> 217 us (0.964)
  waiting for transfers between devices: 81.7 us -> 57.1 us
  starting transfers between devices: 34.3 us -> 51.1 us
  Pallas kernels: 77.5 us -> 65.6 us
  other arithmetic: 11.9 us -> 21.4 us
    ppermute x41 -> x52, waiting for transfers between devices: 81.7 us -> 57.1 us  [swap_with(): return lax.ppermute(v, ('dp', 'fsdp'), perm)]
    ppermute x41 -> x52, starting transfers between devices: 34.3 us -> 51.1 us  [swap_with(): return lax.ppermute(v, ('dp', 'fsdp'), perm)]
    add x11 -> x14, other arithmetic: 10.2 us -> 19.3 us  [halve(): both = [pick(got, i, axis) + pick(keep, i, axis) for i in (1 - at, at)]]
    pallas_call x5, Pallas kernels: 44 us -> 35.2 us  [run(): pl.pallas_call(kernel, out_shape=[jax.ShapeDtypeStruct(s, t) for s, t, _...]
    unnamed x52 -> x92, local copies, waits for them, and re-layouts: 7.26 us -> 10.9 us
    pallas_call x2, Pallas kernels: 6.81 us -> 3.76 us  [join(): pl.pallas_call(kernel, out_shape=[jax.ShapeDtypeStruct(s, F32) for s in o...]
  transfers between devices with their start and end apart: 41 -> 52, of which waited for: 18 -> 17; matrix products, arithmetic and copies ran while one was open for 9% -> 13% of each run, Pallas kernels for 21% -> 17%
where the time goes in v1:
time: 217 us; the launch traced here: 216 us
  Pallas kernels  65.6 us (30%)
  waiting for transfers between devices  57.1 us (26%)
  starting transfers between devices  51.1 us (24%)
  other arithmetic  21.4 us (10%)
  local copies, waits for them, and re-layouts  19.9 us (9%)
    ppermute x52, waiting for transfers between devices, swap_with(): return lax.ppermute(v, ('dp', 'fsdp'), perm)  57.1 us
    ppermute x52, starting transfers between devices, swap_with(): return lax.ppermute(v, ('dp', 'fsdp'), perm)  51.1 us
    pallas_call x5, Pallas kernels, run(): pl.pallas_call(kernel, out_shape=[jax.ShapeDtypeStruct(s, t) for s, t, _...  35.2 us
    pallas_call x1, Pallas kernels, mlp(): pl.pallas_call(lambda *r: mlp_kernel((n, len(w2[1])), *r), name='mlp', ou...  26.7 us
    add x14, other arithmetic, halve(): both = [pick(got, i, axis) + pick(keep, i, axis) for i in (1 - at, at)]  19.3 us
    unnamed x92, local copies, waits for them, and re-layouts  10.9 us
    dynamic_slice x4, local copies, waits for them, and re-layouts, quarter(): return lax.dynamic_slice_in_dim(w, (2 * self.core + side) * rows, rows, 0)  4.65 us
  transfers between devices with their start and end apart: 52, of which 17 were waited for; matrix products, arithmetic and copies ran while one was open for 13% of the time, Pallas kernels for 17%

profile of v1, /device:TPU:0, one launch (start us, length us, event | category | flops | bytes accessed | tf_op | source)
XLA Modules:
  0.0 216.4 jit_solution(11877400227020445426)
XLA Ops:
  2.2 3.0 %collective-permute-start = (f32[12,192]{1,0:T(8,128)S(1)}, f32[12,192]{1,0:T(8,128)S(1)}, u32[]{:S(2)}, u32[]{:S(2)}) collective-permute-start(f32[12,192]{1,0:T(8,128)S(1)} %concatenate.31), channel_id=1, source_target_pairs={{0,1},{1,0},{2,3},{3,2},{4,5},{5,4},{6,7},{7,6},{8,9},{9,8},{10,11... | collective-permute-start | bytes 27656 | tf_op jit(solution)/shard_map/ppermute | solution.py:569
  8.2 1.9 collective-permute-start.9
  12.0 2.6 %collective-permute-done.1.r_4_.r_6_ = f32[48,1152]{1,0:T(8,128)S(1)} collective-permute-done((f32[48,1152]{1,0:T(8,128)S(1)}, f32[48,1152]{1,0:T(8,128)S(1)}, u32[]{:S(2)}, u32[]{:S(2)}) %collective-permute-start.1) | collective-permute-done | bytes 221216 | tf_op jit(solution)/shard_map/ppermute | solution.py:569
  16.8 3.7 %collective-permute-done.2.r_5_.r_7_ = f32[48,1152]{1,0:T(8,128)S(1)} collective-permute-done((f32[48,1152]{1,0:T(8,128)S(1)}, f32[48,1152]{1,0:T(8,128)S(1)}, u32[]{:S(2)}, u32[]{:S(2)}) %collective-permute-start.2) | collective-permute-done | bytes 221216 | tf_op jit(solution)/shard_map/ppermute | solution.py:569
  22.0 4.1 %shard_map.262.qkv_ref = f32[3,197,1152]{2,1,0:T(8,128)S(1)} custom-call(s32[5]{0:T(128)S(1)} %stack.148.r_0_, f32[3,197,384]{2,1,0:T(8,128)S(1)} %copy-done.2, f32[8,384]{1,0:T(8,128)S(1)} %reshape.153.r_2_.r_4_.r_5_.vec_ref, f32[192,1152]{1,0:T(8,128)S(1)} %copy-done, f32[48,1152]{1,0:T(8,128)S(1)} %collective-permute-done.1.r_4_.r_6_, ...), custom_call_target="tpu_custom_call" | custom-call | flops 1568636928 | bytes 8388608 | tf_op jit(solution)/shard_map/pallas_call | solution.py:404
  30.8 7.5 %collective-permute-done.6.r_9_.r_13_.r_8_ = f32[48,1920]{1,0:T(8,128)S(1)} collective-permute-done((f32[48,1920]{1,0:T(8,128)S(1)}, f32[48,1920]{1,0:T(8,128)S(1)}, u32[]{:S(2)}, u32[]{:S(2)}) %collective-permute-start.6) | collective-permute-done | bytes 368672 | tf_op jit(solution)/shard_map/ppermute | solution.py:569
  42.0 6.9 %shard_map.263 = (f32[3,197,384]{2,1,0:T(8,128)S(1)}, bf16[3,6,197,197]{3,2,1,0:T(8,128)(2,1)S(1)}, bf16[3,6,197,197]{3,2,1,0:T(8,128)(2,1)S(1)}) custom-call(s32[1]{0:T(128)} %bitcast.10.offs, f32[3,197,1152]{2,1,0:T(8,128)S(1)} %copy-done.28), custom_call_target="tpu_custom_call" | custom-call | flops 2614394880 | bytes 8388608 | tf_op jit(solution)/shard_map/pallas_call | solution.py:404
  53.5 26.7 %mlp.1 = (f32[3,197,384]{2,1,0:T(8,128)}, f32[3,197,384]{2,1,0:T(8,128)}, f32[3,197,384]{2,1,0:T(8,128)}, f32[1,1536]{1,0:T(1,128)}, f32[1,384]{1,0:T(1,128)}, /...) custom-call(s32[11]{0:T(128)} %concatenate.30.r_0_, ...), custom_call_target="tpu_custom_call" | custom-call | flops 13943439360 | bytes 8388608 | tf_op jit(solution)/shard_map/mlp/pallas_call | solution.py:481
  80.8 7.2 %shard_map.264 = (f32[384,384]{1,0:T(8,128)}, f32[8,384]{1,0:T(8,128)}, f32[3,197,384]{2,1,0:T(8,128)}, f32[3,197,384]{2,1,0:T(8,128)}) custom-call(s32[5]{0:T(128)} %copy-done.22, f32[3,197,384]{2,1,0:T(8,128)} %get-tuple-element.53.r_1_, f32[3,197,384]{2,1,0:T(8,128)} %copy-done.6, f32[3,197,384]{2,1,0:T(8,128)} %r_3_.5, ...), custom_call_target="tpu_custom_call" | custom-call | flops 1045757952 | bytes 8388608 | tf_op jit(solution)/shard_map/pallas_call | solution.py:404
  88.1 2.6 %dynamic-slice_add_fusion.1 = (f32[1,192,768]{2,1,0:T(8,128)}, f32[192,768]{1,0:T(8,128)}) fusion(f32[2,192,768]{2,1,0:T(8,128)S(1)} %copy-done.36, s32[]{:T(128)S(6)} %select_n.147, f32[2,192,768]{2,1,0:T(8,128)} %collective-permute-done.13, s32[]{:T(128)S(6)} %select_n.145), kind=kLoop, calls=%fused_computation.11 | loop fusion | flops 294912 | bytes 3538952 | tf_op jit(solution)/shard_map/add | solution.py:607
  92.3 11.5 %shard_map.265 = (f32[3,197,1152]{2,1,0:T(8,128)S(1)}, f32[2,192,384]{2,1,0:T(8,128)}, f32[2,192,384]{2,1,0:T(8,128)S(1)}, f32[2,192,384]{2,1,0:T(8,128)}, f32[2,192,384]{2,1,0:T(8,128)S(1)}) custom-call(s32[1]{0:T(128)} %bitcast.10.offs, f32[3,197,384]{2,1,0:T(8,128)S(1)} %copy-done.3, f32[3,197,1152]{2,1,0:T(8,128)} %copy-done.27, ...), custom_call_target="tpu_custom_call" | custom-call | flops 5228789760 | bytes 8388608 | tf_op jit(solution)/shard_map/pallas_call | solution.py:404
  108.2 2.0 dynamic-slice_add_fusion.2
  116.0 5.9 %collective-permute-done.16 = f32[2,96,768]{2,1,0:T(8,128)} collective-permute-done((f32[2,96,768]{2,1,0:T(8,128)}, f32[2,96,768]{2,1,0:T(8,128)}, u32[]{:S(2)}, u32[]{:S(2)}) %collective-permute-start.16) | collective-permute-done | bytes 589856 | tf_op jit(solution)/shard_map/ppermute | solution.py:569
  121.8 1.9 bitcast_add_fusion.2
  126.2 7.7 %collective-permute-done.24 = f32[2,96,384]{2,1,0:T(8,128)S(1)} collective-permute-done((f32[2,96,384]{2,1,0:T(8,128)S(1)}, f32[2,96,384]{2,1,0:T(8,128)S(1)}, u32[]{:S(2)}, u32[]{:S(2)}) %collective-permute-start.24) | collective-permute-done | bytes 294944 | tf_op jit(solution)/shard_map/ppermute | solution.py:569
  138.2 2.3 %fusion.7 = (f32[2,2,24,768]{3,2,1,0:T(8,128)}, f32[2,2,1,24,768]{4,3,1,0,2:T(8,128)S(1)}) fusion(s32[]{:T(128)S(6)} %select_n.149, f32[1,2,2,24,768]{4,3,2,1,0:T(8,128)} %bitcast.163, f32[1,2,2,24,768]{4,3,2,1,0:T(8,128)} %bitcast.162, f32[1,2,2,24,768]{4,3,2,1,0:T(8,128)} %bitcast.61, f32[1,2,2,24,768]{4,3,2,1,0:T(8,128)} %bitcast.62, s32[]{:T(128)S(6)} %select_n.153), kind=kLoop, calls=%fused_computation.28 | loop fusion | flops 442368 | bytes 1769480 | tf_op jit(solution)/shard_map/add | solution.py:607
  146.6 5.5 %shard_map.266 = (f32[2,12,192]{2,1,0:T(8,128)S(1)}, f32[3,197,384]{2,1,0:T(8,128)}) custom-call(s32[5]{0:T(128)S(1)} %copy-done.23, f32[3,197,384]{2,1,0:T(8,128)S(1)} %copy-done.4, f32[3,197,1152]{2,1,0:T(8,128)S(1)} %get-tuple-element.65.r_2_, f32[3,197,384]{2,1,0:T(8,128)S(1)} %copy-done.5, f32[8,384]{1,0:T(8,128)S(1)} %copy-done.19, ...), custom_call_target="tpu_custom_call" | custom-call | flops 1568636928 | bytes 8388608 | tf_op jit(solution)/shard_map/pallas_call | solution.py:404
  154.9 2.7 %collective-permute-start.29 = (f32[2,1,24,384]{3,2,1,0:T(8,128)S(1)}, f32[2,1,24,384]{3,2,1,0:T(8,128)S(1)}, u32[]{:S(2)}, u32[]{:S(2)}) collective-permute-start(f32[2,1,24,384]{3,2,1,0:T(8,128)S(1)} %bitcast_add_fusion.9), channel_id=1, source_target_pairs={{0,16},{1,17},{2,18},{3,19},{4,20},{5,21},{6,22},{7,23},{8,24},{9,... | collective-permute-start | bytes 221192 | tf_op jit(solution)/shard_map/ppermute | solution.py:569
  158.9 2.6 %collective-permute-done.29 = f32[2,1,24,384]{3,2,1,0:T(8,128)S(1)} collective-permute-done((f32[2,1,24,384]{3,2,1,0:T(8,128)S(1)}, f32[2,1,24,384]{3,2,1,0:T(8,128)S(1)}, u32[]{:S(2)}, u32[]{:S(2)}) %collective-permute-start.29) | collective-permute-done | bytes 73760 | tf_op jit(solution)/shard_map/ppermute | solution.py:569
  162.4 2.2 %collective-permute-start.30 = (f32[2,24,384]{2,1,0:T(8,128)S(1)}, f32[2,24,384]{2,1,0:T(8,128)S(1)}, u32[]{:S(2)}, u32[]{:S(2)}) collective-permute-start(f32[2,24,384]{2,1,0:T(8,128)S(1)} %bitcast.168), channel_id=1, source_target_pairs={{0,16},{1,17},{2,18},{3,19},{4,20},{5,21},{6,22},{7,23},{8,24},{9,... | collective-permute-start | bytes 221192 | tf_op jit(solution)/shard_map/ppermute | solution.py:569
  164.6 5.0 %collective-permute-done.30 = f32[2,24,384]{2,1,0:T(8,128)S(1)} collective-permute-done((f32[2,24,384]{2,1,0:T(8,128)S(1)}, f32[2,24,384]{2,1,0:T(8,128)S(1)}, u32[]{:S(2)}, u32[]{:S(2)}) %collective-permute-start.30) | collective-permute-done | bytes 73760 | tf_op jit(solution)/shard_map/ppermute | solution.py:569
  169.6 2.1 collective-permute-start.31
  171.8 2.6 %collective-permute-start.33 = (f32[2,24,384]{2,1,0:T(8,128)S(1)}, f32[2,24,384]{2,1,0:T(8,128)S(1)}, u32[]{:S(2)}, u32[]{:S(2)}) collective-permute-start(f32[2,24,384]{2,1,0:T(8,128)S(1)} %pad_maximum_fusion.8), channel_id=1, source_target_pairs={{0,8},{1,9},{2,10},{3,11},{4,12},{5,13},{6,14},{7,15},{8,0},{9,1},... | collective-permute-start | bytes 221192 | tf_op jit(solution)/shard_map/ppermute | solution.py:569
  175.4 3.0 %collective-permute-start.43 = (f32[2,24,768]{2,1,0:T(8,128)S(1)}, f32[2,24,768]{2,1,0:T(8,128)S(1)}, u32[]{:S(2)}, u32[]{:S(2)}) collective-permute-start(f32[2,24,768]{2,1,0:T(8,128)S(1)} %bitcast.165), channel_id=1, source_target_pairs={{0,16},{1,17},{2,18},{3,19},{4,20},{5,21},{6,22},{7,23},{8,24},{9,... | collective-permute-start | bytes 442376 | tf_op jit(solution)/shard_map/ppermute | solution.py:569
  178.4 4.4 %collective-permute-done.43 = f32[2,24,768]{2,1,0:T(8,128)S(1)} collective-permute-done((f32[2,24,768]{2,1,0:T(8,128)S(1)}, f32[2,24,768]{2,1,0:T(8,128)S(1)}, u32[]{:S(2)}, u32[]{:S(2)}) %collective-permute-start.43) | collective-permute-done | bytes 147488 | tf_op jit(solution)/shard_map/ppermute | solution.py:569
  183.9 4.2 %collective-permute-done.46 = f32[2,24,768]{2,1,0:T(8,128)S(1)} collective-permute-done((f32[2,24,768]{2,1,0:T(8,128)S(1)}, f32[2,24,768]{2,1,0:T(8,128)S(1)}, u32[]{:S(2)}, u32[]{:S(2)}) %collective-permute-start.46) | collective-permute-done | bytes 147488 | tf_op jit(solution)/shard_map/ppermute | solution.py:569
  189.0 2.4 %collective-permute-start.45 = (f32[4,24,768]{2,1,0:T(8,128)S(1)}, f32[4,24,768]{2,1,0:T(8,128)S(1)}, u32[]{:S(2)}, u32[]{:S(2)}) collective-permute-start(f32[4,24,768]{2,1,0:T(8,128)S(1)} %pad_maximum_fusion.1.refs_0_), channel_id=1, source_target_pairs={{0,8},{1,9},{2,10},{3,11},{4,12},{5,13},{6,14},{7,15},{8,0},{9,1},... | collective-permute-start | bytes 884744 | tf_op jit(solution)/shard_map/ppermute | solution.py:569
  191.7 3.4 %collective-permute-done.21 = f32[12,192]{1,0:T(8,128)S(1)} collective-permute-done((f32[12,192]{1,0:T(8,128)S(1)}, f32[12,192]{1,0:T(8,128)S(1)}, u32[]{:S(2)}, u32[]{:S(2)}) %collective-permute-start.21) | collective-permute-done | bytes 9248 | tf_op jit(solution)/shard_map/ppermute | solution.py:569
  196.8 2.0 collective-permute-done.22
  198.9 2.9 %collective-permute-start.23 = (f32[12,192]{1,0:T(8,128)S(1)}, f32[12,192]{1,0:T(8,128)S(1)}, u32[]{:S(2)}, u32[]{:S(2)}) collective-permute-start(f32[12,192]{1,0:T(8,128)S(1)} %add.359), channel_id=1, source_target_pairs={{0,16},{1,17},{2,18},{3,19},{4,20},{5,21},{6,22},{7,23},{8,24},{9,... | collective-permute-start | bytes 27656 | tf_op jit(solution)/shard_map/ppermute | solution.py:569
  207.4 2.4 %collective-permute-done.32.refs_1_ = f32[4,24,384]{2,1,0:T(8,128)S(1)} collective-permute-done((f32[4,24,384]{2,1,0:T(8,128)S(1)}, f32[4,24,384]{2,1,0:T(8,128)S(1)}, u32[]{:S(2)}, u32[]{:S(2)}) %collective-permute-start.32) | collective-permute-done | bytes 147488 | tf_op jit(solution)/shard_map/ppermute | solution.py:569
  214.3 2.1 shard_map.268
  (227 shorter events, 68.1 us)
Async XLA Ops:
  2.2 18.3 %collective-permute-start = (f32[12,192]{1,0:T(8,128)S(1)}, f32[12,192]{1,0:T(8,128)S(1)}, u32[]{:S(2)}, u32[]{:S(2)}) collective-permute-start(f32[12,192]{1,0:T(8,128)S(1)} %concatenate.31), channel_id=1, source_target_pairs={{0,1},{1,0},{2,3},{3,2},{4,5},{5,4},{6,7},{7,6},{8,9},{9,8},{10,11... | collective-permute-start | bytes 27656 | tf_op jit(solution)/shard_map/ppermute | solution.py:569
  6.2 8.4 %collective-permute-start.1 = (f32[48,1152]{1,0:T(8,128)S(1)}, f32[48,1152]{1,0:T(8,128)S(1)}, u32[]{:S(2)}, u32[]{:S(2)}) collective-permute-start(f32[48,1152]{1,0:T(8,128)S(1)} %constant_dynamic-slice_fusion.3), channel_id=1, source_target_pairs={{0,1},{1,0},{2,3},{3,2},{4,5},{5,4},{6,7},{7,6},{8,9},{9,8},{10,11... | collective-permute-start | bytes 663560 | tf_op jit(solution)/shard_map/ppermute | solution.py:569
  8.2 21.0 %collective-permute-start.9 = (f32[192,384]{1,0:T(8,128)}, f32[192,384]{1,0:T(8,128)}, u32[]{:S(2)}, u32[]{:S(2)}) collective-permute-start(f32[192,384]{1,0:T(8,128)} %constant_dynamic-slice_fusion), channel_id=1, source_target_pairs={{0,1},{1,0},{2,3},{3,2},{4,5},{5,4},{6,7},{7,6},{8,9},{9,8},{10,11... | collective-permute-start | bytes 884744 | tf_op jit(solution)/shard_map/ppermute | solution.py:569
  16.1 11.6 %collective-permute-start.5 = (f32[48,1920]{1,0:T(8,128)S(1)}, f32[48,1920]{1,0:T(8,128)S(1)}, u32[]{:S(2)}, u32[]{:S(2)}) collective-permute-start(f32[48,1920]{1,0:T(8,128)S(1)} %pad_maximum_fusion), channel_id=1, source_target_pairs={{0,1},{1,0},{2,3},{3,2},{4,5},{5,4},{6,7},{7,6},{8,9},{9,8},{10,11... | collective-permute-start | bytes 1105928 | tf_op jit(solution)/shard_map/ppermute | solution.py:569
  27.7 10.6 %collective-permute-start.6 = (f32[48,1920]{1,0:T(8,128)S(1)}, f32[48,1920]{1,0:T(8,128)S(1)}, u32[]{:S(2)}, u32[]{:S(2)}) collective-permute-start(f32[48,1920]{1,0:T(8,128)S(1)} %collective-permute-done.5.r_8_.r_12_.r_7_), channel_id=1, source_target_pairs={{0,4},{1,5},{2,6},{3,7},{4,0},{5,1},{6,2},{7,3},{8,12},{9,13},{10,... | collective-permute-start | bytes 1105928 | tf_op jit(solution)/shard_map/ppermute | solution.py:569
  29.2 10.3 %collective-permute-start.10 = (f32[192,384]{1,0:T(8,128)}, f32[192,384]{1,0:T(8,128)S(1)}, u32[]{:S(2)}, u32[]{:S(2)}) collective-permute-start(f32[192,384]{1,0:T(8,128)} %collective-permute-done.9.r_17_), channel_id=1, source_target_pairs={{0,8},{1,9},{2,10},{3,11},{4,12},{5,13},{6,14},{7,15},{8,0},{9,1},... | collective-permute-start | bytes 884744 | tf_op jit(solution)/shard_map/ppermute | solution.py:569
  30.8 21.7 %collective-permute-start.7 = (f32[48,1920]{1,0:T(8,128)S(1)}, f32[48,1920]{1,0:T(8,128)S(1)}, u32[]{:S(2)}, u32[]{:S(2)}) collective-permute-start(f32[48,1920]{1,0:T(8,128)S(1)} %collective-permute-done.5.r_8_.r_12_.r_7_), channel_id=1, source_target_pairs={{0,2},{1,3},{2,0},{3,1},{4,6},{5,7},{6,4},{7,5},{8,10},{9,11},{10,... | collective-permute-start | bytes 1105928 | tf_op jit(solution)/shard_map/ppermute | solution.py:569
  38.3 14.2 %collective-permute-start.8 = (f32[48,1920]{1,0:T(8,128)S(1)}, f32[48,1920]{1,0:T(8,128)S(1)}, u32[]{:S(2)}, u32[]{:S(2)}) collective-permute-start(f32[48,1920]{1,0:T(8,128)S(1)} %collective-permute-done.6.r_9_.r_13_.r_8_), channel_id=1, source_target_pairs={{0,2},{1,3},{2,0},{3,1},{4,6},{5,7},{6,4},{7,5},{8,10},{9,11},{10,... | collective-permute-start | bytes 1105928 | tf_op jit(solution)/shard_map/ppermute | solution.py:569
  39.0 13.5 %collective-permute-start.11 = (f32[192,384]{1,0:T(8,128)}, f32[192,384]{1,0:T(8,128)S(1)}, u32[]{:S(2)}, u32[]{:S(2)}) collective-permute-start(f32[192,384]{1,0:T(8,128)} %collective-permute-done.9.r_17_), channel_id=1, source_target_pairs={{0,2},{1,3},{2,0},{3,1},{4,6},{5,7},{6,4},{7,5},{8,10},{9,11},{10,... | collective-permute-start | bytes 884744 | tf_op jit(solution)/shard_map/ppermute | solution.py:569
  39.5 13.0 %collective-permute-start.12 = (f32[192,384]{1,0:T(8,128)S(1)}, f32[192,384]{1,0:T(8,128)S(1)}, u32[]{:S(2)}, u32[]{:S(2)}) collective-permute-start(f32[192,384]{1,0:T(8,128)S(1)} %collective-permute-done.10.r_18_), channel_id=1, source_target_pairs={{0,2},{1,3},{2,0},{3,1},{4,6},{5,7},{6,4},{7,5},{8,10},{9,11},{10,... | collective-permute-start | bytes 884744 | tf_op jit(solution)/shard_map/ppermute | solution.py:569
  80.2 7.8 %collective-permute-start.13 = (f32[2,192,768]{2,1,0:T(8,128)}, f32[2,192,768]{2,1,0:T(8,128)}, u32[]{:S(2)}, u32[]{:S(2)}) collective-permute-start(f32[2,192,768]{2,1,0:T(8,128)} %get-tuple-element.56), channel_id=1, source_target_pairs={{0,2},{1,3},{2,0},{3,1},{4,6},{5,7},{6,4},{7,5},{8,10},{9,11},{10,... | collective-permute-start | bytes 3538952 | tf_op jit(solution)/shard_map/ppermute | solution.py:569
  80.7 10.3 %collective-permute-start.14 = (f32[2,192,768]{2,1,0:T(8,128)}, f32[2,192,768]{2,1,0:T(8,128)S(1)}, u32[]{:S(2)}, u32[]{:S(2)}) collective-permute-start(f32[2,192,768]{2,1,0:T(8,128)} %get-tuple-element.58), channel_id=1, source_target_pairs={{0,2},{1,3},{2,0},{3,1},{4,6},{5,7},{6,4},{7,5},{8,10},{9,11},{10,... | collective-permute-start | bytes 3538952 | tf_op jit(solution)/shard_map/ppermute | solution.py:569
  90.6 17.5 %collective-permute-start.15 = (f32[192,768]{1,0:T(8,128)}, f32[192,768]{1,0:T(8,128)}, u32[]{:S(2)}, u32[]{:S(2)}) collective-permute-start(f32[192,768]{1,0:T(8,128)} %get-tuple-element.80), channel_id=1, source_target_pairs={{0,1},{1,0},{2,3},{3,2},{4,5},{5,4},{6,7},{7,6},{8,9},{9,8},{10,11... | collective-permute-start | bytes 1769480 | tf_op jit(solution)/shard_map/ppermute | solution.py:569
  105.3 7.9 %collective-permute-start.18 = (f32[2,192,384]{2,1,0:T(8,128)}, f32[2,192,384]{2,1,0:T(8,128)}, u32[]{:S(2)}, u32[]{:S(2)}) collective-permute-start(f32[2,192,384]{2,1,0:T(8,128)} %get-tuple-element.64), channel_id=1, source_target_pairs={{0,2},{1,3},{2,0},{3,1},{4,6},{5,7},{6,4},{7,5},{8,10},{9,11},{10,... | collective-permute-start | bytes 1769480 | tf_op jit(solution)/shard_map/ppermute | solution.py:569
  105.3 16.5 %collective-permute-start.16 = (f32[2,96,768]{2,1,0:T(8,128)}, f32[2,96,768]{2,1,0:T(8,128)}, u32[]{:S(2)}, u32[]{:S(2)}) collective-permute-start(f32[2,96,768]{2,1,0:T(8,128)} %fusion), channel_id=1, source_target_pairs={{0,4},{1,5},{2,6},{3,7},{4,0},{5,1},{6,2},{7,3},{8,12},{9,13},{10,... | collective-permute-start | bytes 1769480 | tf_op jit(solution)/shard_map/ppermute | solution.py:569
  110.2 27.9 %collective-permute-start.40 = (f32[96,768]{1,0:T(8,128)}, f32[96,768]{1,0:T(8,128)}, u32[]{:S(2)}, u32[]{:S(2)}) collective-permute-start(f32[96,768]{1,0:T(8,128)} %get-tuple-element.84), channel_id=1, source_target_pairs={{0,4},{1,5},{2,6},{3,7},{4,0},{5,1},{6,2},{7,3},{8,12},{9,13},{10,... | collective-permute-start | bytes 884744 | tf_op jit(solution)/shard_map/ppermute | solution.py:569
  111.8 22.1 %collective-permute-start.24 = (f32[2,96,384]{2,1,0:T(8,128)S(1)}, f32[2,96,384]{2,1,0:T(8,128)S(1)}, u32[]{:S(2)}, u32[]{:S(2)}) collective-permute-start(f32[2,96,384]{2,1,0:T(8,128)S(1)} %fusion.12), channel_id=1, source_target_pairs={{0,4},{1,5},{2,6},{3,7},{4,0},{5,1},{6,2},{7,3},{8,12},{9,13},{10,... | collective-permute-start | bytes 884744 | tf_op jit(solution)/shard_map/ppermute | solution.py:569
  114.4 21.4 %collective-permute-start.26 = (f32[192,384]{1,0:T(8,128)S(1)}, f32[192,384]{1,0:T(8,128)S(1)}, u32[]{:S(2)}, u32[]{:S(2)}) collective-permute-start(f32[192,384]{1,0:T(8,128)S(1)} %get-tuple-element.88), channel_id=1, source_target_pairs={{0,1},{1,0},{2,3},{3,2},{4,5},{5,4},{6,7},{7,6},{8,9},{9,8},{10,11... | collective-permute-start | bytes 884744 | tf_op jit(solution)/shard_map/ppermute | solution.py:569
  123.8 14.3 %collective-permute-start.39 = (f32[96,768]{1,0:T(8,128)}, f32[96,768]{1,0:T(8,128)}, u32[]{:S(2)}, u32[]{:S(2)}) collective-permute-start(f32[96,768]{1,0:T(8,128)} %get-tuple-element.86), channel_id=1, source_target_pairs={{0,1},{1,0},{2,3},{3,2},{4,5},{5,4},{6,7},{7,6},{8,9},{9,8},{10,11... | collective-permute-start | bytes 884744 | tf_op jit(solution)/shard_map/ppermute | solution.py:569
  134.7 7.3 %collective-permute-start.25 = (f32[96,384]{1,0:T(8,128)}, f32[96,384]{1,0:T(8,128)S(1)}, u32[]{:S(2)}, u32[]{:S(2)}) collective-permute-start(f32[96,384]{1,0:T(8,128)} %get-tuple-element.93), channel_id=1, source_target_pairs={{0,1},{1,0},{2,3},{3,2},{4,5},{5,4},{6,7},{7,6},{8,9},{9,8},{10,11... | collective-permute-start | bytes 442376 | tf_op jit(solution)/shard_map/ppermute | solution.py:569
  140.4 17.2 %collective-permute-start.41 = (f32[2,2,24,768]{3,2,1,0:T(8,128)}, f32[2,2,24,768]{3,2,1,0:T(8,128)}, u32[]{:S(2)}, u32[]{:S(2)}) collective-permute-start(f32[2,2,24,768]{3,2,1,0:T(8,128)} %get-tuple-element.81), channel_id=1, source_target_pairs={{0,8},{1,9},{2,10},{3,11},{4,12},{5,13},{6,14},{7,15},{8,0},{9,1},... | collective-permute-start | bytes 884744 | tf_op jit(solution)/shard_map/ppermute | solution.py:569
  144.4 9.6 %collective-permute-start.28 = (f32[2,2,24,384]{3,2,1,0:T(8,128)}, f32[2,2,24,384]{3,2,1,0:T(8,128)}, u32[]{:S(2)}, u32[]{:S(2)}) collective-permute-start(f32[2,2,24,384]{3,2,1,0:T(8,128)} %get-tuple-element.89), channel_id=1, source_target_pairs={{0,8},{1,9},{2,10},{3,11},{4,12},{5,13},{6,14},{7,15},{8,0},{9,1},... | collective-permute-start | bytes 442376 | tf_op jit(solution)/shard_map/ppermute | solution.py:569
  153.3 38.0 %collective-permute-start.20 = (f32[12,192]{1,0:T(8,128)S(1)}, f32[12,192]{1,0:T(8,128)S(1)}, u32[]{:S(2)}, u32[]{:S(2)}) collective-permute-start(f32[12,192]{1,0:T(8,128)S(1)} %dynamic-slice_bitcast_fusion), channel_id=1, source_target_pairs={{0,1},{1,0},{2,3},{3,2},{4,5},{5,4},{6,7},{7,6},{8,9},{9,8},{10,11... | collective-permute-start | bytes 27656 | tf_op jit(solution)/shard_map/ppermute | solution.py:569
  158.6 15.9 %collective-permute-start.42 = (f32[2,1,24,768]{3,2,1,0:T(8,128)S(1)}, f32[2,1,24,768]{3,2,1,0:T(8,128)S(1)}, u32[]{:S(2)}, u32[]{:S(2)}) collective-permute-start(f32[2,1,24,768]{3,2,1,0:T(8,128)S(1)} %bitcast_add_fusion.5), channel_id=1, source_target_pairs={{0,16},{1,17},{2,18},{3,19},{4,20},{5,21},{6,22},{7,23},{8,24},{9,... | collective-permute-start | bytes 442376 | tf_op jit(solution)/shard_map/ppermute | solution.py:569
  162.4 7.2 %collective-permute-start.30 = (f32[2,24,384]{2,1,0:T(8,128)S(1)}, f32[2,24,384]{2,1,0:T(8,128)S(1)}, u32[]{:S(2)}, u32[]{:S(2)}) collective-permute-start(f32[2,24,384]{2,1,0:T(8,128)S(1)} %bitcast.168), channel_id=1, source_target_pairs={{0,16},{1,17},{2,18},{3,19},{4,20},{5,21},{6,22},{7,23},{8,24},{9,... | collective-permute-start | bytes 221192 | tf_op jit(solution)/shard_map/ppermute | solution.py:569
  169.6 32.1 %collective-permute-start.31 = (f32[2,24,384]{2,1,0:T(8,128)S(1)}, f32[2,24,384]{2,1,0:T(8,128)S(1)}, u32[]{:S(2)}, u32[]{:S(2)}) collective-permute-start(f32[2,24,384]{2,1,0:T(8,128)S(1)} %pad_maximum_fusion.7), channel_id=1, source_target_pairs={{0,4},{1,5},{2,6},{3,7},{4,0},{5,1},{6,2},{7,3},{8,12},{9,13},{10,... | collective-permute-start | bytes 221192 | tf_op jit(solution)/shard_map/ppermute | solution.py:569
  171.8 12.0 %collective-permute-start.33 = (f32[2,24,384]{2,1,0:T(8,128)S(1)}, f32[2,24,384]{2,1,0:T(8,128)S(1)}, u32[]{:S(2)}, u32[]{:S(2)}) collective-permute-start(f32[2,24,384]{2,1,0:T(8,128)S(1)} %pad_maximum_fusion.8), channel_id=1, source_target_pairs={{0,8},{1,9},{2,10},{3,11},{4,12},{5,13},{6,14},{7,15},{8,0},{9,1},... | collective-permute-start | bytes 221192 | tf_op jit(solution)/shard_map/ppermute | solution.py:569
  175.4 7.4 %collective-permute-start.43 = (f32[2,24,768]{2,1,0:T(8,128)S(1)}, f32[2,24,768]{2,1,0:T(8,128)S(1)}, u32[]{:S(2)}, u32[]{:S(2)}) collective-permute-start(f32[2,24,768]{2,1,0:T(8,128)S(1)} %bitcast.165), channel_id=1, source_target_pairs={{0,16},{1,17},{2,18},{3,19},{4,20},{5,21},{6,22},{7,23},{8,24},{9,... | collective-permute-start | bytes 442376 | tf_op jit(solution)/shard_map/ppermute | solution.py:569
  183.8 19.7 %collective-permute-start.37 = (f32[4,24,384]{2,1,0:T(8,128)S(1)}, f32[4,24,384]{2,1,0:T(8,128)S(1)}, u32[]{:S(2)}, u32[]{:S(2)}) collective-permute-start(f32[4,24,384]{2,1,0:T(8,128)S(1)} %pad_maximum_fusion.4.refs_2_), channel_id=1, source_target_pairs={{0,2},{1,3},{2,0},{3,1},{4,6},{5,7},{6,4},{7,5},{8,10},{9,11},{10,... | collective-permute-start | bytes 442376 | tf_op jit(solution)/shard_map/ppermute | solution.py:569
  188.1 21.7 %collective-permute-start.47 = (f32[4,24,768]{2,1,0:T(8,128)S(1)}, f32[4,24,768]{2,1,0:T(8,128)S(1)}, u32[]{:S(2)}, u32[]{:S(2)}) collective-permute-start(f32[4,24,768]{2,1,0:T(8,128)S(1)} %pad_maximum_fusion.2.refs_2_), channel_id=1, source_target_pairs={{0,4},{1,5},{2,6},{3,7},{4,0},{5,1},{6,2},{7,3},{8,12},{9,13},{10,... | collective-permute-start | bytes 884744 | tf_op jit(solution)/shard_map/ppermute | solution.py:569
  189.0 21.3 %collective-permute-start.45 = (f32[4,24,768]{2,1,0:T(8,128)S(1)}, f32[4,24,768]{2,1,0:T(8,128)S(1)}, u32[]{:S(2)}, u32[]{:S(2)}) collective-permute-start(f32[4,24,768]{2,1,0:T(8,128)S(1)} %pad_maximum_fusion.1.refs_0_), channel_id=1, source_target_pairs={{0,8},{1,9},{2,10},{3,11},{4,12},{5,13},{6,14},{7,15},{8,0},{9,1},... | collective-permute-start | bytes 884744 | tf_op jit(solution)/shard_map/ppermute | solution.py:569
  206.9 7.3 %collective-permute-start.50 = (f32[4,24,768]{2,1,0:T(8,128)S(1)}, f32[4,24,768]{2,1,0:T(8,128)S(1)}, u32[]{:S(2)}, u32[]{:S(2)}) collective-permute-start(f32[4,24,768]{2,1,0:T(8,128)S(1)} %pad_maximum_fusion.2.refs_2_), channel_id=1, source_target_pairs={{0,2},{1,3},{2,0},{3,1},{4,6},{5,7},{6,4},{7,5},{8,10},{9,11},{10,... | collective-permute-start | bytes 884744 | tf_op jit(solution)/shard_map/ppermute | solution.py:569
  (66 other events, 348.3 us)

commit v2 on v1

--- a/solution.py
+++ b/solution.py
@@ -451,7 +451,7 @@
     probs = image(b, heads, s, s, dtype=BF16)
     return run(
         attn_fwd_kernel, zero, [qkv], [], [image(b, s, d), probs, probs], [],
-        30 * b * s * d * d,
+        30 * b * s * d * d, vmem=56,
     )
 
 
@@ -603,30 +603,32 @@
         b = over(a)
         return [a, b, self.over_core(a), self.over_core(b)]
 
-    def halve(self, axis, at, got, keep):
-        both = [pick(got, i, axis) + pick(keep, i, axis) for i in (1 - at, at)]
-        return both[0], both[1]
-
-    def halve_x(self, got, keep):
-        shape = keep.shape
+    def halve(self, axis, at, terms):
+        return sum(pick(t, 1 - at, axis) for t in terms), [pick(t, at, axis) for t in terms]
+
+    def halve_y(self, terms):
+        return self.halve(0, self.y, terms)
+
+    def halve_x(self, terms):
+        shape = terms[0].shape
         shape = shape[:-2] + (2, shape[-2] // 2, shape[-1])
-        return self.halve(len(shape) - 3, self.x, got.reshape(shape), keep.reshape(shape))
-
-    def halve_z(self, bit, got, keep):
-        shape = keep.shape
-        shape = shape[:-3] + (shape[-3] // 2, 2) + shape[-2:]
-        at = (self.z // (1 << bit)) % 2
-        return self.halve(len(shape) - 3, at, got.reshape(shape), keep.reshape(shape))
-
-    def reduce_z(self, got, keep):
-        shape = keep.shape
-        shape = shape[:-2] + (self.nz, shape[-2] // self.nz, shape[-1])
-        got, keep = got.reshape(shape), keep.reshape(shape)
+        return self.halve(len(shape) - 3, self.x, [t.reshape(shape) for t in terms])
+
+    def reduce_z(self, groups):
+        rows, cols = groups[0][0].shape
+        r = rows // self.nz
+        n = self.nz
         for bit in range(self.bits):
-            send, keep = self.halve_z(bit, got, keep)
+            at = (self.z // (1 << bit)) % 2
+            halves = [
+                self.halve(1, at, [t.reshape(n // 2, 2, r, cols) for t in terms])
+                for terms in groups
+            ]
+            send = jnp.stack([h[0] for h in halves])
+            n //= 2
             got = self.over_z(send, 1 << bit)
-        total = got + keep
-        return total.reshape(total.shape[:-3] + total.shape[-2:])
+            groups = [h[1] + [got[i]] for i, h in enumerate(halves)]
+        return jnp.stack([sum(terms).reshape(r, cols) for terms in groups])
 
     def all_reduce_z(self, v):
         for bit in range(self.bits):
@@ -785,37 +787,35 @@
     got2 = c.over_core(send2)
     got1 = c.over_core(send1)
     gwp, gva, dmid, dctx = mlp_mid(dh2, ctx, dy, mid, vec, joint)
-    send2, keep2 = c.halve_x(got2, keep2)
-    send1, keep1 = c.halve(0, c.y, got1, keep1)
+    send2, keep2 = c.halve_x([got2, keep2])
+    send1, keep1 = c.halve_y([got1, keep1])
     got2 = c.over_x(send2)
     got1 = c.over_y(send1)
-    dctx = tie(dctx, send1, keep1, send2, keep2)
+    dctx = tie(dctx, send1, send2)
     dj, send3, keep3, send4, keep4 = attn_bwd(x, qkv, ph, p_lo, ctx, dctx, vec, gwp, core, 2)
     got3 = c.over_core(send3)
     got4 = c.over_core(send4)
-    send2, keep2 = c.halve(0, c.y, got2, keep2)
-    send1, keep1 = c.halve_x(got1, keep1)
+    send2, keep2 = c.halve_y([got2, *keep2])
+    send1, keep1 = c.halve_x([got1, *keep1])
     got2 = c.over_y(send2)
     got1 = c.over_x(send1)
-    dj = tie(dj, send3, send4, send1, keep1, send2, keep2)
+    dj = tie(dj, send3, send4, send1, send2)
     gs, dx = input_grad(x, dj, dmid, vec, w_qkv, gva, gb1, gb2, 2)
-    send3, keep3 = c.halve_x(got3, keep3)
-    send4, keep4 = c.halve(0, c.y, got4, keep4)
+    send3, keep3 = c.halve_x([got3, keep3])
+    send4, keep4 = c.halve_y([got4, keep4])
     got3 = c.over_x(send3)
     got4 = c.over_y(send4)
     gs = gs + c.over_core(tie(gs, send3, send4))
     gs_y = c.over_y(pick(gs, 1 - c.y))
     gs = pick(gs, c.y) + gs_y
     gs_x = c.over_x(gs)
-    gotf, keepf = jnp.stack([got2, got1]), jnp.stack([keep2, keep1])
-    f = c.reduce_z(gotf, keepf)
+    f = c.reduce_z([[got2, *keep2], [got1, *keep1]])
     f, moves_f = c.gather(f)
-    send3, keep3 = c.halve(0, c.y, got3, keep3)
-    send4, keep4 = c.halve_x(got4, keep4)
+    send3, keep3 = c.halve_y([got3, *keep3])
+    send4, keep4 = c.halve_x([got4, *keep4])
     got3 = c.over_y(send3)
     got4 = c.over_x(send4)
-    gota, keepa = jnp.stack([got3, got4]), jnp.stack([keep3, keep4])
-    a = c.reduce_z(gota, keepa)
+    a = c.reduce_z([[got3, *keep3], [got4, *keep4]])
     gs = c.all_reduce_z(gs + gs_x)
     a, moves_a = c.gather(a)
     gw2, gw1 = c.join_mlp(f, moves_f)

time: 217 us -> 192 us (0.88)
  other arithmetic: 21.4 us -> 4.99 us
  starting transfers between devices: 51.1 us -> 41.2 us
  waiting for transfers between devices: 57.1 us -> 64.4 us
  local copies, waits for them, and re-layouts: 19.9 us -> 12.7 us
    add x16 -> x13, other arithmetic: 21.1 us -> 2.75 us  [the longest x11 2.65 us: halve(): sum((pick(t, 1 - at, axis) for t in terms))]
    ppermute x52, starting transfers between devices: 51.1 us -> 41.2 us  [swap_with(): return lax.ppermute(v, ('dp', 'fsdp'), perm)]
    unnamed x92 -> x46, local copies, waits for them, and re-layouts: 10.9 us -> 2.42 us
    ppermute x52, waiting for transfers between devices: 57.1 us -> 64.4 us  [swap_with(): return lax.ppermute(v, ('dp', 'fsdp'), perm)]
  transfers between devices with their start and end apart: 52 -> 52, of which waited for: 17 -> 22; matrix products, arithmetic and copies ran while one was open for 13% -> 7% of each run, Pallas kernels for 17% -> 20%
where the time goes in v2:
time: 192 us; the launch traced here: 191 us
  Pallas kernels  66.8 us (35%)
  waiting for transfers between devices  64.4 us (34%)
  starting transfers between devices  41.2 us (21%)
  local copies, waits for them, and re-layouts  12.7 us (7%)
  other arithmetic  4.99 us (3%)
    ppermute x52, waiting for transfers between devices, swap_with(): return lax.ppermute(v, ('dp', 'fsdp'), perm)  64.4 us
    ppermute x52, starting transfers between devices, swap_with(): return lax.ppermute(v, ('dp', 'fsdp'), perm)  41.2 us
    pallas_call x5, Pallas kernels, run(): pl.pallas_call(kernel, out_shape=[jax.ShapeDtypeStruct(s, t) for s, t, _...  36.4 us
    pallas_call x1, Pallas kernels, mlp(): pl.pallas_call(lambda *r: mlp_kernel((n, len(w2[1])), *r), name='mlp', ou...  26.7 us
    dynamic_slice x4, local copies, waits for them, and re-layouts, quarter(): return lax.dynamic_slice_in_dim(w, (2 * self.core + side) * rows, rows, 0)  4.64 us
  transfers between devices with their start and end apart: 52, of which 22 were waited for; matrix products, arithmetic and copies ran while one was open for 7% of the time, Pallas kernels for 20%

profile of v2, /device:TPU:0, one launch (start us, length us, event | category | flops | bytes accessed | tf_op | source)
XLA Modules:
  0.0 191.3 jit_solution(13443325569553162762)
XLA Ops:
  1.7 3.1 %collective-permute-start.1 = (f32[48,1152]{1,0:T(8,128)S(1)}, f32[48,1152]{1,0:T(8,128)S(1)}, u32[]{:S(2)}, u32[]{:S(2)}) collective-permute-start(f32[48,1152]{1,0:T(8,128)S(1)} %constant_dynamic-slice_fusion.21), channel_id=1, source_target_pairs={{0,1},{1,0},{2,3},{3,2},{4,5},{5,4},{6,7},{7,6},{8,9},{9,8},{10,11... | collective-permute-start | bytes 663560 | tf_op jit(solution)/shard_map/ppermute | solution.py:569
  8.4 1.9 %collective-permute-done.1.r_4_.r_6_ = f32[48,1152]{1,0:T(8,128)S(1)} collective-permute-done((f32[48,1152]{1,0:T(8,128)S(1)}, f32[48,1152]{1,0:T(8,128)S(1)}, u32[]{:S(2)}, u32[]{:S(2)}) %collective-permute-start.1) | collective-permute-done | bytes 221216 | tf_op jit(solution)/shard_map/ppermute | solution.py:569
  10.3 1.7 collective-permute-start.2
  13.6 1.7 constant_dynamic-slice_fusion.18
  18.2 4.1 %shard_map.262.qkv_ref = f32[3,197,1152]{2,1,0:T(8,128)S(1)} custom-call(s32[5]{0:T(128)S(1)} %stack.138.r_0_, f32[3,197,384]{2,1,0:T(8,128)S(1)} %copy-done.1, f32[8,384]{1,0:T(8,128)S(1)} %reshape.761.r_2_.r_4_.r_5_.vec_ref, f32[192,1152]{1,0:T(8,128)S(1)} %copy-done, f32[48,1152]{1,0:T(8,128)S(1)} %collective-permute-done.1.r_4_.r_6_, ...), custom_call_target="tpu_custom_call" | custom-call | flops 1568636928 | bytes 8388608 | tf_op jit(solution)/shard_map/pallas_call | solution.py:404
  25.3 2.3 %collective-permute-done.9.r_17_ = f32[192,384]{1,0:T(8,128)} collective-permute-done((f32[192,384]{1,0:T(8,128)}, f32[192,384]{1,0:T(8,128)}, u32[]{:S(2)}, u32[]{:S(2)}) %collective-permute-start.9) | collective-permute-done | bytes 294944 | tf_op jit(solution)/shard_map/ppermute | solution.py:569
  29.1 5.3 %collective-permute-done.6.r_9_.r_13_.r_8_ = f32[48,1920]{1,0:T(8,128)S(1)} collective-permute-done((f32[48,1920]{1,0:T(8,128)S(1)}, f32[48,1920]{1,0:T(8,128)S(1)}, u32[]{:S(2)}, u32[]{:S(2)}) %collective-permute-start.6) | collective-permute-done | bytes 368672 | tf_op jit(solution)/shard_map/ppermute | solution.py:569
  36.4 9.1 %shard_map.263 = (f32[3,197,384]{2,1,0:T(8,128)}, bf16[3,6,197,197]{3,2,1,0:T(8,128)(2,1)}, bf16[3,6,197,197]{3,2,1,0:T(8,128)(2,1)}) custom-call(s32[1]{0:T(128)} %bitcast.10.offs, f32[3,197,1152]{2,1,0:T(8,128)} %copy-done.14), custom_call_target="tpu_custom_call" | custom-call | flops 2614394880 | bytes 8388608 | tf_op jit(solution)/shard_map/pallas_call | solution.py:404
  46.4 26.7 %mlp.1 = (f32[3,197,384]{2,1,0:T(8,128)}, f32[3,197,384]{2,1,0:T(8,128)}, f32[3,197,384]{2,1,0:T(8,128)}, f32[1,1536]{1,0:T(1,128)}, f32[1,384]{1,0:T(1,128)}, /...) custom-call(s32[11]{0:T(128)} %concatenate.26.r_0_, ...), custom_call_target="tpu_custom_call" | custom-call | flops 13943439360 | bytes 8388608 | tf_op jit(solution)/shard_map/mlp/pallas_call | solution.py:481
  73.7 7.2 %shard_map.264 = (f32[384,384]{1,0:T(8,128)}, f32[8,384]{1,0:T(8,128)}, f32[3,197,384]{2,1,0:T(8,128)}, f32[3,197,384]{2,1,0:T(8,128)}) custom-call(s32[5]{0:T(128)} %copy-done.9, f32[3,197,384]{2,1,0:T(8,128)} %get-tuple-element.53.r_1_, f32[3,197,384]{2,1,0:T(8,128)} %get-tuple-element.47.r_2_.ctx_ref, f32[3,197,384]{2,1,0:T(8,128)} %r_3_.5, ...), custom_call_target="tpu_custom_call" | custom-call | flops 1045757952 | bytes 8388608 | tf_op jit(solution)/shard_map/pallas_call | solution.py:404
  83.8 1.6 constant_dynamic-slice_fusion.17
  85.5 1.6 collective-permute-start.15
  87.1 10.5 %shard_map.265 = (f32[3,197,1152]{2,1,0:T(8,128)S(1)}, f32[2,192,384]{2,1,0:T(8,128)S(1)}, f32[2,192,384]{2,1,0:T(8,128)S(1)}, f32[2,192,384]{2,1,0:T(8,128)S(1)}, f32[2,192,384]{2,1,0:T(8,128)S(1)}) custom-call(s32[1]{0:T(128)} %bitcast.10.offs, f32[3,197,384]{2,1,0:T(8,128)S(1)} %copy-done.2, f32[3,197,1152]{2,1,0:T(8,128)} %copy-done.14, ...), custom_call_target="tpu_custom_call" | custom-call | flops 5228789760 | bytes 8388608 | tf_op jit(solution)/shard_map/pallas_call | solution.py:404
  103.4 1.6 collective-permute-start.26
  105.0 5.5 %shard_map.266 = (f32[2,12,192]{2,1,0:T(8,128)S(1)}, f32[3,197,384]{2,1,0:T(8,128)}) custom-call(s32[5]{0:T(128)S(1)} %copy-done.10, f32[3,197,384]{2,1,0:T(8,128)S(1)} %copy-done.2, f32[3,197,1152]{2,1,0:T(8,128)S(1)} %get-tuple-element.65.r_2_, f32[3,197,384]{2,1,0:T(8,128)S(1)} %copy-done.4, f32[8,384]{1,0:T(8,128)S(1)} %copy-done.6, ...), custom_call_target="tpu_custom_call" | custom-call | flops 1568636928 | bytes 8388608 | tf_op jit(solution)/shard_map/pallas_call | solution.py:404
  112.3 3.9 %collective-permute-done.24 = f32[2,96,384]{2,1,0:T(8,128)S(1)} collective-permute-done((f32[2,96,384]{2,1,0:T(8,128)S(1)}, f32[2,96,384]{2,1,0:T(8,128)S(1)}, u32[]{:S(2)}, u32[]{:S(2)}) %collective-permute-start.24) | collective-permute-done | bytes 294944 | tf_op jit(solution)/shard_map/ppermute | solution.py:569
  118.4 3.0 %collective-permute-done.25 = f32[96,384]{1,0:T(8,128)S(1)} collective-permute-done((f32[96,384]{1,0:T(8,128)S(1)}, f32[96,384]{1,0:T(8,128)S(1)}, u32[]{:S(2)}, u32[]{:S(2)}) %collective-permute-start.25) | collective-permute-done | bytes 147488 | tf_op jit(solution)/shard_map/ppermute | solution.py:569
  123.0 1.6 collective-permute-start.28
  125.2 5.3 %collective-permute-done.28 = f32[2,2,24,384]{3,2,1,0:T(8,128)S(1)} collective-permute-done((f32[2,2,24,384]{3,2,1,0:T(8,128)S(1)}, f32[2,2,24,384]{3,2,1,0:T(8,128)S(1)}, u32[]{:S(2)}, u32[]{:S(2)}) %collective-permute-start.28) | collective-permute-done | bytes 147488 | tf_op jit(solution)/shard_map/ppermute | solution.py:569
  130.5 1.9 %collective-permute-start.29 = (f32[2,1,24,384]{3,2,1,0:T(8,128)S(1)}, f32[2,1,24,384]{3,2,1,0:T(8,128)S(1)}, u32[]{:S(2)}, u32[]{:S(2)}) collective-permute-start(f32[2,1,24,384]{3,2,1,0:T(8,128)S(1)} %pad_maximum_fusion.13), channel_id=1, source_target_pairs={{0,16},{1,17},{2,18},{3,19},{4,20},{5,21},{6,22},{7,23},{8,24},{9,... | collective-permute-start | bytes 221192 | tf_op jit(solution)/shard_map/ppermute | solution.py:569
  133.7 5.6 %collective-permute-done.29 = f32[2,1,24,384]{3,2,1,0:T(8,128)S(1)} collective-permute-done((f32[2,1,24,384]{3,2,1,0:T(8,128)S(1)}, f32[2,1,24,384]{3,2,1,0:T(8,128)S(1)}, u32[]{:S(2)}, u32[]{:S(2)}) %collective-permute-start.29) | collective-permute-done | bytes 73760 | tf_op jit(solution)/shard_map/ppermute | solution.py:569
  139.4 3.0 %collective-permute-start.42 = (f32[2,1,24,768]{3,2,1,0:T(8,128)S(1)}, f32[2,1,24,768]{3,2,1,0:T(8,128)S(1)}, u32[]{:S(2)}, u32[]{:S(2)}) collective-permute-start(f32[2,1,24,768]{3,2,1,0:T(8,128)S(1)} %pad_maximum_fusion.9), channel_id=1, source_target_pairs={{0,16},{1,17},{2,18},{3,19},{4,20},{5,21},{6,22},{7,23},{8,24},{9,... | collective-permute-start | bytes 442376 | tf_op jit(solution)/shard_map/ppermute | solution.py:569
  142.4 5.2 %collective-permute-done.30 = f32[2,24,384]{2,1,0:T(8,128)S(1)} collective-permute-done((f32[2,24,384]{2,1,0:T(8,128)S(1)}, f32[2,24,384]{2,1,0:T(8,128)S(1)}, u32[]{:S(2)}, u32[]{:S(2)}) %collective-permute-start.30) | collective-permute-done | bytes 73760 | tf_op jit(solution)/shard_map/ppermute | solution.py:569
  147.6 4.2 %collective-permute-done.42 = f32[2,1,24,768]{3,2,1,0:T(8,128)S(1)} collective-permute-done((f32[2,1,24,768]{3,2,1,0:T(8,128)S(1)}, f32[2,1,24,768]{3,2,1,0:T(8,128)S(1)}, u32[]{:S(2)}, u32[]{:S(2)}) %collective-permute-start.42) | collective-permute-done | bytes 147488 | tf_op jit(solution)/shard_map/ppermute | solution.py:569
  154.1 4.1 %collective-permute-done.43 = f32[2,24,768]{2,1,0:T(8,128)S(1)} collective-permute-done((f32[2,24,768]{2,1,0:T(8,128)S(1)}, f32[2,24,768]{2,1,0:T(8,128)S(1)}, u32[]{:S(2)}, u32[]{:S(2)}) %collective-permute-start.43) | collective-permute-done | bytes 147488 | tf_op jit(solution)/shard_map/ppermute | solution.py:569
  160.5 3.2 %collective-permute-done.46 = f32[2,24,768]{2,1,0:T(8,128)S(1)} collective-permute-done((f32[2,24,768]{2,1,0:T(8,128)S(1)}, f32[2,24,768]{2,1,0:T(8,128)S(1)}, u32[]{:S(2)}, u32[]{:S(2)}) %collective-permute-start.46) | collective-permute-done | bytes 147488 | tf_op jit(solution)/shard_map/ppermute | solution.py:569
  167.0 3.6 %collective-permute-done.21 = f32[12,192]{1,0:T(8,128)S(1)} collective-permute-done((f32[12,192]{1,0:T(8,128)S(1)}, f32[12,192]{1,0:T(8,128)S(1)}, u32[]{:S(2)}, u32[]{:S(2)}) %collective-permute-start.21) | collective-permute-done | bytes 9248 | tf_op jit(solution)/shard_map/ppermute | solution.py:569
  171.8 2.7 %collective-permute-done.22 = f32[12,192]{1,0:T(8,128)S(1)} collective-permute-done((f32[12,192]{1,0:T(8,128)S(1)}, f32[12,192]{1,0:T(8,128)S(1)}, u32[]{:S(2)}, u32[]{:S(2)}) %collective-permute-start.22) | collective-permute-done | bytes 9248 | tf_op jit(solution)/shard_map/ppermute | solution.py:569
  175.4 3.8 %collective-permute-done.23 = f32[12,192]{1,0:T(8,128)S(1)} collective-permute-done((f32[12,192]{1,0:T(8,128)S(1)}, f32[12,192]{1,0:T(8,128)S(1)}, u32[]{:S(2)}, u32[]{:S(2)}) %collective-permute-start.23) | collective-permute-done | bytes 9248 | tf_op jit(solution)/shard_map/ppermute | solution.py:569
  180.7 3.7 %collective-permute-done.32.refs_1_ = f32[4,24,384]{2,1,0:T(8,128)S(1)} collective-permute-done((f32[4,24,384]{2,1,0:T(8,128)S(1)}, f32[4,24,384]{2,1,0:T(8,128)S(1)}, u32[]{:S(2)}, u32[]{:S(2)}) %collective-permute-start.32) | collective-permute-done | bytes 147488 | tf_op jit(solution)/shard_map/ppermute | solution.py:569
  187.5 1.6 shard_map.267
  189.2 2.1 %shard_map.268 = (f32[768,384]{1,0:T(8,128)}, f32[192,1536]{1,0:T(8,128)}) custom-call(s32[3]{0:T(128)S(1)} %pad_add_fusion.pos, f32[4,24,768]{2,1,0:T(8,128)S(1)} %pad_maximum_fusion.2.refs_0_, f32[4,24,768]{2,1,0:T(8,128)S(1)} %collective-permute-done.45.refs_1_, f32[4,24,768]{2,1,0:T(8,128)S(1)} %pad_maximum_fusion.3.refs_2_, ...), custom_call_target="tpu_custom_call" | custom-call | tf_op jit(solution)/shard_map/pallas_call | solution.py:692
  (193 shorter events, 47.7 us)
Async XLA Ops:
  1.7 8.7 %collective-permute-start.1 = (f32[48,1152]{1,0:T(8,128)S(1)}, f32[48,1152]{1,0:T(8,128)S(1)}, u32[]{:S(2)}, u32[]{:S(2)}) collective-permute-start(f32[48,1152]{1,0:T(8,128)S(1)} %constant_dynamic-slice_fusion.21), channel_id=1, source_target_pairs={{0,1},{1,0},{2,3},{3,2},{4,5},{5,4},{6,7},{7,6},{8,9},{9,8},{10,11... | collective-permute-start | bytes 663560 | tf_op jit(solution)/shard_map/ppermute | solution.py:569
  6.3 10.4 %collective-permute-start = (f32[12,192]{1,0:T(8,128)S(1)}, f32[12,192]{1,0:T(8,128)S(1)}, u32[]{:S(2)}, u32[]{:S(2)}) collective-permute-start(f32[12,192]{1,0:T(8,128)S(1)} %concatenate.27), channel_id=1, source_target_pairs={{0,1},{1,0},{2,3},{3,2},{4,5},{5,4},{6,7},{7,6},{8,9},{9,8},{10,11... | collective-permute-start | bytes 27656 | tf_op jit(solution)/shard_map/ppermute | solution.py:569
  10.3 6.4 %collective-permute-start.2 = (f32[48,1152]{1,0:T(8,128)S(1)}, f32[48,1152]{1,0:T(8,128)S(1)}, u32[]{:S(2)}, u32[]{:S(2)}) collective-permute-start(f32[48,1152]{1,0:T(8,128)S(1)} %collective-permute-done.1.r_4_.r_6_), channel_id=1, source_target_pairs={{0,4},{1,5},{2,6},{3,7},{4,0},{5,1},{6,2},{7,3},{8,12},{9,13},{10,... | collective-permute-start | bytes 663560 | tf_op jit(solution)/shard_map/ppermute | solution.py:569
  12.1 11.8 %collective-permute-start.5 = (f32[48,1920]{1,0:T(8,128)S(1)}, f32[48,1920]{1,0:T(8,128)S(1)}, u32[]{:S(2)}, u32[]{:S(2)}) collective-permute-start(f32[48,1920]{1,0:T(8,128)S(1)} %pad_maximum_fusion), channel_id=1, source_target_pairs={{0,1},{1,0},{2,3},{3,2},{4,5},{5,4},{6,7},{7,6},{8,9},{9,8},{10,11... | collective-permute-start | bytes 1105928 | tf_op jit(solution)/shard_map/ppermute | solution.py:569
  15.3 12.2 %collective-permute-start.9 = (f32[192,384]{1,0:T(8,128)}, f32[192,384]{1,0:T(8,128)}, u32[]{:S(2)}, u32[]{:S(2)}) collective-permute-start(f32[192,384]{1,0:T(8,128)} %constant_dynamic-slice_fusion.18), channel_id=1, source_target_pairs={{0,1},{1,0},{2,3},{3,2},{4,5},{5,4},{6,7},{7,6},{8,9},{9,8},{10,11... | collective-permute-start | bytes 884744 | tf_op jit(solution)/shard_map/ppermute | solution.py:569
  23.8 10.6 %collective-permute-start.6 = (f32[48,1920]{1,0:T(8,128)S(1)}, f32[48,1920]{1,0:T(8,128)S(1)}, u32[]{:S(2)}, u32[]{:S(2)}) collective-permute-start(f32[48,1920]{1,0:T(8,128)S(1)} %collective-permute-done.5.r_8_.r_12_.r_7_), channel_id=1, source_target_pairs={{0,4},{1,5},{2,6},{3,7},{4,0},{5,1},{6,2},{7,3},{8,12},{9,13},{10,... | collective-permute-start | bytes 1105928 | tf_op jit(solution)/shard_map/ppermute | solution.py:569
  27.6 8.1 %collective-permute-start.10 = (f32[192,384]{1,0:T(8,128)}, f32[192,384]{1,0:T(8,128)}, u32[]{:S(2)}, u32[]{:S(2)}) collective-permute-start(f32[192,384]{1,0:T(8,128)} %collective-permute-done.9.r_17_), channel_id=1, source_target_pairs={{0,8},{1,9},{2,10},{3,11},{4,12},{5,13},{6,14},{7,15},{8,0},{9,1},... | collective-permute-start | bytes 884744 | tf_op jit(solution)/shard_map/ppermute | solution.py:569
  29.1 16.4 %collective-permute-start.7 = (f32[48,1920]{1,0:T(8,128)S(1)}, f32[48,1920]{1,0:T(8,128)S(1)}, u32[]{:S(2)}, u32[]{:S(2)}) collective-permute-start(f32[48,1920]{1,0:T(8,128)S(1)} %collective-permute-done.5.r_8_.r_12_.r_7_), channel_id=1, source_target_pairs={{0,2},{1,3},{2,0},{3,1},{4,6},{5,7},{6,4},{7,5},{8,10},{9,11},{10,... | collective-permute-start | bytes 1105928 | tf_op jit(solution)/shard_map/ppermute | solution.py:569
  34.5 11.1 %collective-permute-start.8 = (f32[48,1920]{1,0:T(8,128)S(1)}, f32[48,1920]{1,0:T(8,128)S(1)}, u32[]{:S(2)}, u32[]{:S(2)}) collective-permute-start(f32[48,1920]{1,0:T(8,128)S(1)} %collective-permute-done.6.r_9_.r_13_.r_8_), channel_id=1, source_target_pairs={{0,2},{1,3},{2,0},{3,1},{4,6},{5,7},{6,4},{7,5},{8,10},{9,11},{10,... | collective-permute-start | bytes 1105928 | tf_op jit(solution)/shard_map/ppermute | solution.py:569
  35.2 10.3 %collective-permute-start.11 = (f32[192,384]{1,0:T(8,128)}, f32[192,384]{1,0:T(8,128)}, u32[]{:S(2)}, u32[]{:S(2)}) collective-permute-start(f32[192,384]{1,0:T(8,128)} %collective-permute-done.9.r_17_), channel_id=1, source_target_pairs={{0,2},{1,3},{2,0},{3,1},{4,6},{5,7},{6,4},{7,5},{8,10},{9,11},{10,... | collective-permute-start | bytes 884744 | tf_op jit(solution)/shard_map/ppermute | solution.py:569
  35.7 9.9 %collective-permute-start.12 = (f32[192,384]{1,0:T(8,128)}, f32[192,384]{1,0:T(8,128)}, u32[]{:S(2)}, u32[]{:S(2)}) collective-permute-start(f32[192,384]{1,0:T(8,128)} %collective-permute-done.10.r_18_), channel_id=1, source_target_pairs={{0,2},{1,3},{2,0},{3,1},{4,6},{5,7},{6,4},{7,5},{8,10},{9,11},{10,... | collective-permute-start | bytes 884744 | tf_op jit(solution)/shard_map/ppermute | solution.py:569
  73.1 7.9 %collective-permute-start.14 = (f32[2,192,768]{2,1,0:T(8,128)}, f32[2,192,768]{2,1,0:T(8,128)}, u32[]{:S(2)}, u32[]{:S(2)}) collective-permute-start(f32[2,192,768]{2,1,0:T(8,128)} %get-tuple-element.58), channel_id=1, source_target_pairs={{0,2},{1,3},{2,0},{3,1},{4,6},{5,7},{6,4},{7,5},{8,10},{9,11},{10,... | collective-permute-start | bytes 3538952 | tf_op jit(solution)/shard_map/ppermute | solution.py:569
  73.6 10.1 %collective-permute-start.13 = (f32[2,192,768]{2,1,0:T(8,128)}, f32[2,192,768]{2,1,0:T(8,128)}, u32[]{:S(2)}, u32[]{:S(2)}) collective-permute-start(f32[2,192,768]{2,1,0:T(8,128)} %get-tuple-element.56), channel_id=1, source_target_pairs={{0,2},{1,3},{2,0},{3,1},{4,6},{5,7},{6,4},{7,5},{8,10},{9,11},{10,... | collective-permute-start | bytes 3538952 | tf_op jit(solution)/shard_map/ppermute | solution.py:569
  82.3 17.0 %collective-permute-start.16 = (f32[2,96,768]{2,1,0:T(8,128)S(1)}, f32[2,96,768]{2,1,0:T(8,128)S(1)}, u32[]{:S(2)}, u32[]{:S(2)}) collective-permute-start(f32[2,96,768]{2,1,0:T(8,128)S(1)} %fusion), channel_id=1, source_target_pairs={{0,4},{1,5},{2,6},{3,7},{4,0},{5,1},{6,2},{7,3},{8,12},{9,13},{10,... | collective-permute-start | bytes 1769480 | tf_op jit(solution)/shard_map/ppermute | solution.py:569
  85.5 15.5 %collective-permute-start.15 = (f32[192,768]{1,0:T(8,128)S(1)}, f32[192,768]{1,0:T(8,128)S(1)}, u32[]{:S(2)}, u32[]{:S(2)}) collective-permute-start(f32[192,768]{1,0:T(8,128)S(1)} %get-tuple-element.80), channel_id=1, source_target_pairs={{0,1},{1,0},{2,3},{3,2},{4,5},{5,4},{6,7},{7,6},{8,9},{9,8},{10,11... | collective-permute-start | bytes 1769480 | tf_op jit(solution)/shard_map/ppermute | solution.py:569
  100.3 18.0 %collective-permute-start.39 = (f32[96,768]{1,0:T(8,128)S(1)}, f32[96,768]{1,0:T(8,128)S(1)}, u32[]{:S(2)}, u32[]{:S(2)}) collective-permute-start(f32[96,768]{1,0:T(8,128)S(1)} %bitcast_add_fusion.2), channel_id=1, source_target_pairs={{0,1},{1,0},{2,3},{3,2},{4,5},{5,4},{6,7},{7,6},{8,9},{9,8},{10,11... | collective-permute-start | bytes 884744 | tf_op jit(solution)/shard_map/ppermute | solution.py:569
  101.1 23.6 %collective-permute-start.40 = (f32[96,768]{1,0:T(8,128)S(1)}, f32[96,768]{1,0:T(8,128)S(1)}, u32[]{:S(2)}, u32[]{:S(2)}) collective-permute-start(f32[96,768]{1,0:T(8,128)S(1)} %get-tuple-element.83), channel_id=1, source_target_pairs={{0,4},{1,5},{2,6},{3,7},{4,0},{5,1},{6,2},{7,3},{8,12},{9,13},{10,... | collective-permute-start | bytes 884744 | tf_op jit(solution)/shard_map/ppermute | solution.py:569
  102.4 13.8 %collective-permute-start.24 = (f32[2,96,384]{2,1,0:T(8,128)S(1)}, f32[2,96,384]{2,1,0:T(8,128)S(1)}, u32[]{:S(2)}, u32[]{:S(2)}) collective-permute-start(f32[2,96,384]{2,1,0:T(8,128)S(1)} %fusion.1), channel_id=1, source_target_pairs={{0,4},{1,5},{2,6},{3,7},{4,0},{5,1},{6,2},{7,3},{8,12},{9,13},{10,... | collective-permute-start | bytes 884744 | tf_op jit(solution)/shard_map/ppermute | solution.py:569
  103.4 14.3 %collective-permute-start.26 = (f32[192,384]{1,0:T(8,128)S(1)}, f32[192,384]{1,0:T(8,128)S(1)}, u32[]{:S(2)}, u32[]{:S(2)}) collective-permute-start(f32[192,384]{1,0:T(8,128)S(1)} %get-tuple-element.87), channel_id=1, source_target_pairs={{0,1},{1,0},{2,3},{3,2},{4,5},{5,4},{6,7},{7,6},{8,9},{9,8},{10,11... | collective-permute-start | bytes 884744 | tf_op jit(solution)/shard_map/ppermute | solution.py:569
  111.7 54.0 %collective-permute-start.20 = (f32[12,192]{1,0:T(8,128)S(1)}, f32[12,192]{1,0:T(8,128)S(1)}, u32[]{:S(2)}, u32[]{:S(2)}) collective-permute-start(f32[12,192]{1,0:T(8,128)S(1)} %fusion.12), channel_id=1, source_target_pairs={{0,1},{1,0},{2,3},{3,2},{4,5},{5,4},{6,7},{7,6},{8,9},{9,8},{10,11... | collective-permute-start | bytes 27656 | tf_op jit(solution)/shard_map/ppermute | solution.py:569
  123.0 7.5 %collective-permute-start.28 = (f32[2,2,24,384]{3,2,1,0:T(8,128)S(1)}, f32[2,2,24,384]{3,2,1,0:T(8,128)S(1)}, u32[]{:S(2)}, u32[]{:S(2)}) collective-permute-start(f32[2,2,24,384]{3,2,1,0:T(8,128)S(1)} %pad_maximum_fusion.6), channel_id=1, source_target_pairs={{0,8},{1,9},{2,10},{3,11},{4,12},{5,13},{6,14},{7,15},{8,0},{9,1},... | collective-permute-start | bytes 442376 | tf_op jit(solution)/shard_map/ppermute | solution.py:569
  124.7 8.9 %collective-permute-start.41 = (f32[2,2,24,768]{3,2,1,0:T(8,128)S(1)}, f32[2,2,24,768]{3,2,1,0:T(8,128)S(1)}, u32[]{:S(2)}, u32[]{:S(2)}) collective-permute-start(f32[2,2,24,768]{3,2,1,0:T(8,128)S(1)} %pad_maximum_fusion.1), channel_id=1, source_target_pairs={{0,8},{1,9},{2,10},{3,11},{4,12},{5,13},{6,14},{7,15},{8,0},{9,1},... | collective-permute-start | bytes 884744 | tf_op jit(solution)/shard_map/ppermute | solution.py:569
  130.5 8.7 %collective-permute-start.29 = (f32[2,1,24,384]{3,2,1,0:T(8,128)S(1)}, f32[2,1,24,384]{3,2,1,0:T(8,128)S(1)}, u32[]{:S(2)}, u32[]{:S(2)}) collective-permute-start(f32[2,1,24,384]{3,2,1,0:T(8,128)S(1)} %pad_maximum_fusion.13), channel_id=1, source_target_pairs={{0,16},{1,17},{2,18},{3,19},{4,20},{5,21},{6,22},{7,23},{8,24},{9,... | collective-permute-start | bytes 221192 | tf_op jit(solution)/shard_map/ppermute | solution.py:569
  139.3 8.3 %collective-permute-start.30 = (f32[2,24,384]{2,1,0:T(8,128)S(1)}, f32[2,24,384]{2,1,0:T(8,128)S(1)}, u32[]{:S(2)}, u32[]{:S(2)}) collective-permute-start(f32[2,24,384]{2,1,0:T(8,128)S(1)} %pad_maximum_fusion.12), channel_id=1, source_target_pairs={{0,16},{1,17},{2,18},{3,19},{4,20},{5,21},{6,22},{7,23},{8,24},{9,... | collective-permute-start | bytes 221192 | tf_op jit(solution)/shard_map/ppermute | solution.py:569
  139.4 12.3 %collective-permute-start.42 = (f32[2,1,24,768]{3,2,1,0:T(8,128)S(1)}, f32[2,1,24,768]{3,2,1,0:T(8,128)S(1)}, u32[]{:S(2)}, u32[]{:S(2)}) collective-permute-start(f32[2,1,24,768]{3,2,1,0:T(8,128)S(1)} %pad_maximum_fusion.9), channel_id=1, source_target_pairs={{0,16},{1,17},{2,18},{3,19},{4,20},{5,21},{6,22},{7,23},{8,24},{9,... | collective-permute-start | bytes 442376 | tf_op jit(solution)/shard_map/ppermute | solution.py:569
  151.8 6.3 %collective-permute-start.43 = (f32[2,24,768]{2,1,0:T(8,128)S(1)}, f32[2,24,768]{2,1,0:T(8,128)S(1)}, u32[]{:S(2)}, u32[]{:S(2)}) collective-permute-start(f32[2,24,768]{2,1,0:T(8,128)S(1)} %pad_maximum_fusion.5), channel_id=1, source_target_pairs={{0,16},{1,17},{2,18},{3,19},{4,20},{5,21},{6,22},{7,23},{8,24},{9,... | collective-permute-start | bytes 442376 | tf_op jit(solution)/shard_map/ppermute | solution.py:569
  151.9 6.9 %collective-permute-start.33 = (f32[2,24,384]{2,1,0:T(8,128)S(1)}, f32[2,24,384]{2,1,0:T(8,128)S(1)}, u32[]{:S(2)}, u32[]{:S(2)}) collective-permute-start(f32[2,24,384]{2,1,0:T(8,128)S(1)} %pad_maximum_fusion.14), channel_id=1, source_target_pairs={{0,8},{1,9},{2,10},{3,11},{4,12},{5,13},{6,14},{7,15},{8,0},{9,1},... | collective-permute-start | bytes 221192 | tf_op jit(solution)/shard_map/ppermute | solution.py:569
  153.5 21.9 %collective-permute-start.31 = (f32[2,24,384]{2,1,0:T(8,128)S(1)}, f32[2,24,384]{2,1,0:T(8,128)S(1)}, u32[]{:S(2)}, u32[]{:S(2)}) collective-permute-start(f32[2,24,384]{2,1,0:T(8,128)S(1)} %pad_maximum_fusion.11), channel_id=1, source_target_pairs={{0,4},{1,5},{2,6},{3,7},{4,0},{5,1},{6,2},{7,3},{8,12},{9,13},{10,... | collective-permute-start | bytes 221192 | tf_op jit(solution)/shard_map/ppermute | solution.py:569
  158.3 7.0 %collective-permute-start.44 = (f32[2,24,768]{2,1,0:T(8,128)S(1)}, f32[2,24,768]{2,1,0:T(8,128)S(1)}, u32[]{:S(2)}, u32[]{:S(2)}) collective-permute-start(f32[2,24,768]{2,1,0:T(8,128)S(1)} %pad_maximum_fusion.4), channel_id=1, source_target_pairs={{0,4},{1,5},{2,6},{3,7},{4,0},{5,1},{6,2},{7,3},{8,12},{9,13},{10,... | collective-permute-start | bytes 442376 | tf_op jit(solution)/shard_map/ppermute | solution.py:569
  158.9 21.2 %collective-permute-start.34 = (f32[4,24,384]{2,1,0:T(8,128)S(1)}, f32[4,24,384]{2,1,0:T(8,128)S(1)}, u32[]{:S(2)}, u32[]{:S(2)}) collective-permute-start(f32[4,24,384]{2,1,0:T(8,128)S(1)} %pad_maximum_fusion.8.refs_2_), channel_id=1, source_target_pairs={{0,4},{1,5},{2,6},{3,7},{4,0},{5,1},{6,2},{7,3},{8,12},{9,13},{10,... | collective-permute-start | bytes 442376 | tf_op jit(solution)/shard_map/ppermute | solution.py:569
  163.7 21.1 %collective-permute-start.47 = (f32[4,24,768]{2,1,0:T(8,128)S(1)}, f32[4,24,768]{2,1,0:T(8,128)S(1)}, u32[]{:S(2)}, u32[]{:S(2)}) collective-permute-start(f32[4,24,768]{2,1,0:T(8,128)S(1)} %pad_maximum_fusion.3.refs_2_), channel_id=1, source_target_pairs={{0,4},{1,5},{2,6},{3,7},{4,0},{5,1},{6,2},{7,3},{8,12},{9,13},{10,... | collective-permute-start | bytes 884744 | tf_op jit(solution)/shard_map/ppermute | solution.py:569
  165.3 19.6 %collective-permute-start.45 = (f32[4,24,768]{2,1,0:T(8,128)S(1)}, f32[4,24,768]{2,1,0:T(8,128)S(1)}, u32[]{:S(2)}, u32[]{:S(2)}) collective-permute-start(f32[4,24,768]{2,1,0:T(8,128)S(1)} %pad_maximum_fusion.2.refs_0_), channel_id=1, source_target_pairs={{0,8},{1,9},{2,10},{3,11},{4,12},{5,13},{6,14},{7,15},{8,0},{9,1},... | collective-permute-start | bytes 884744 | tf_op jit(solution)/shard_map/ppermute | solution.py:569
  (43 other events, 221.5 us)

commit v3 on v2

--- a/solution.py
+++ b/solution.py
@@ -513,13 +513,12 @@
     return run(
         lambda *r: mid_kernel(1 + len(pieces), *r),
         offs,
-        [dh2, ctx, dy, mid],
-        [vec, wp, *pieces],
+        in_hbm([dh2, ctx, dy, mid]),
+        [vec, *in_hbm([wp, *pieces])],
         [const(d, d), const(8, d), image(b, s, d), image(b, s, d)],
         pair_scratch(d, d),
         12 * b * s * d * d,
         {2 + i: ((p.shape[0], d), p.shape[1] // d - 1) for i, p in enumerate(pieces)},
-        vmem=56,
     )
 
 
@@ -551,6 +550,10 @@
         [pltpu.VMEM((3 * d, 3 * d), BF16), pltpu.VMEM((8, d), F32)],
         18 * b * s * d * d,
     )
+
+
+def in_hbm(values):
+    return [pltpu.with_memory_space_constraint(v, pltpu.HBM) for v in values]
 
 
 def tie(v, *after):
@@ -775,7 +778,7 @@
     joint = [c.quarter(wfc1, c.x), c.quarter(wproj, c.x)]
     joint = c.over_y(jnp.concatenate(joint, axis=1))
     w_2 = c.over_y(c.quarter(wfc2, z0))
-    qkv = qkv_call(x, vec, w_qkv)
+    qkv = in_hbm([qkv_call(x, vec, w_qkv)])[0]
     pieces = c.finish(tie(joint, qkv), c.over_x)
     joint = c.quarter_offs(wproj.shape[0], c.x), [wproj, wfc1, *pieces]
     ctx, ph, p_lo = attn_fwd(qkv, core)

time: 192 us -> 191 us (level)
  transfers between devices with their start and end apart: 52 -> 52, of which waited for: 22 -> 22; matrix products, arithmetic and copies ran while one was open for 7% -> 7% of each run, Pallas kernels for 20% -> 19%
where the time goes in v3:
time: 191 us; the launch traced here: 190 us
  Pallas kernels  65.8 us (34%)
  waiting for transfers between devices  64.5 us (34%)
  starting transfers between devices  41.2 us (22%)
  local copies, waits for them, and re-layouts  12.6 us (7%)
  other arithmetic  4.77 us (2%)
    ppermute x52, waiting for transfers between devices, swap_with(): return lax.ppermute(v, ('dp', 'fsdp'), perm)  64.5 us
    ppermute x52, starting transfers between devices, swap_with(): return lax.ppermute(v, ('dp', 'fsdp'), perm)  41.2 us
    pallas_call x5, Pallas kernels, run(): pl.pallas_call(kernel, out_shape=[jax.ShapeDtypeStruct(s, t) for s, t, _...  35.3 us
    pallas_call x1, Pallas kernels, mlp(): pl.pallas_call(lambda *r: mlp_kernel((n, len(w2[1])), *r), name='mlp', ou...  26.8 us
    dynamic_slice x4, local copies, waits for them, and re-layouts, quarter(): return lax.dynamic_slice_in_dim(w, (2 * self.core + side) * rows, rows, 0)  4.64 us
  transfers between devices with their start and end apart: 52, of which 22 were waited for; matrix products, arithmetic and copies ran while one was open for 7% of the time, Pallas kernels for 19%

profile of v3, /device:TPU:0, one launch (start us, length us, event | category | flops | bytes accessed | tf_op | source)
XLA Modules:
  0.0 190.1 jit_solution(13593533795498431475)
XLA Ops:
  1.7 3.1 %collective-permute-start.1 = (f32[48,1152]{1,0:T(8,128)S(1)}, f32[48,1152]{1,0:T(8,128)S(1)}, u32[]{:S(2)}, u32[]{:S(2)}) collective-permute-start(f32[48,1152]{1,0:T(8,128)S(1)} %constant_dynamic-slice_fusion.21), channel_id=1, source_target_pairs={{0,1},{1,0},{2,3},{3,2},{4,5},{5,4},{6,7},{7,6},{8,9},{9,8},{10,11... | collective-permute-start | bytes 663560 | tf_op jit(solution)/shard_map/ppermute | solution.py:572
  8.4 1.9 %collective-permute-done.1.r_4_.r_6_ = f32[48,1152]{1,0:T(8,128)S(1)} collective-permute-done((f32[48,1152]{1,0:T(8,128)S(1)}, f32[48,1152]{1,0:T(8,128)S(1)}, u32[]{:S(2)}, u32[]{:S(2)}) %collective-permute-start.1) | collective-permute-done | bytes 221216 | tf_op jit(solution)/shard_map/ppermute | solution.py:572
  10.3 1.7 collective-permute-start.2
  12.1 1.6 collective-permute-start.5
  13.6 1.7 constant_dynamic-slice_fusion.18
  18.2 4.1 %shard_map.262.qkv_ref = f32[3,197,1152]{2,1,0:T(8,128)S(1)} custom-call(s32[5]{0:T(128)S(1)} %stack.138.r_0_, f32[3,197,384]{2,1,0:T(8,128)S(1)} %copy-done.1, f32[8,384]{1,0:T(8,128)S(1)} %reshape.761.r_2_.r_4_.r_5_.vec_ref, f32[192,1152]{1,0:T(8,128)S(1)} %copy-done, f32[48,1152]{1,0:T(8,128)S(1)} %collective-permute-done.1.r_4_.r_6_, ...), custom_call_target="tpu_custom_call" | custom-call | flops 1568636928 | bytes 8388608 | tf_op jit(solution)/shard_map/pallas_call | solution.py:404
  25.3 2.3 %collective-permute-done.9.r_17_ = f32[192,384]{1,0:T(8,128)} collective-permute-done((f32[192,384]{1,0:T(8,128)}, f32[192,384]{1,0:T(8,128)}, u32[]{:S(2)}, u32[]{:S(2)}) %collective-permute-start.9) | collective-permute-done | bytes 294944 | tf_op jit(solution)/shard_map/ppermute | solution.py:572
  27.6 1.6 collective-permute-start.10
  29.1 5.3 %collective-permute-done.6.r_9_.r_13_.r_8_ = f32[48,1920]{1,0:T(8,128)S(1)} collective-permute-done((f32[48,1920]{1,0:T(8,128)S(1)}, f32[48,1920]{1,0:T(8,128)S(1)}, u32[]{:S(2)}, u32[]{:S(2)}) %collective-permute-start.6) | collective-permute-done | bytes 368672 | tf_op jit(solution)/shard_map/ppermute | solution.py:572
  36.4 9.1 %shard_map.263 = (f32[3,197,384]{2,1,0:T(8,128)}, bf16[3,6,197,197]{3,2,1,0:T(8,128)(2,1)}, bf16[3,6,197,197]{3,2,1,0:T(8,128)(2,1)}) custom-call(s32[1]{0:T(128)} %bitcast.10.offs, f32[3,197,1152]{2,1,0:T(8,128)} %copy-done.8), custom_call_target="tpu_custom_call" | custom-call | flops 2614394880 | bytes 8388608 | tf_op jit(solution)/shard_map/pallas_call | solution.py:404
  46.4 26.8 %mlp.1 = (f32[3,197,384]{2,1,0:T(8,128)}, f32[3,197,384]{2,1,0:T(8,128)}, f32[3,197,384]{2,1,0:T(8,128)}, f32[1,1536]{1,0:T(1,128)}, f32[1,384]{1,0:T(1,128)}, /...) custom-call(s32[11]{0:T(128)} %concatenate.26.r_0_, ...), custom_call_target="tpu_custom_call" | custom-call | flops 13943439360 | bytes 8388608 | tf_op jit(solution)/shard_map/mlp/pallas_call | solution.py:481
  73.9 6.1 %shard_map.264 = (f32[384,384]{1,0:T(8,128)S(1)}, f32[8,384]{1,0:T(8,128)S(1)}, f32[3,197,384]{2,1,0:T(8,128)S(1)}, f32[3,197,384]{2,1,0:T(8,128)S(1)}) custom-call(s32[5]{0:T(128)S(1)} %stack.138.r_0_, f32[3,197,384]{2,1,0:T(8,128)} %get-tuple-element.53.r_1_, f32[3,197,384]{2,1,0:T(8,128)} %get-tuple-element.47.r_2_.ctx_ref, f32[3,197,384]{2,1,0:T(8,128)} %r_3_.5, ...), custom_call_target="tpu_custom_call" | custom-call | flops 1045757952 | bytes 8388608 | tf_op jit(solution)/shard_map/pallas_call | solution.py:404
  85.9 10.5 %shard_map.265 = (f32[3,197,1152]{2,1,0:T(8,128)S(1)}, f32[2,192,384]{2,1,0:T(8,128)S(1)}, f32[2,192,384]{2,1,0:T(8,128)S(1)}, f32[2,192,384]{2,1,0:T(8,128)S(1)}, f32[2,192,384]{2,1,0:T(8,128)S(1)}) custom-call(s32[1]{0:T(128)} %bitcast.10.offs, f32[3,197,384]{2,1,0:T(8,128)S(1)} %copy-done.2, f32[3,197,1152]{2,1,0:T(8,128)} %copy-done.8, ...), custom_call_target="tpu_custom_call" | custom-call | flops 5228789760 | bytes 8388608 | tf_op jit(solution)/shard_map/pallas_call | solution.py:404
  103.8 5.5 %shard_map.266 = (f32[2,12,192]{2,1,0:T(8,128)S(1)}, f32[3,197,384]{2,1,0:T(8,128)}) custom-call(s32[5]{0:T(128)S(1)} %stack.138.r_0_, f32[3,197,384]{2,1,0:T(8,128)S(1)} %copy-done.2, f32[3,197,1152]{2,1,0:T(8,128)S(1)} %get-tuple-element.65.r_2_, f32[3,197,384]{2,1,0:T(8,128)S(1)} %get-tuple-element.66.r_3_, f32[8,384]{1,0:T(8,128)S(1)} %copy-done.5, ...), custom_call_target="tpu_custom_call" | custom-call | flops 1568636928 | bytes 8388608 | tf_op jit(solution)/shard_map/pallas_call | solution.py:404
  111.3 4.0 %collective-permute-done.24 = f32[2,96,384]{2,1,0:T(8,128)S(1)} collective-permute-done((f32[2,96,384]{2,1,0:T(8,128)S(1)}, f32[2,96,384]{2,1,0:T(8,128)S(1)}, u32[]{:S(2)}, u32[]{:S(2)}) %collective-permute-start.24) | collective-permute-done | bytes 294944 | tf_op jit(solution)/shard_map/ppermute | solution.py:572
  117.2 3.3 %collective-permute-done.25 = f32[96,384]{1,0:T(8,128)S(1)} collective-permute-done((f32[96,384]{1,0:T(8,128)S(1)}, f32[96,384]{1,0:T(8,128)S(1)}, u32[]{:S(2)}, u32[]{:S(2)}) %collective-permute-start.25) | collective-permute-done | bytes 147488 | tf_op jit(solution)/shard_map/ppermute | solution.py:572
  121.8 1.7 collective-permute-start.28
  124.1 5.3 %collective-permute-done.28 = f32[2,2,24,384]{3,2,1,0:T(8,128)S(1)} collective-permute-done((f32[2,2,24,384]{3,2,1,0:T(8,128)S(1)}, f32[2,2,24,384]{3,2,1,0:T(8,128)S(1)}, u32[]{:S(2)}, u32[]{:S(2)}) %collective-permute-start.28) | collective-permute-done | bytes 147488 | tf_op jit(solution)/shard_map/ppermute | solution.py:572
  129.4 2.0 %collective-permute-start.29 = (f32[2,1,24,384]{3,2,1,0:T(8,128)S(1)}, f32[2,1,24,384]{3,2,1,0:T(8,128)S(1)}, u32[]{:S(2)}, u32[]{:S(2)}) collective-permute-start(f32[2,1,24,384]{3,2,1,0:T(8,128)S(1)} %pad_maximum_fusion.13), channel_id=1, source_target_pairs={{0,16},{1,17},{2,18},{3,19},{4,20},{5,21},{6,22},{7,23},{8,24},{9,... | collective-permute-start | bytes 221192 | tf_op jit(solution)/shard_map/ppermute | solution.py:572
  132.6 5.6 %collective-permute-done.29 = f32[2,1,24,384]{3,2,1,0:T(8,128)S(1)} collective-permute-done((f32[2,1,24,384]{3,2,1,0:T(8,128)S(1)}, f32[2,1,24,384]{3,2,1,0:T(8,128)S(1)}, u32[]{:S(2)}, u32[]{:S(2)}) %collective-permute-start.29) | collective-permute-done | bytes 73760 | tf_op jit(solution)/shard_map/ppermute | solution.py:572
  138.3 3.0 %collective-permute-start.42 = (f32[2,1,24,768]{3,2,1,0:T(8,128)S(1)}, f32[2,1,24,768]{3,2,1,0:T(8,128)S(1)}, u32[]{:S(2)}, u32[]{:S(2)}) collective-permute-start(f32[2,1,24,768]{3,2,1,0:T(8,128)S(1)} %pad_maximum_fusion.9), channel_id=1, source_target_pairs={{0,16},{1,17},{2,18},{3,19},{4,20},{5,21},{6,22},{7,23},{8,24},{9,... | collective-permute-start | bytes 442376 | tf_op jit(solution)/shard_map/ppermute | solution.py:572
  141.3 5.3 %collective-permute-done.30 = f32[2,24,384]{2,1,0:T(8,128)S(1)} collective-permute-done((f32[2,24,384]{2,1,0:T(8,128)S(1)}, f32[2,24,384]{2,1,0:T(8,128)S(1)}, u32[]{:S(2)}, u32[]{:S(2)}) %collective-permute-start.30) | collective-permute-done | bytes 73760 | tf_op jit(solution)/shard_map/ppermute | solution.py:572
  146.6 4.0 %collective-permute-done.42 = f32[2,1,24,768]{3,2,1,0:T(8,128)S(1)} collective-permute-done((f32[2,1,24,768]{3,2,1,0:T(8,128)S(1)}, f32[2,1,24,768]{3,2,1,0:T(8,128)S(1)}, u32[]{:S(2)}, u32[]{:S(2)}) %collective-permute-start.42) | collective-permute-done | bytes 147488 | tf_op jit(solution)/shard_map/ppermute | solution.py:572
  152.9 4.1 %collective-permute-done.43 = f32[2,24,768]{2,1,0:T(8,128)S(1)} collective-permute-done((f32[2,24,768]{2,1,0:T(8,128)S(1)}, f32[2,24,768]{2,1,0:T(8,128)S(1)}, u32[]{:S(2)}, u32[]{:S(2)}) %collective-permute-start.43) | collective-permute-done | bytes 147488 | tf_op jit(solution)/shard_map/ppermute | solution.py:572
  157.7 1.6 collective-permute-start.34
  159.3 3.2 %collective-permute-done.46 = f32[2,24,768]{2,1,0:T(8,128)S(1)} collective-permute-done((f32[2,24,768]{2,1,0:T(8,128)S(1)}, f32[2,24,768]{2,1,0:T(8,128)S(1)}, u32[]{:S(2)}, u32[]{:S(2)}) %collective-permute-start.46) | collective-permute-done | bytes 147488 | tf_op jit(solution)/shard_map/ppermute | solution.py:572
  165.9 3.6 %collective-permute-done.21 = f32[12,192]{1,0:T(8,128)S(1)} collective-permute-done((f32[12,192]{1,0:T(8,128)S(1)}, f32[12,192]{1,0:T(8,128)S(1)}, u32[]{:S(2)}, u32[]{:S(2)}) %collective-permute-start.21) | collective-permute-done | bytes 9248 | tf_op jit(solution)/shard_map/ppermute | solution.py:572
  170.6 2.6 %collective-permute-done.22 = f32[12,192]{1,0:T(8,128)S(1)} collective-permute-done((f32[12,192]{1,0:T(8,128)S(1)}, f32[12,192]{1,0:T(8,128)S(1)}, u32[]{:S(2)}, u32[]{:S(2)}) %collective-permute-start.22) | collective-permute-done | bytes 9248 | tf_op jit(solution)/shard_map/ppermute | solution.py:572
  174.2 3.8 %collective-permute-done.23 = f32[12,192]{1,0:T(8,128)S(1)} collective-permute-done((f32[12,192]{1,0:T(8,128)S(1)}, f32[12,192]{1,0:T(8,128)S(1)}, u32[]{:S(2)}, u32[]{:S(2)}) %collective-permute-start.23) | collective-permute-done | bytes 9248 | tf_op jit(solution)/shard_map/ppermute | solution.py:572
  179.5 3.6 %collective-permute-done.32.refs_1_ = f32[4,24,384]{2,1,0:T(8,128)S(1)} collective-permute-done((f32[4,24,384]{2,1,0:T(8,128)S(1)}, f32[4,24,384]{2,1,0:T(8,128)S(1)}, u32[]{:S(2)}, u32[]{:S(2)}) %collective-permute-start.32) | collective-permute-done | bytes 147488 | tf_op jit(solution)/shard_map/ppermute | solution.py:572
  186.3 1.6 shard_map.267
  188.0 2.1 %shard_map.268 = (f32[768,384]{1,0:T(8,128)}, f32[192,1536]{1,0:T(8,128)}) custom-call(s32[3]{0:T(128)S(1)} %pad_add_fusion.pos, f32[4,24,768]{2,1,0:T(8,128)S(1)} %pad_maximum_fusion.2.refs_0_, f32[4,24,768]{2,1,0:T(8,128)S(1)} %collective-permute-done.45.refs_1_, f32[4,24,768]{2,1,0:T(8,128)S(1)} %pad_maximum_fusion.3.refs_2_, ...), custom_call_target="tpu_custom_call" | custom-call | tf_op jit(solution)/shard_map/pallas_call | solution.py:695
  (181 shorter events, 47.2 us)
Async XLA Ops:
  1.7 8.7 %collective-permute-start.1 = (f32[48,1152]{1,0:T(8,128)S(1)}, f32[48,1152]{1,0:T(8,128)S(1)}, u32[]{:S(2)}, u32[]{:S(2)}) collective-permute-start(f32[48,1152]{1,0:T(8,128)S(1)} %constant_dynamic-slice_fusion.21), channel_id=1, source_target_pairs={{0,1},{1,0},{2,3},{3,2},{4,5},{5,4},{6,7},{7,6},{8,9},{9,8},{10,11... | collective-permute-start | bytes 663560 | tf_op jit(solution)/shard_map/ppermute | solution.py:572
  6.3 10.4 %collective-permute-start = (f32[12,192]{1,0:T(8,128)S(1)}, f32[12,192]{1,0:T(8,128)S(1)}, u32[]{:S(2)}, u32[]{:S(2)}) collective-permute-start(f32[12,192]{1,0:T(8,128)S(1)} %concatenate.27), channel_id=1, source_target_pairs={{0,1},{1,0},{2,3},{3,2},{4,5},{5,4},{6,7},{7,6},{8,9},{9,8},{10,11... | collective-permute-start | bytes 27656 | tf_op jit(solution)/shard_map/ppermute | solution.py:572
  10.3 6.4 %collective-permute-start.2 = (f32[48,1152]{1,0:T(8,128)S(1)}, f32[48,1152]{1,0:T(8,128)S(1)}, u32[]{:S(2)}, u32[]{:S(2)}) collective-permute-start(f32[48,1152]{1,0:T(8,128)S(1)} %collective-permute-done.1.r_4_.r_6_), channel_id=1, source_target_pairs={{0,4},{1,5},{2,6},{3,7},{4,0},{5,1},{6,2},{7,3},{8,12},{9,13},{10,... | collective-permute-start | bytes 663560 | tf_op jit(solution)/shard_map/ppermute | solution.py:572
  12.1 11.8 %collective-permute-start.5 = (f32[48,1920]{1,0:T(8,128)S(1)}, f32[48,1920]{1,0:T(8,128)S(1)}, u32[]{:S(2)}, u32[]{:S(2)}) collective-permute-start(f32[48,1920]{1,0:T(8,128)S(1)} %pad_maximum_fusion), channel_id=1, source_target_pairs={{0,1},{1,0},{2,3},{3,2},{4,5},{5,4},{6,7},{7,6},{8,9},{9,8},{10,11... | collective-permute-start | bytes 1105928 | tf_op jit(solution)/shard_map/ppermute | solution.py:572
  15.3 12.2 %collective-permute-start.9 = (f32[192,384]{1,0:T(8,128)}, f32[192,384]{1,0:T(8,128)}, u32[]{:S(2)}, u32[]{:S(2)}) collective-permute-start(f32[192,384]{1,0:T(8,128)} %constant_dynamic-slice_fusion.18), channel_id=1, source_target_pairs={{0,1},{1,0},{2,3},{3,2},{4,5},{5,4},{6,7},{7,6},{8,9},{9,8},{10,11... | collective-permute-start | bytes 884744 | tf_op jit(solution)/shard_map/ppermute | solution.py:572
  23.8 10.6 %collective-permute-start.6 = (f32[48,1920]{1,0:T(8,128)S(1)}, f32[48,1920]{1,0:T(8,128)S(1)}, u32[]{:S(2)}, u32[]{:S(2)}) collective-permute-start(f32[48,1920]{1,0:T(8,128)S(1)} %collective-permute-done.5.r_8_.r_12_.r_7_), channel_id=1, source_target_pairs={{0,4},{1,5},{2,6},{3,7},{4,0},{5,1},{6,2},{7,3},{8,12},{9,13},{10,... | collective-permute-start | bytes 1105928 | tf_op jit(solution)/shard_map/ppermute | solution.py:572
  27.6 8.1 %collective-permute-start.10 = (f32[192,384]{1,0:T(8,128)}, f32[192,384]{1,0:T(8,128)}, u32[]{:S(2)}, u32[]{:S(2)}) collective-permute-start(f32[192,384]{1,0:T(8,128)} %collective-permute-done.9.r_17_), channel_id=1, source_target_pairs={{0,8},{1,9},{2,10},{3,11},{4,12},{5,13},{6,14},{7,15},{8,0},{9,1},... | collective-permute-start | bytes 884744 | tf_op jit(solution)/shard_map/ppermute | solution.py:572
  29.1 16.4 %collective-permute-start.7 = (f32[48,1920]{1,0:T(8,128)S(1)}, f32[48,1920]{1,0:T(8,128)S(1)}, u32[]{:S(2)}, u32[]{:S(2)}) collective-permute-start(f32[48,1920]{1,0:T(8,128)S(1)} %collective-permute-done.5.r_8_.r_12_.r_7_), channel_id=1, source_target_pairs={{0,2},{1,3},{2,0},{3,1},{4,6},{5,7},{6,4},{7,5},{8,10},{9,11},{10,... | collective-permute-start | bytes 1105928 | tf_op jit(solution)/shard_map/ppermute | solution.py:572
  34.5 11.1 %collective-permute-start.8 = (f32[48,1920]{1,0:T(8,128)S(1)}, f32[48,1920]{1,0:T(8,128)S(1)}, u32[]{:S(2)}, u32[]{:S(2)}) collective-permute-start(f32[48,1920]{1,0:T(8,128)S(1)} %collective-permute-done.6.r_9_.r_13_.r_8_), channel_id=1, source_target_pairs={{0,2},{1,3},{2,0},{3,1},{4,6},{5,7},{6,4},{7,5},{8,10},{9,11},{10,... | collective-permute-start | bytes 1105928 | tf_op jit(solution)/shard_map/ppermute | solution.py:572
  35.2 10.3 %collective-permute-start.11 = (f32[192,384]{1,0:T(8,128)}, f32[192,384]{1,0:T(8,128)}, u32[]{:S(2)}, u32[]{:S(2)}) collective-permute-start(f32[192,384]{1,0:T(8,128)} %collective-permute-done.9.r_17_), channel_id=1, source_target_pairs={{0,2},{1,3},{2,0},{3,1},{4,6},{5,7},{6,4},{7,5},{8,10},{9,11},{10,... | collective-permute-start | bytes 884744 | tf_op jit(solution)/shard_map/ppermute | solution.py:572
  35.7 9.9 %collective-permute-start.12 = (f32[192,384]{1,0:T(8,128)}, f32[192,384]{1,0:T(8,128)}, u32[]{:S(2)}, u32[]{:S(2)}) collective-permute-start(f32[192,384]{1,0:T(8,128)} %collective-permute-done.10.r_18_), channel_id=1, source_target_pairs={{0,2},{1,3},{2,0},{3,1},{4,6},{5,7},{6,4},{7,5},{8,10},{9,11},{10,... | collective-permute-start | bytes 884744 | tf_op jit(solution)/shard_map/ppermute | solution.py:572
  73.2 6.7 %collective-permute-start.14 = (f32[2,192,768]{2,1,0:T(8,128)}, f32[2,192,768]{2,1,0:T(8,128)}, u32[]{:S(2)}, u32[]{:S(2)}) collective-permute-start(f32[2,192,768]{2,1,0:T(8,128)} %get-tuple-element.58), channel_id=1, source_target_pairs={{0,2},{1,3},{2,0},{3,1},{4,6},{5,7},{6,4},{7,5},{8,10},{9,11},{10,... | collective-permute-start | bytes 3538952 | tf_op jit(solution)/shard_map/ppermute | solution.py:572
  73.8 9.0 %collective-permute-start.13 = (f32[2,192,768]{2,1,0:T(8,128)}, f32[2,192,768]{2,1,0:T(8,128)}, u32[]{:S(2)}, u32[]{:S(2)}) collective-permute-start(f32[2,192,768]{2,1,0:T(8,128)} %get-tuple-element.56), channel_id=1, source_target_pairs={{0,2},{1,3},{2,0},{3,1},{4,6},{5,7},{6,4},{7,5},{8,10},{9,11},{10,... | collective-permute-start | bytes 3538952 | tf_op jit(solution)/shard_map/ppermute | solution.py:572
  81.3 16.9 %collective-permute-start.16 = (f32[2,96,768]{2,1,0:T(8,128)S(1)}, f32[2,96,768]{2,1,0:T(8,128)S(1)}, u32[]{:S(2)}, u32[]{:S(2)}) collective-permute-start(f32[2,96,768]{2,1,0:T(8,128)S(1)} %fusion), channel_id=1, source_target_pairs={{0,4},{1,5},{2,6},{3,7},{4,0},{5,1},{6,2},{7,3},{8,12},{9,13},{10,... | collective-permute-start | bytes 1769480 | tf_op jit(solution)/shard_map/ppermute | solution.py:572
  84.3 15.6 %collective-permute-start.15 = (f32[192,768]{1,0:T(8,128)S(1)}, f32[192,768]{1,0:T(8,128)S(1)}, u32[]{:S(2)}, u32[]{:S(2)}) collective-permute-start(f32[192,768]{1,0:T(8,128)S(1)} %get-tuple-element.80), channel_id=1, source_target_pairs={{0,1},{1,0},{2,3},{3,2},{4,5},{5,4},{6,7},{7,6},{8,9},{9,8},{10,11... | collective-permute-start | bytes 1769480 | tf_op jit(solution)/shard_map/ppermute | solution.py:572
  99.2 18.0 %collective-permute-start.39 = (f32[96,768]{1,0:T(8,128)S(1)}, f32[96,768]{1,0:T(8,128)S(1)}, u32[]{:S(2)}, u32[]{:S(2)}) collective-permute-start(f32[96,768]{1,0:T(8,128)S(1)} %bitcast_add_fusion.2), channel_id=1, source_target_pairs={{0,1},{1,0},{2,3},{3,2},{4,5},{5,4},{6,7},{7,6},{8,9},{9,8},{10,11... | collective-permute-start | bytes 884744 | tf_op jit(solution)/shard_map/ppermute | solution.py:572
  100.1 23.4 %collective-permute-start.40 = (f32[96,768]{1,0:T(8,128)S(1)}, f32[96,768]{1,0:T(8,128)S(1)}, u32[]{:S(2)}, u32[]{:S(2)}) collective-permute-start(f32[96,768]{1,0:T(8,128)S(1)} %get-tuple-element.83), channel_id=1, source_target_pairs={{0,4},{1,5},{2,6},{3,7},{4,0},{5,1},{6,2},{7,3},{8,12},{9,13},{10,... | collective-permute-start | bytes 884744 | tf_op jit(solution)/shard_map/ppermute | solution.py:572
  101.2 14.0 %collective-permute-start.24 = (f32[2,96,384]{2,1,0:T(8,128)S(1)}, f32[2,96,384]{2,1,0:T(8,128)S(1)}, u32[]{:S(2)}, u32[]{:S(2)}) collective-permute-start(f32[2,96,384]{2,1,0:T(8,128)S(1)} %fusion.1), channel_id=1, source_target_pairs={{0,4},{1,5},{2,6},{3,7},{4,0},{5,1},{6,2},{7,3},{8,12},{9,13},{10,... | collective-permute-start | bytes 884744 | tf_op jit(solution)/shard_map/ppermute | solution.py:572
  102.4 14.1 %collective-permute-start.26 = (f32[192,384]{1,0:T(8,128)S(1)}, f32[192,384]{1,0:T(8,128)S(1)}, u32[]{:S(2)}, u32[]{:S(2)}) collective-permute-start(f32[192,384]{1,0:T(8,128)S(1)} %get-tuple-element.87), channel_id=1, source_target_pairs={{0,1},{1,0},{2,3},{3,2},{4,5},{5,4},{6,7},{7,6},{8,9},{9,8},{10,11... | collective-permute-start | bytes 884744 | tf_op jit(solution)/shard_map/ppermute | solution.py:572
  110.5 54.0 %collective-permute-start.20 = (f32[12,192]{1,0:T(8,128)S(1)}, f32[12,192]{1,0:T(8,128)S(1)}, u32[]{:S(2)}, u32[]{:S(2)}) collective-permute-start(f32[12,192]{1,0:T(8,128)S(1)} %fusion.12), channel_id=1, source_target_pairs={{0,1},{1,0},{2,3},{3,2},{4,5},{5,4},{6,7},{7,6},{8,9},{9,8},{10,11... | collective-permute-start | bytes 27656 | tf_op jit(solution)/shard_map/ppermute | solution.py:572
  121.8 7.5 %collective-permute-start.28 = (f32[2,2,24,384]{3,2,1,0:T(8,128)S(1)}, f32[2,2,24,384]{3,2,1,0:T(8,128)S(1)}, u32[]{:S(2)}, u32[]{:S(2)}) collective-permute-start(f32[2,2,24,384]{3,2,1,0:T(8,128)S(1)} %pad_maximum_fusion.6), channel_id=1, source_target_pairs={{0,8},{1,9},{2,10},{3,11},{4,12},{5,13},{6,14},{7,15},{8,0},{9,1},... | collective-permute-start | bytes 442376 | tf_op jit(solution)/shard_map/ppermute | solution.py:572
  123.6 8.9 %collective-permute-start.41 = (f32[2,2,24,768]{3,2,1,0:T(8,128)S(1)}, f32[2,2,24,768]{3,2,1,0:T(8,128)S(1)}, u32[]{:S(2)}, u32[]{:S(2)}) collective-permute-start(f32[2,2,24,768]{3,2,1,0:T(8,128)S(1)} %pad_maximum_fusion.1), channel_id=1, source_target_pairs={{0,8},{1,9},{2,10},{3,11},{4,12},{5,13},{6,14},{7,15},{8,0},{9,1},... | collective-permute-start | bytes 884744 | tf_op jit(solution)/shard_map/ppermute | solution.py:572
  129.4 8.8 %collective-permute-start.29 = (f32[2,1,24,384]{3,2,1,0:T(8,128)S(1)}, f32[2,1,24,384]{3,2,1,0:T(8,128)S(1)}, u32[]{:S(2)}, u32[]{:S(2)}) collective-permute-start(f32[2,1,24,384]{3,2,1,0:T(8,128)S(1)} %pad_maximum_fusion.13), channel_id=1, source_target_pairs={{0,16},{1,17},{2,18},{3,19},{4,20},{5,21},{6,22},{7,23},{8,24},{9,... | collective-permute-start | bytes 221192 | tf_op jit(solution)/shard_map/ppermute | solution.py:572
  138.2 8.4 %collective-permute-start.30 = (f32[2,24,384]{2,1,0:T(8,128)S(1)}, f32[2,24,384]{2,1,0:T(8,128)S(1)}, u32[]{:S(2)}, u32[]{:S(2)}) collective-permute-start(f32[2,24,384]{2,1,0:T(8,128)S(1)} %pad_maximum_fusion.12), channel_id=1, source_target_pairs={{0,16},{1,17},{2,18},{3,19},{4,20},{5,21},{6,22},{7,23},{8,24},{9,... | collective-permute-start | bytes 221192 | tf_op jit(solution)/shard_map/ppermute | solution.py:572
  138.3 12.3 %collective-permute-start.42 = (f32[2,1,24,768]{3,2,1,0:T(8,128)S(1)}, f32[2,1,24,768]{3,2,1,0:T(8,128)S(1)}, u32[]{:S(2)}, u32[]{:S(2)}) collective-permute-start(f32[2,1,24,768]{3,2,1,0:T(8,128)S(1)} %pad_maximum_fusion.9), channel_id=1, source_target_pairs={{0,16},{1,17},{2,18},{3,19},{4,20},{5,21},{6,22},{7,23},{8,24},{9,... | collective-permute-start | bytes 442376 | tf_op jit(solution)/shard_map/ppermute | solution.py:572
  150.7 6.3 %collective-permute-start.43 = (f32[2,24,768]{2,1,0:T(8,128)S(1)}, f32[2,24,768]{2,1,0:T(8,128)S(1)}, u32[]{:S(2)}, u32[]{:S(2)}) collective-permute-start(f32[2,24,768]{2,1,0:T(8,128)S(1)} %pad_maximum_fusion.5), channel_id=1, source_target_pairs={{0,16},{1,17},{2,18},{3,19},{4,20},{5,21},{6,22},{7,23},{8,24},{9,... | collective-permute-start | bytes 442376 | tf_op jit(solution)/shard_map/ppermute | solution.py:572
  150.8 6.9 %collective-permute-start.33 = (f32[2,24,384]{2,1,0:T(8,128)S(1)}, f32[2,24,384]{2,1,0:T(8,128)S(1)}, u32[]{:S(2)}, u32[]{:S(2)}) collective-permute-start(f32[2,24,384]{2,1,0:T(8,128)S(1)} %pad_maximum_fusion.14), channel_id=1, source_target_pairs={{0,8},{1,9},{2,10},{3,11},{4,12},{5,13},{6,14},{7,15},{8,0},{9,1},... | collective-permute-start | bytes 221192 | tf_op jit(solution)/shard_map/ppermute | solution.py:572
  152.4 21.9 %collective-permute-start.31 = (f32[2,24,384]{2,1,0:T(8,128)S(1)}, f32[2,24,384]{2,1,0:T(8,128)S(1)}, u32[]{:S(2)}, u32[]{:S(2)}) collective-permute-start(f32[2,24,384]{2,1,0:T(8,128)S(1)} %pad_maximum_fusion.11), channel_id=1, source_target_pairs={{0,4},{1,5},{2,6},{3,7},{4,0},{5,1},{6,2},{7,3},{8,12},{9,13},{10,... | collective-permute-start | bytes 221192 | tf_op jit(solution)/shard_map/ppermute | solution.py:572
  157.1 7.0 %collective-permute-start.44 = (f32[2,24,768]{2,1,0:T(8,128)S(1)}, f32[2,24,768]{2,1,0:T(8,128)S(1)}, u32[]{:S(2)}, u32[]{:S(2)}) collective-permute-start(f32[2,24,768]{2,1,0:T(8,128)S(1)} %pad_maximum_fusion.4), channel_id=1, source_target_pairs={{0,4},{1,5},{2,6},{3,7},{4,0},{5,1},{6,2},{7,3},{8,12},{9,13},{10,... | collective-permute-start | bytes 442376 | tf_op jit(solution)/shard_map/ppermute | solution.py:572
  157.7 21.3 %collective-permute-start.34 = (f32[4,24,384]{2,1,0:T(8,128)S(1)}, f32[4,24,384]{2,1,0:T(8,128)S(1)}, u32[]{:S(2)}, u32[]{:S(2)}) collective-permute-start(f32[4,24,384]{2,1,0:T(8,128)S(1)} %pad_maximum_fusion.8.refs_2_), channel_id=1, source_target_pairs={{0,4},{1,5},{2,6},{3,7},{4,0},{5,1},{6,2},{7,3},{8,12},{9,13},{10,... | collective-permute-start | bytes 442376 | tf_op jit(solution)/shard_map/ppermute | solution.py:572
  162.6 21.1 %collective-permute-start.47 = (f32[4,24,768]{2,1,0:T(8,128)S(1)}, f32[4,24,768]{2,1,0:T(8,128)S(1)}, u32[]{:S(2)}, u32[]{:S(2)}) collective-permute-start(f32[4,24,768]{2,1,0:T(8,128)S(1)} %pad_maximum_fusion.3.refs_2_), channel_id=1, source_target_pairs={{0,4},{1,5},{2,6},{3,7},{4,0},{5,1},{6,2},{7,3},{8,12},{9,13},{10,... | collective-permute-start | bytes 884744 | tf_op jit(solution)/shard_map/ppermute | solution.py:572
  164.2 19.6 %collective-permute-start.45 = (f32[4,24,768]{2,1,0:T(8,128)S(1)}, f32[4,24,768]{2,1,0:T(8,128)S(1)}, u32[]{:S(2)}, u32[]{:S(2)}) collective-permute-start(f32[4,24,768]{2,1,0:T(8,128)S(1)} %pad_maximum_fusion.2.refs_0_), channel_id=1, source_target_pairs={{0,8},{1,9},{2,10},{3,11},{4,12},{5,13},{6,14},{7,15},{8,0},{9,1},... | collective-permute-start | bytes 884744 | tf_op jit(solution)/shard_map/ppermute | solution.py:572
  (37 other events, 211.7 us)
